TPU v7x, 512 devices: a whole 4x8x8 slice. The times are simulated.
512 devices in a mesh: seq: 128 (over z, y_lo, x), doc: 4 (over y_hi, core).
Axes of the slice: x: 4, y: 8 (y_hi: 2, y_lo: 4; y = y_hi * 4 + y_lo), z: 8, core: 2. Of those that a mesh axis runs over, the one named last changes fastest.
Arguments:
- inputs: bfloat16 [65536, 1024], P('seq', 'doc'), may hold values from -4 to 4
- queries: bfloat16 [65536, 1024], P('seq', 'doc'), may hold values from -128 to 128
- keys_values: bfloat16 [2, 65536, 1024], P(None, 'seq', 'doc'), may hold values from -10 to 10
- slot_weight: bfloat16 [1024, 4096], P(None, 'doc'), may hold values from -3 to 3
- slot_gain: float32 [2, 1024], P(None, 'doc'), may hold values from 0.1 to 1.9
- slot_bias: float32 [2, 1024], P(None, 'doc'), may hold values from -3 to 3
- bounds: int32 [2, 65536], P(None, 'seq'), may hold values from 0 to 65536, as said below
Outputs:
- attended: bfloat16 [65536, 1024], P('seq', 'doc')
Inputs may be any that keep to these rules, and one draw needn't show every extreme that they name: The sequence holds exactly 2 documents in order, the first starting at 0 and each of 16384 tokens or more: bounds[0, i] <= i < bounds[1, i], and every token of a document has the same pair.
All inputs are finite; a program needn't handle non-finite values.
Results may differ from a plain program's by a relative error of at most 0.0045.
Values may be sent and summed in bfloat16 or wider, within the bound.
No kernel may reach another device: no remote copies, remote signals or barrier semaphores. Data moves between devices by JAX's collectives and lax.ppermute only.
A program may use at most 64 MiB of HBM per device.

v0:
```python
import jax
import jax.numpy as jnp
from jax import lax
from jax.sharding import Mesh
from jax.sharding import PartitionSpec as P

DH = 64
R = 256
W = 128
DOCS = 2
SEQ = ("seq_0", "seq_1", "seq_2")


epsilon = 1e-05


def sent_to_all(array, axis):
    devices = lax.axis_size(axis)
    return lax.all_to_all(
        jnp.broadcast_to(array[None], (devices, *array.shape)), axis, 0, 0, tiled=True
    )


def laid_out(tiles, dim):
    tiles = jnp.moveaxis(tiles, 0, dim)
    lengths = tiles.shape
    return tiles.reshape(*lengths[:dim], lengths[dim] * lengths[dim + 1], *lengths[dim + 2 :])


def gathered_copies(array, axis, dim):
    tiles = sent_to_all(array, axis)
    return laid_out(tiles, dim)


def over_copies(array, axis):
    return sent_to_all(array, axis).max(axis=0)


def over_axes(array, axes):
    far, near = axes
    nearer = over_copies(array, near)
    return over_copies(nearer, far)


def cut_along(array, dim, devices):
    lengths = array.shape
    tiles = array.reshape(*lengths[:dim], devices, lengths[dim] // devices, *lengths[dim + 1 :])
    return jnp.moveaxis(tiles, dim, 0)


def sent_and_summed(array, axis, dim):
    devices = lax.axis_size(axis)
    tiles = lax.all_to_all(cut_along(array, dim, devices), axis, 0, 0, tiled=True)
    return jnp.sum(tiles, axis=0)


def sum_in_two_steps(array, axes, dim):
    far, near = axes
    tiles = cut_along(array, dim, lax.axis_size(far))
    nearer = sent_and_summed(tiles, near, dim + 1)
    arrived = lax.all_to_all(nearer, far, split_axis=0, concat_axis=0, tiled=True)
    return arrived.sum(axis=0)


def padded_to(lines, devices):
    spare = -len(lines) % devices
    return jnp.pad(lines, [(0, spare)] + [(0, 0)] * (lines.ndim - 1))


def whole_of(array, axes, dim):
    far, near = axes
    tiles = sent_to_all(sent_to_all(array, far), near)
    return laid_out(tiles.swapaxes(0, 1).reshape(-1, *array.shape), dim)


def total_of(array, axes):
    lines = array.reshape(-1, array.shape[-1])
    own = sum_in_two_steps(
        padded_to(lines, lax.axis_size(axes[0]) * lax.axis_size(axes[1])), axes, 0
    )
    whole = whole_of(own, axes, 0)
    return whole[: len(lines)].reshape(array.shape)


def extended(array, sides, width):
    for axis, dim in sides:
        devices, length = (lax.axis_size(axis), array.shape[dim])
        up = [(i, (i + 1) % devices) for i in range(devices - 1)]
        down = [(j, i) for i, j in up]
        last = lax.slice_in_dim(array, length - width, length, axis=dim)
        first = lax.slice_in_dim(array, 0, width, axis=dim)
        before = lax.ppermute(last, axis, up)
        after = lax.ppermute(first, axis, down)
        array = jnp.concatenate([before, array, after], axis=dim)
    return array


def normalize(numerator, gain, bias):
    mean_val = jnp.mean(numerator, axis=-1, keepdims=True)
    centred = numerator - mean_val
    variance = jnp.mean(centred * centred, axis=-1, keepdims=True)
    return centred * lax.rsqrt(variance + epsilon) * gain + bias


def attend(query_block, window, lower, upper, first_pos, slot_keys, slot_values):
    q_len = query_block.shape[0]
    k_len = window.shape[1]
    second = (lower > 0)[None, :, None]
    near_scores = (
        jnp.einsum("qhe,khe->hqk", query_block, window[0], preferred_element_type=jnp.float32)
        * 0.125
    )
    far_all = (
        jnp.einsum("qhe,ghre->ghqr", query_block, slot_keys, preferred_element_type=jnp.float32)
        * 0.125
    )
    far_scores = jnp.where(second, far_all[1], far_all[0])
    query_pos = first_pos + jnp.arange(q_len, dtype=jnp.int32)
    key_pos = first_pos - W + jnp.arange(k_len, dtype=jnp.int32)
    offset = key_pos[None, :] - query_pos[:, None]
    allowed = (
        (jnp.abs(offset) <= W)
        & (key_pos[None, :] >= lower[:, None])
        & (key_pos[None, :] < upper[:, None])
    )
    near_scores = jnp.where(allowed[None], near_scores, -jnp.inf)
    row_top = jnp.maximum(jnp.max(near_scores, axis=-1), jnp.max(far_scores, axis=-1))
    near_weight = jnp.exp(near_scores - row_top[..., None])
    far_weight = jnp.exp(far_scores - row_top[..., None])
    row_total = jnp.sum(near_weight, axis=-1) + jnp.sum(far_weight, axis=-1)
    far_b = far_weight.astype(jnp.bfloat16)
    zero_val = jnp.zeros((), jnp.bfloat16)
    result = jnp.einsum(
        "hqk,khe->qhe",
        near_weight.astype(jnp.bfloat16),
        window[1],
        preferred_element_type=jnp.float32,
    )
    result = result + jnp.einsum(
        "hqr,hre->qhe",
        jnp.where(second, zero_val, far_b),
        slot_values[0],
        preferred_element_type=jnp.float32,
    )
    result = result + jnp.einsum(
        "hqr,hre->qhe",
        jnp.where(second, far_b, zero_val),
        slot_values[1],
        preferred_element_type=jnp.float32,
    )
    result = result / jnp.transpose(row_total)[:, :, None]
    return result.reshape(q_len, -1).astype(jnp.bfloat16)


def on_device(inputs, queries, keys_values, slot_weight, slot_gain, slot_bias, bounds):
    tok_rows = inputs.shape[0]
    local_heads = queries.shape[1] // DH
    owner = bounds[0] > 0
    logits = jnp.dot(
        gathered_copies(inputs, "doc", 1), slot_weight, preferred_element_type=jnp.float32
    )
    first_top = jnp.max(jnp.where(owner[:, None], -jnp.inf, logits), axis=0)
    other_top = jnp.max(jnp.where(owner[:, None], logits, -jnp.inf), axis=0)
    slot_top = over_axes(jnp.stack([first_top, other_top]), (("seq_0", "seq_1"), "seq_2"))
    top_rows = jnp.where(owner[:, None], slot_top[1][None, :], slot_top[0][None, :])
    proj = jnp.exp(logits - top_rows).astype(jnp.bfloat16).reshape(tok_rows, local_heads, R)
    zero_val = jnp.zeros((), jnp.bfloat16)
    split_proj = jnp.stack(
        [
            jnp.where(owner[:, None, None], zero_val, proj),
            jnp.where(owner[:, None, None], proj, zero_val),
        ]
    )
    kv_pair = keys_values.reshape(2, tok_rows, local_heads, DH)
    numerator = jnp.einsum(
        "gthr,stha->ghrsa", split_proj, kv_pair, preferred_element_type=jnp.float32
    )
    numerator = numerator.reshape(DOCS * local_heads * R, 2 * DH)
    gain_rows = jnp.broadcast_to(
        jnp.transpose(slot_gain.reshape(2, local_heads, DH), (1, 0, 2))[None, :, None],
        (DOCS, local_heads, R, 2, DH),
    ).reshape(DOCS * local_heads * R, 2, DH)
    bias_rows = jnp.broadcast_to(
        jnp.transpose(slot_bias.reshape(2, local_heads, DH), (1, 0, 2))[None, :, None],
        (DOCS, local_heads, R, 2, DH),
    ).reshape(DOCS * local_heads * R, 2, DH)
    summed = total_of(numerator, (("seq_0", "seq_1"), "seq_2"))
    slot_table = normalize(
        summed.reshape(DOCS * local_heads * R, 2, DH), gain_rows, bias_rows
    ).astype(jnp.bfloat16)
    slot_table = slot_table.reshape(DOCS, local_heads, R, 2, DH)
    slot_keys = slot_table[:, :, :, 0]
    slot_values = slot_table[:, :, :, 1]
    kv_rims = extended(keys_values, ((SEQ, 1),), W)
    block_len = min(512, tok_rows)
    root = lax.axis_index(SEQ) * tok_rows
    query_block = queries.reshape(block_len, local_heads, DH)
    window = kv_rims.reshape(2, block_len + 2 * W, local_heads, DH)
    lower = bounds[0, 0:block_len]
    upper = bounds[1, 0:block_len]
    pieces = attend(query_block, window, lower, upper, root + 0, slot_keys, slot_values)
    return pieces


def solution(mesh):
    finer = Mesh(
        mesh.devices.reshape(8, 4, 4, mesh.shape["doc"]), ("seq_0", "seq_1", "seq_2", "doc")
    )
    return jax.shard_map(
        on_device,
        mesh=finer,
        in_specs=(
            P(SEQ, "doc"),
            P(SEQ, "doc"),
            P(None, SEQ, "doc"),
            P(None, "doc"),
            P(None, "doc"),
            P(None, "doc"),
            P(None, SEQ),
        ),
        out_specs=P(SEQ, "doc"),
        check_vma=False,
    )
```

profile of v0, /device:TPU:2, one launch (start us, length us, event | category | flops | bytes accessed | tf_op | source)
XLA Modules:
  0.0 224.2 jit_solution(16659267005539253286)
XLA Ops:
  0.0 1.3 copy.109
  1.3 1.1 broadcast_in_dim.123
  2.3 7.1 %all-to-all-start = ((bf16[4,512,256]{1,2,0:T(8,128)(2,1)}), bf16[4,512,256]{1,2,0:T(8,128)(2,1)S(1)}, u32[]{:S(2)}, u32[]{:S(2)}) async-start(bf16[4,512,256]{1,2,0:T(8,128)(2,1)} %broadcast_in_dim.123), calls=%async_computation | async-start | bytes 2097152 | tf_op jit(solution)/shard_map/all_to_all | solution.py:19
  9.4 28.0 %all-to-all-done = bf16[4,512,256]{1,2,0:T(8,128)(2,1)S(1)} async-done(((bf16[4,512,256]{1,2,0:T(8,128)(2,1)}), bf16[4,512,256]{1,2,0:T(8,128)(2,1)S(1)}, u32[]{:S(2)}, u32[]{:S(2)}) %all-to-all-start) | async-done | bytes 1048608 | tf_op jit(solution)/shard_map/all_to_all | solution.py:19
  37.5 1.0 copy-done.4
  38.5 4.0 %select_reduce_fusion.1 = (f32[1024]{0:T(1024)S(1)}, f32[1024]{0:T(1024)S(1)}, f32[512,1024]{1,0:T(8,128)}) fusion(pred[512]{0:T(512)(128)(4,1)S(1)} %broadcast_compare_fusion, bf16[512,1024]{0,1:T(8,128)(2,1)} %bitcast.98, bf16[1024,1024]{1,0:T(8,128)(2,1)S(1)} %copy-done), kind=kOutput, calls=%fused_computation.19 | convolution fusion | flops 1075836928 | bytes 5251584 | tf_op jit(solution)/shard_map/dot_general | solution.py:159
  42.5 8.6 %all_to_all.35 = f32[4,2,1024]{2,1,0:T(2,128)S(1)} all-to-all(f32[4,2,1024]{2,1,0:T(2,128)S(1)} %broadcast_in_dim.170), channel_id=1, replica_groups=mesh['seq_0'=8,'seq_1'=4,'seq_2'=4,'doc'=4] {'seq_2'}, dimensions={0} | all-to-all | bytes 65536 | tf_op jit(solution)/shard_map/all_to_all | solution.py:19
  51.1 0.8 broadcast_in_dim.171
  51.9 12.4 %all-to-all-start.2 = ((f32[32,2,1024]{2,1,0:T(2,128)}), f32[32,2,1024]{2,1,0:T(2,128)S(1)}, u32[]{:S(2)}, u32[]{:S(2)}) async-start(f32[32,2,1024]{2,1,0:T(2,128)} %broadcast_in_dim.171), calls=%async_computation.2 | async-start | bytes 524288 | tf_op jit(solution)/shard_map/all_to_all | solution.py:19
  64.3 1.0 copy.114
  65.3 10.9 %all-to-all-done.2 = f32[32,2,1024]{2,1,0:T(2,128)S(1)} async-done(((f32[32,2,1024]{2,1,0:T(2,128)}), f32[32,2,1024]{2,1,0:T(2,128)S(1)}, u32[]{:S(2)}, u32[]{:S(2)}) %all-to-all-start.2) | async-done | bytes 262176 | tf_op jit(solution)/shard_map/all_to_all | solution.py:19
  76.2 0.1 reduce_max.58
  76.3 2.0 exponential_convert_fusion
  78.3 1.6 reshape.205
  79.9 1.5 broadcast_select_fusion.1
  81.4 0.4 fusion.14
  81.9 2.3 %copy.116 = f32[2,4,256,2,64]{4,3,2,1,0:T(2,128)} copy(f32[2,4,256,2,64]{2,4,3,0,1:T(8,128)S(1)} %fusion.14) | data formatting | bytes 2097152 | tf_op jit(solution)/shard_map/gthr,stha->ghrsa/transpose | solution.py:175
  84.2 2.6 %reshape_reshape.3 = f32[32,4,16,128]{3,2,1,0:T(8,128)S(1)} reshape(f32[2,4,256,2,64]{4,3,2,1,0:T(2,128)} %copy.116) | data formatting | bytes 2097152 | tf_op jit(solution)/shard_map/reshape;reshape | solution.py:47
  86.9 15.2 %all_to_all.36 = f32[4,32,16,128]{3,2,1,0:T(8,128)S(1)} all-to-all(f32[4,32,16,128]{3,2,1,0:T(8,128)S(1)} %copy.117), channel_id=1, replica_groups=mesh['seq_0'=8,'seq_1'=4,'seq_2'=4,'doc'=4] {'seq_2'}, dimensions={0} | all-to-all | bytes 2097152 | tf_op jit(solution)/shard_map/all_to_all | solution.py:53
  102.1 0.8 reduce_sum.54
  102.8 5.1 %all-to-all-start.4 = ((f32[32,16,128]{2,1,0:T(8,128)}), f32[32,16,128]{2,1,0:T(8,128)S(1)}, u32[]{:S(2)}, u32[]{:S(2)}) async-start(f32[32,16,128]{2,1,0:T(8,128)} %reduce_sum.54), calls=%async_computation.4 | async-start | bytes 524288 | tf_op jit(solution)/shard_map/all_to_all | solution.py:61
  107.9 1.6 fusion.39
  109.6 3.4 %collective-permute-start.1 = (bf16[2,128,256]{2,1,0:T(8,128)(2,1)}, bf16[2,128,256]{2,1,0:T(8,128)(2,1)}, u32[]{:S(2)}, u32[]{:S(2)}) collective-permute-start(bf16[2,128,256]{2,1,0:T(8,128)(2,1)} %get-tuple-element.13), channel_id=1, source_target_pairs={{4,0},{8,4},{12,8},{16,12},{20,16},{24,20},{28,24},{32,28},{36,32}... | collective-permute-start | bytes 393224 | tf_op jit(solution)/shard_map/ppermute | solution.py:93
  113.0 2.5 %collective-permute-start = (bf16[2,128,256]{2,1,0:T(8,128)(2,1)S(1)}, bf16[2,128,256]{2,1,0:T(8,128)(2,1)S(1)}, u32[]{:S(2)}, u32[]{:S(2)}) collective-permute-start(bf16[2,128,256]{2,1,0:T(8,128)(2,1)S(1)} %get-tuple-element.14), channel_id=1, source_target_pairs={{0,4},{4,8},{8,12},{12,16},{16,20},{20,24},{24,28},{28,32},{32,36}... | collective-permute-start | bytes 393224 | tf_op jit(solution)/shard_map/ppermute | solution.py:92
  115.4 4.4 %all-to-all-done.4 = f32[32,16,128]{2,1,0:T(8,128)S(1)} async-done(((f32[32,16,128]{2,1,0:T(8,128)}), f32[32,16,128]{2,1,0:T(8,128)S(1)}, u32[]{:S(2)}, u32[]{:S(2)}) %all-to-all-start.4) | async-done | bytes 262176 | tf_op jit(solution)/shard_map/all_to_all | solution.py:61
  119.9 0.7 broadcast_in_dim.176
  120.6 5.6 %all-to-all-start.5 = ((f32[32,16,128]{2,1,0:T(8,128)}), f32[32,16,128]{2,1,0:T(8,128)S(1)}, u32[]{:S(2)}, u32[]{:S(2)}) async-start(f32[32,16,128]{2,1,0:T(8,128)} %broadcast_in_dim.176), calls=%async_computation.5 | async-start | bytes 524288 | tf_op jit(solution)/shard_map/all_to_all | solution.py:19
  126.3 0.7 reshape.207
  127.0 0.7 reshape.208
  127.7 0.8 copy.108
  128.5 0.7 fusion.13
  129.2 0.7 constant_dynamic-update-slice_fusion.2
  129.9 8.4 %all-to-all-done.5 = f32[32,16,128]{2,1,0:T(8,128)S(1)} async-done(((f32[32,16,128]{2,1,0:T(8,128)}), f32[32,16,128]{2,1,0:T(8,128)S(1)}, u32[]{:S(2)}, u32[]{:S(2)}) %all-to-all-start.5) | async-done | bytes 262176 | tf_op jit(solution)/shard_map/all_to_all | solution.py:19
  138.2 1.1 broadcast_in_dim.177
  139.3 8.7 %all-to-all-start.6 = ((f32[4,32,16,128]{3,2,1,0:T(8,128)}), f32[4,32,16,128]{3,2,1,0:T(8,128)S(1)}, u32[]{:S(2)}, u32[]{:S(2)}) async-start(f32[4,32,16,128]{3,2,1,0:T(8,128)} %broadcast_in_dim.177), calls=%async_computation.6 | async-start | bytes 2097152 | tf_op jit(solution)/shard_map/all_to_all | solution.py:19
  148.0 1.9 constant_dynamic-update-slice_fusion.1
  149.9 1.6 constant_dynamic-update-slice_fusion
  151.4 2.0 fusion.38
  153.5 1.9 copy.106
  155.4 1.9 copy.107
  157.3 5.6 %fusion.2 = (f32[4,512]{1,0:T(4,128)}, f32[4,768,512]{2,1,0:T(8,128)}) fusion(pred[512,768]{0,1:T(8,128)(4,1)S(1)} %fusion.13, bf16[768,4,64]{0,2,1:T(8,128)(2,1)} %bitcast.97, bf16[512,4,64]{0,2,1:T(8,128)(2,1)} %bitcast.95), kind=kOutput, calls=%fused_computation.4 | convolution fusion | flops 206043136 | bytes 7348224 | tf_op jit(solution)/shard_map/qhe,khe->hqk/dot_general | solution.py:110
  162.9 1.0 copy-done.2
  163.9 1.4 copy.118
  165.3 2.5 %reshape_reshape_reshape.6 = f32[2048,2,64]{2,1,0:T(2,128)} reshape(f32[32,4,16,128]{3,2,1,0:T(8,128)S(1)} %copy.118) | data formatting | bytes 2097152 | tf_op jit(solution)/shard_map/reshape;reshape;reshape | solution.py:189
  167.8 2.5 %reshape_reshape_reshape.5 = f32[2,4,256,2,64]{4,3,2,1,0:T(2,128)} reshape(f32[32,4,16,128]{3,2,1,0:T(8,128)S(1)} %copy.118) | data formatting | bytes 2097152 | tf_op jit(solution)/shard_map/reshape;reshape;reshape | solution.py:189
  170.3 3.9 %copy.122 = f32[2,4,256,2,64]{2,4,0,1,3:T(8,128)} copy(f32[2,4,256,2,64]{4,3,2,1,0:T(2,128)} %reshape_reshape_reshape.5) | data formatting | bytes 2097152 | tf_op jit(solution)/shard_map/reshape;reshape;reshape | solution.py:189
  174.3 5.7 %reduce_sum.56 = f32[2048,2]{1,0:T(8,128)} reduce(f32[2048,2,64]{2,1,0:T(2,128)} %reshape_reshape_reshape.6, f32[]{:T(128)} %constant.41.clone.1), dimensions={2}, to_apply=%region_7.8 | reduce | flops 258048 | bytes 1064964 | tf_op jit(solution)/shard_map/reduce_sum | solution.py:99
  180.0 1.4 broadcast_multiply_fusion
  181.4 0.5 copy-done.1
  181.9 29.1 %multiply_reduce_fusion = f32[2048,2]{1,0:T(8,128)S(1)} fusion(f32[2048,2,64]{2,1,0:T(2,128)S(1)} %copy-done.1, f32[2048,2]{1,0:T(8,128)S(1)} %broadcast_multiply_fusion), kind=kLoop, calls=%fused_computation.16 | loop fusion | flops 782336 | bytes 1081344 | tf_op jit(solution)/shard_map/reduce_sum | solution.py:101
  210.9 1.1 add_rsqrt_fusion
  212.1 1.6 copy.125
  213.6 0.9 copy.121
  214.6 1.5 add_convert_fusion
  216.1 1.9 multiply_bitcast_fusion
  218.0 0.5 fusion.36
  218.5 0.2 copy-done.8
  218.7 0.3 fusion.10
  219.0 0.5 fusion.22
  219.4 0.2 slice-done.1
  219.7 1.4 fusion
  221.1 1.8 fusion.17
  222.9 0.5 fusion.20
  223.4 0.8 copy.130
  (43 shorter events, 0.3 us)
Async XLA Ops:
  0.0 38.5 %copy-start = (bf16[1024,1024]{1,0:T(8,128)(2,1)S(1)}, bf16[1024,1024]{1,0:T(8,128)(2,1)}, u32[]{:S(2)}) copy-start(bf16[1024,1024]{1,0:T(8,128)(2,1)} %param.10) | copy-start | bytes 6291460
  0.0 9.4 %copy-start.11 = (s32[2,512]{1,0:T(2,128)S(1)}, s32[2,512]{1,0:T(2,128)}, u32[]{:S(2)}) copy-start(s32[2,512]{1,0:T(2,128)} %param.13) | copy-start | bytes 12292
  2.3 35.1 %all-to-all-start = ((bf16[4,512,256]{1,2,0:T(8,128)(2,1)}), bf16[4,512,256]{1,2,0:T(8,128)(2,1)S(1)}, u32[]{:S(2)}, u32[]{:S(2)}) async-start(bf16[4,512,256]{1,2,0:T(8,128)(2,1)} %broadcast_in_dim.123), calls=%async_computation | async-start | bytes 2097152 | tf_op jit(solution)/shard_map/all_to_all | solution.py:19
  9.4 70.5 %copy-start.9 = (pred[512]{0:T(512)(128)(4,1)}, pred[512]{0:T(512)(128)(4,1)S(1)}, u32[]{:S(2)}) copy-start(pred[512]{0:T(512)(128)(4,1)S(1)} %broadcast_compare_fusion) | copy-start | bytes 1540
  37.4 1.0 copy-start.4
  38.5 25.8 %copy-start.3 = (bf16[2,512,256]{2,1,0:T(8,128)(2,1)S(1)}, bf16[2,512,256]{2,1,0:T(8,128)(2,1)}, u32[]{:S(2)}) copy-start(bf16[2,512,256]{2,1,0:T(8,128)(2,1)} %param.9) | copy-start | bytes 1572868
  51.9 24.4 %all-to-all-start.2 = ((f32[32,2,1024]{2,1,0:T(2,128)}), f32[32,2,1024]{2,1,0:T(2,128)S(1)}, u32[]{:S(2)}, u32[]{:S(2)}) async-start(f32[32,2,1024]{2,1,0:T(2,128)} %broadcast_in_dim.171), calls=%async_computation.2 | async-start | bytes 524288 | tf_op jit(solution)/shard_map/all_to_all | solution.py:19
  79.9 1.5 copy-start.5
  102.1 24.3 %copy-start.12 = (f32[2,256]{1,0:T(2,128)S(1)}, f32[2,256]{1,0:T(2,128)}, u32[]{:S(2)}) copy-start(f32[2,256]{1,0:T(2,128)} %param.11) | copy-start | bytes 6148
  102.1 24.9 %copy-start.13 = (f32[2,256]{1,0:T(2,128)S(1)}, f32[2,256]{1,0:T(2,128)}, u32[]{:S(2)}) copy-start(f32[2,256]{1,0:T(2,128)} %param.12) | copy-start | bytes 6148
  102.1 25.6 %copy-start.7 = (bf16[512,256]{1,0:T(8,128)(2,1)S(1)}, bf16[512,256]{1,0:T(8,128)(2,1)}, u32[]{:S(2)}) copy-start(bf16[512,256]{1,0:T(8,128)(2,1)} %param.8) | copy-start | bytes 786436
  102.8 17.0 %all-to-all-start.4 = ((f32[32,16,128]{2,1,0:T(8,128)}), f32[32,16,128]{2,1,0:T(8,128)S(1)}, u32[]{:S(2)}, u32[]{:S(2)}) async-start(f32[32,16,128]{2,1,0:T(8,128)} %reduce_sum.54), calls=%async_computation.4 | async-start | bytes 524288 | tf_op jit(solution)/shard_map/all_to_all | solution.py:61
  109.6 40.3 %collective-permute-start.1 = (bf16[2,128,256]{2,1,0:T(8,128)(2,1)}, bf16[2,128,256]{2,1,0:T(8,128)(2,1)}, u32[]{:S(2)}, u32[]{:S(2)}) collective-permute-start(bf16[2,128,256]{2,1,0:T(8,128)(2,1)} %get-tuple-element.13), channel_id=1, source_target_pairs={{4,0},{8,4},{12,8},{16,12},{20,16},{24,20},{28,24},{32,28},{36,32}... | collective-permute-start | bytes 393224 | tf_op jit(solution)/shard_map/ppermute | solution.py:93
  113.0 16.2 %collective-permute-start = (bf16[2,128,256]{2,1,0:T(8,128)(2,1)S(1)}, bf16[2,128,256]{2,1,0:T(8,128)(2,1)S(1)}, u32[]{:S(2)}, u32[]{:S(2)}) collective-permute-start(bf16[2,128,256]{2,1,0:T(8,128)(2,1)S(1)} %get-tuple-element.14), channel_id=1, source_target_pairs={{0,4},{4,8},{8,12},{12,16},{16,20},{20,24},{24,28},{28,32},{32,36}... | collective-permute-start | bytes 393224 | tf_op jit(solution)/shard_map/ppermute | solution.py:92
  120.6 17.6 %all-to-all-start.5 = ((f32[32,16,128]{2,1,0:T(8,128)}), f32[32,16,128]{2,1,0:T(8,128)S(1)}, u32[]{:S(2)}, u32[]{:S(2)}) async-start(f32[32,16,128]{2,1,0:T(8,128)} %broadcast_in_dim.176), calls=%async_computation.5 | async-start | bytes 524288 | tf_op jit(solution)/shard_map/all_to_all | solution.py:19
  139.3 23.6 %all-to-all-start.6 = ((f32[4,32,16,128]{3,2,1,0:T(8,128)}), f32[4,32,16,128]{3,2,1,0:T(8,128)S(1)}, u32[]{:S(2)}, u32[]{:S(2)}) async-start(f32[4,32,16,128]{3,2,1,0:T(8,128)} %broadcast_in_dim.177), calls=%async_computation.6 | async-start | bytes 2097152 | tf_op jit(solution)/shard_map/all_to_all | solution.py:19
  162.9 1.0 copy-start.2
  180.0 1.9 copy-start.1
  216.1 1.9 copy-start.10
  216.1 3.4 %slice-start = ((s8[6291456]{0:T(1024)(128)(4,1)}), s8[4194304]{0:T(1024)(128)(4,1)S(1)}, s32[]{:S(2)}) async-start(s8[6291456]{0:T(1024)(128)(4,1)} %bitcast.89), calls=%async_computation.7 | async-start | bytes 8388608
  218.0 0.7 copy-start.8
  218.0 1.7 slice-start.1
  219.7 1.4 copy-start.6
where the time goes:
time: 225 us; the launch traced here: 224 us
  waiting for transfers between devices  51.8 us (23%)
  other arithmetic  46.2 us (21%)
  starting transfers between devices  44.8 us (20%)
  local copies, waits for them, and re-layouts  42.8 us (19%)
  blocking collectives  23.8 us (11%)
  matrix products  14.6 us (6%)
    all_to_all x4, waiting for transfers between devices, sent_to_all(): lax.all_to_all(jnp.broadcast_to(array[None], (devices, *array.shape)), ax...  47.3 us
    all_to_all x4, starting transfers between devices, sent_to_all(): lax.all_to_all(jnp.broadcast_to(array[None], (devices, *array.shape)), ax...  33.9 us
    reduce_sum x1, other arithmetic, normalize(): variance = jnp.mean(centred * centred, axis=-1, keepdims=True)  29.1 us
    all_to_all x1, blocking collectives, sent_and_summed(): lax.all_to_all(cut_along(array, dim, devices), axis, 0, 0, tiled=True)  15.2 us
    another operation x3, local copies, waits for them, and re-layouts, on_device(): summed.reshape(DOCS * local_heads * R, 2, DH)  8.98 us
    all_to_all x1, blocking collectives, sent_to_all(): lax.all_to_all(jnp.broadcast_to(array[None], (devices, *array.shape)), ax...  8.62 us
    unnamed x37, local copies, waits for them, and re-layouts  8.5 us
    reduce_sum x1, other arithmetic, normalize(): mean_val = jnp.mean(numerator, axis=-1, keepdims=True)  5.72 us
  transfers between devices with their start and end apart: 7, of which 4 were waited for; matrix products, arithmetic and copies ran while one was open for 10% of the time, Pallas kernels for 0%

commit v1 on v0

v1 whole, which is shorter than its diff:
```python
import functools

import jax
import jax.numpy as jnp
from jax import lax
from jax.experimental import pallas as pl
from jax.experimental.pallas import tpu as pltpu
from jax.sharding import Mesh
from jax.sharding import PartitionSpec as P

DH = 64
R = 256
W = 128
HEADS = 4
LANES = 128
ROWS = 8
SEQ = ("z", "yl", "x")
DOC = ("yh", "c")
EPS = 1e-05
LOW = -1e30
SWAP = [(0, 1), (1, 0)]

f32 = jnp.float32
bf16 = jnp.bfloat16
VMEM = pl.BlockSpec(memory_space=pltpu.VMEM)
SMEM = pl.BlockSpec(memory_space=pltpu.SMEM)


def call(kernel, out_shape, n_in, vmem_mib, flops, nbytes, exps=0):
    single = not isinstance(out_shape, (list, tuple))
    return pl.pallas_call(
        kernel,
        out_shape=out_shape,
        in_specs=[SMEM] + [VMEM] * n_in,
        out_specs=VMEM if single else [VMEM] * len(out_shape),
        compiler_params=pltpu.CompilerParams(vmem_limit_bytes=vmem_mib << 20),
        cost_estimate=pl.CostEstimate(flops=flops, bytes_accessed=nbytes, transcendentals=exps),
    )


def dot_nt(a, b):
    return lax.dot_general(a, b, (((1,), (1,)), ((), ())), preferred_element_type=f32)


def lanes_of(shape):
    return lax.broadcasted_iota(jnp.int32, shape, len(shape) - 1)


def prep_kernel(scal, q_ref, kv_ref, q2_ref, kvh_ref):
    tokens = q_ref.shape[0]
    local = scal[0]
    second = lax.broadcasted_iota(jnp.int32, (tokens, LANES), 0) >= local
    left = lanes_of((tokens, LANES)) < DH
    for pair in range(HEADS // 2):
        cols = slice(pair * LANES, (pair + 1) * LANES)
        query = q_ref[:, cols].astype(f32) * 0.125
        keys = kv_ref[0, :, cols].astype(f32)
        values = kv_ref[1, :, cols].astype(f32)
        query_r = pltpu.roll(query, DH, 1)
        keys_r = pltpu.roll(keys, DH, 1)
        values_r = pltpu.roll(values, DH, 1)
        for half in range(2):
            h = 2 * pair + half
            both = jnp.where(left, query, query_r) if half == 0 else jnp.where(left, query_r, query)
            q2_ref[h] = jnp.where(left == second, 0.0, both).astype(bf16)
            joined = jnp.where(left, keys, values_r) if half == 0 else jnp.where(left, keys_r, values)
            kvh_ref[h, :, :LANES] = jnp.where(second, 0.0, joined).astype(bf16)
            kvh_ref[h, :, LANES:] = jnp.where(second, joined, 0.0).astype(bf16)


def near_kernel(scal, q_ref, kv_ref, before_ref, after_ref, o_ref, stat_ref):
    tokens = q_ref.shape[0]
    local, base, total = scal[0], scal[1], scal[2]
    blocks = tokens // W
    span = 3 * W
    row = lax.broadcasted_iota(jnp.int32, (W, span), 0)
    col = lax.broadcasted_iota(jnp.int32, (W, span), 1)
    band = (col >= row) & (col - row <= 2 * W)
    left = lanes_of((W, LANES)) < DH
    lane = lanes_of((W, LANES))

    def piece(s, at, cols):
        if at < 0:
            return before_ref[s, :, cols]
        if at >= blocks:
            return after_ref[s, :, cols]
        return kv_ref[s, at * W : (at + 1) * W, cols]

    for b in range(blocks):
        query_pos = row + b * W
        key_pos = col + (b - 1) * W
        allowed = (
            band
            & ((query_pos >= local) == (key_pos >= local))
            & (key_pos + base >= 0)
            & (key_pos + base < total)
        )
        stats = jnp.zeros((W, LANES), f32)
        for pair in range(HEADS // 2):
            cols = slice(pair * LANES, (pair + 1) * LANES)
            query = q_ref[b * W : (b + 1) * W, cols].astype(f32) * 0.125
            keys = jnp.concatenate([piece(0, b + i, cols) for i in (-1, 0, 1)], axis=0)
            values = jnp.concatenate([piece(1, b + i, cols) for i in (-1, 0, 1)], axis=0)
            outs = []
            for half in range(2):
                h = 2 * pair + half
                mine = jnp.where(left == (half == 0), query, 0.0).astype(bf16)
                scores = jnp.where(allowed, dot_nt(mine, keys), LOW)
                top = jnp.max(scores, axis=1, keepdims=True)
                weight = jnp.exp(scores - top)
                total_w = jnp.sum(weight, axis=1, keepdims=True)
                outs.append(jnp.dot(weight.astype(bf16), values, preferred_element_type=f32))
                stats = jnp.where(lane == h, top, stats)
                stats = jnp.where(lane == HEADS + h, total_w, stats)
            o_ref[b * W : (b + 1) * W, cols] = jnp.where(left, outs[0], outs[1])
        stat_ref[b * W : (b + 1) * W, :] = stats


def pieces_of(top):
    a = top.astype(bf16).astype(f32)
    b = (top - a).astype(bf16).astype(f32)
    return a, b, top - a - b


def project_kernel(scal, x0, x1, x2, x3, wt_ref, kvh_ref, out_ref):
    tokens = x0.shape[0]
    local = scal[0]
    second = lax.broadcasted_iota(jnp.int32, (R, tokens), 1) >= local
    mixed = jnp.logical_and(local > 0, local < tokens)
    lane = lanes_of((R, LANES))
    at_a = lane == 0
    at_b = lane == DH
    left = lane < DH
    for h in range(HEADS):
        rows = slice(h * R, (h + 1) * R)
        logits = dot_nt(wt_ref[scal[3], rows, :], x0[...])
        logits += dot_nt(wt_ref[scal[4], rows, :], x1[...])
        logits += dot_nt(wt_ref[scal[5], rows, :], x2[...])
        logits += dot_nt(wt_ref[scal[6], rows, :], x3[...])
        top0 = jnp.maximum(jnp.max(jnp.where(second, LOW, logits), axis=1, keepdims=True), LOW)
        top1 = jnp.maximum(jnp.max(jnp.where(second, logits, LOW), axis=1, keepdims=True), LOW)
        a0, b0, c0 = pieces_of(top0)
        a1, b1, c1 = pieces_of(top1)
        proj = jnp.exp(logits - jnp.where(second, a1 + b1, a0 + b0)).astype(bf16)
        sums = jnp.dot(proj, kvh_ref[h], preferred_element_type=f32)
        n0 = sums[:, :LANES]
        n1 = sums[:, LANES:]
        n0 = n0 - jnp.where(left, n0[:, 0:1], n0[:, DH : DH + 1])
        n1 = n1 - jnp.where(left, n1[:, 0:1], n1[:, DH : DH + 1])
        late = local <= 0
        a_p, b_p, c_p = (jnp.where(late, u1, u0) for u0, u1 in ((a0, a1), (b0, b1), (c0, c1)))
        body = jnp.where(mixed, n0, n0 + n1)
        hi = body.astype(bf16).astype(f32)
        rest = jnp.where(mixed, n1, body - hi)
        hi = jnp.where(at_a, a_p, jnp.where(at_b, b_p, hi))
        rest = jnp.where(
            at_a,
            jnp.where(mixed, a1, c_p),
            jnp.where(at_b, jnp.where(mixed, b1, jnp.zeros_like(b1)), rest),
        )
        parts = R // ROWS
        packed = jnp.concatenate(
            [hi.reshape(parts, ROWS, LANES), rest.reshape(parts, ROWS, LANES)], axis=1
        )
        out_ref[h * parts : (h + 1) * parts] = packed.astype(bf16)


def combine_kernel(scal, in_ref, gain_ref, bias_ref, out_ref):
    senders = in_ref.shape[0]
    split, tokens = scal[0], scal[1]
    edge = split // tokens
    has_edge = lax.rem(split, tokens) != 0
    shape = (senders, ROWS, LANES)
    j = lax.broadcasted_iota(jnp.int32, shape, 0)
    is_edge = jnp.logical_and(j == edge, has_edge)
    late = j * tokens >= split
    first = in_ref[:, :ROWS, :].astype(f32)
    other = in_ref[:, ROWS:, :].astype(f32)
    top = first[:, :, 0:1] + first[:, :, DH : DH + 1]
    top = jnp.broadcast_to(top, shape)
    fine = jnp.where(is_edge, 0.0, jnp.broadcast_to(other[:, :, 0:1], shape))
    value = jnp.where(is_edge, first, first + other)
    extra = in_ref[edge % senders].astype(f32)[ROWS:]
    extra_top = jnp.broadcast_to(extra[:, 0:1] + extra[:, DH : DH + 1], (ROWS, LANES))
    extra_top = jnp.where(has_edge, extra_top, LOW)
    top0 = jnp.max(jnp.where(late, LOW, top), axis=0)
    full0 = jnp.max(jnp.where(late, LOW, top + fine), axis=0)
    top1 = jnp.maximum(jnp.max(jnp.where(late, top, LOW), axis=0), extra_top)
    full1 = jnp.maximum(jnp.max(jnp.where(late, top + fine, LOW), axis=0), extra_top)
    weight = jnp.exp(top - jnp.where(late, top1[None], top0[None]))
    value = value * weight
    n0 = jnp.sum(jnp.where(late, 0.0, value), axis=0)
    n1 = jnp.sum(jnp.where(late, value, 0.0), axis=0)
    n1 = n1 + jnp.where(has_edge, extra * jnp.exp(extra_top - top1), 0.0)
    lane = lanes_of((ROWS, LANES))
    left = lane < DH
    used = jnp.logical_and(lane != 0, lane != DH)
    gain = gain_ref[...]
    bias = bias_ref[...]

    def halves(v):
        a = jnp.sum(jnp.where(left, v, 0.0), axis=1, keepdims=True)
        b = jnp.sum(jnp.where(left, 0.0, v), axis=1, keepdims=True)
        return jnp.where(left, a, b) * (1.0 / DH)

    def norm(n, top_v, full_v):
        n = jnp.where(used, n, 0.0)
        centred = n - halves(n)
        variance = halves(centred * centred)
        scale = jnp.exp(2.0 * (full_v - top_v))
        return centred * lax.rsqrt(variance + EPS * scale) * gain + bias

    t0 = norm(n0, top0, full0)
    t1 = norm(n1, top1, full1)
    keys = jnp.where(left, t0, pltpu.roll(t1, DH, 1))
    values = jnp.where(left, pltpu.roll(t0, DH, 1), t1)
    chunk = jnp.concatenate([keys, values], axis=0)[None]
    out_ref[...] = jnp.broadcast_to(chunk, out_ref.shape).astype(bf16)


def far_kernel(scal, q2_ref, tab_ref, o_ref, stat_ref, out_ref):
    tokens = o_ref.shape[0]
    local = scal[0]
    lane = lanes_of((tokens, LANES))
    left = lane < DH
    second = lax.broadcasted_iota(jnp.int32, (tokens, LANES), 0) >= local
    parts = R // ROWS
    stats = stat_ref[...]
    for pair in range(HEADS // 2):
        cols = slice(pair * LANES, (pair + 1) * LANES)
        near = o_ref[:, cols]
        outs = []
        for half in range(2):
            h = 2 * pair + half
            table = tab_ref[h * parts : (h + 1) * parts].astype(f32)
            keys = table[:, :ROWS].reshape(R, LANES).astype(bf16)
            values = table[:, ROWS:].reshape(R, LANES).astype(bf16)
            scores = dot_nt(q2_ref[h], keys)
            near_top = stats[:, h : h + 1]
            near_total = stats[:, HEADS + h : HEADS + h + 1]
            top = jnp.maximum(jnp.max(scores, axis=1, keepdims=True), near_top)
            weight = jnp.exp(scores - top)
            scale = jnp.exp(near_top - top)
            total = jnp.sum(weight, axis=1, keepdims=True) + near_total * scale
            far = jnp.dot(weight.astype(bf16), values, preferred_element_type=f32)
            swap = second if half == 0 else jnp.logical_not(second)
            far = jnp.where(swap, pltpu.roll(far, DH, 1), far)
            outs.append((near * scale + far) / total)
        out_ref[:, cols] = jnp.where(left, outs[0], outs[1]).astype(bf16)


def on_device(inputs, queries, keys_values, slot_weight, slot_gain, slot_bias, bounds):
    tokens, width = inputs.shape
    shards = lax.axis_size(SEQ)
    shard = lax.axis_index(SEQ)
    split = jnp.where(bounds[0, 0] > 0, bounds[0, 0], bounds[1, 0])
    base = shard * tokens
    yh, c = lax.axis_index("yh"), lax.axis_index("c")
    scal = jnp.stack(
        [
            split - base,
            base,
            jnp.int32(shards * tokens),
            yh * 2 + c,
            yh * 2 + 1 - c,
            (1 - yh) * 2 + c,
            (1 - yh) * 2 + 1 - c,
        ]
    ).astype(jnp.int32)
    scal2 = jnp.stack([split, jnp.int32(tokens)]).astype(jnp.int32)

    x2 = lax.ppermute(inputs, "yh", SWAP)
    x1 = lax.ppermute(inputs, "c", SWAP)
    x3 = lax.ppermute(x2, "c", SWAP)
    up = [(i, i + 1) for i in range(shards - 1)]
    down = [(j, i) for i, j in up]
    before = lax.ppermute(keys_values[:, tokens - W :], SEQ, up)
    after = lax.ppermute(keys_values[:, :W], SEQ, down)

    weight_t = jnp.swapaxes(slot_weight.reshape(4, width, HEADS * R), 1, 2)
    q2, kvh = call(
        prep_kernel,
        [
            jax.ShapeDtypeStruct((HEADS, tokens, LANES), bf16),
            jax.ShapeDtypeStruct((HEADS, tokens, 2 * LANES), bf16),
        ],
        2, 16, 0, 3 << 20,
    )(scal, queries, keys_values)

    sent = call(
        project_kernel,
        jax.ShapeDtypeStruct((shards, 2 * ROWS, LANES), bf16),
        6, 24, 2 * tokens * HEADS * R * (4 * width + 2 * LANES), 5 << 20, tokens * HEADS * R,
    )(scal, inputs, x1, x2, x3, weight_t, kvh)
    arrived = lax.all_to_all(sent, SEQ, 0, 0, tiled=True)

    near, stats = call(
        near_kernel,
        [
            jax.ShapeDtypeStruct((tokens, HEADS * DH), f32),
            jax.ShapeDtypeStruct((tokens, LANES), f32),
        ],
        4, 16, 4 * tokens * 3 * W * HEADS * LANES, 2 << 20, tokens * 3 * W * HEADS,
    )(scal, queries, keys_values, before, after)

    head = shard * ROWS // R
    gain = lax.dynamic_slice_in_dim(slot_gain, head * DH, DH, 1).reshape(1, 2 * DH)
    bias = lax.dynamic_slice_in_dim(slot_bias, head * DH, DH, 1).reshape(1, 2 * DH)
    chunk = call(
        combine_kernel,
        jax.ShapeDtypeStruct((shards, 2 * ROWS, LANES), bf16),
        3, 16, 0, 1 << 20, 1 << 17,
    )(scal2, arrived, gain, bias)
    table = lax.all_to_all(chunk, SEQ, 0, 0, tiled=True)

    return call(
        far_kernel,
        jax.ShapeDtypeStruct((tokens, HEADS * DH), bf16),
        4, 24, 4 * tokens * R * HEADS * LANES, 2 << 20, tokens * R * HEADS,
    )(scal, q2, table, near, stats)


def solution(mesh):
    finer = Mesh(mesh.devices.reshape(8, 4, 4, 2, 2), SEQ + DOC)
    return jax.shard_map(
        on_device,
        mesh=finer,
        in_specs=(
            P(SEQ, DOC),
            P(SEQ, DOC),
            P(None, SEQ, DOC),
            P(None, DOC),
            P(None, DOC),
            P(None, DOC),
            P(None, SEQ),
        ),
        out_specs=P(SEQ, DOC),
        check_vma=False,
    )
```

time: 225 us -> 109 us (0.48)
  other arithmetic: 46.2 us -> 0.07 us
  local copies, waits for them, and re-layouts: 42.8 us -> 6.36 us
  blocking collectives: 23.8 us -> 0 us
  Pallas kernels: 0 us -> 18.2 us
  matrix products: 14.6 us -> 0 us
  waiting for transfers between devices: 51.8 us -> 37.4 us
    reduce_sum x6 -> x0, other arithmetic: 37.3 us -> none  [the longest x1 29.1 us: normalize(): variance = jnp.mean(centred * centred, axis=-1, keepdims=True)]
    all_to_all x5 -> x2, waiting for transfers between devices: 51.8 us -> 25.1 us  [the longest x1 19.9 us: on_device(): arrived = lax.all_to_all(sent, SEQ, 0, 0, tiled=True)]
    all_to_all x2 -> x0, blocking collectives: 23.8 us -> none  [the longest x1 15.2 us: sent_and_summed(): lax.all_to_all(cut_along(array, dim, devices), axis, 0, 0, tiled=True)]
    pallas_call x0 -> x5, Pallas kernels: none -> 18.2 us  [the longest x1 5.26 us: on_device(): call(far_kernel, jax.ShapeDtypeStruct((tokens, HEADS * DH), bf16), 4, 24,...]
    dot_general x7 -> x0, matrix products: 14.6 us -> none  [the longest x1 5.57 us: attend(): jnp.einsum('qhe,khe->hqk', query_block, window[0], preferred_element_type...]
    ppermute x2 -> x5, waiting for transfers between devices: 0.01 us -> 12.3 us  [the longest x1 6.49 us: on_device(): x2 = lax.ppermute(inputs, 'yh', SWAP)]
    all_to_all x5 -> x2, starting transfers between devices: 39 us -> 27.1 us  [the longest x1 20.5 us: on_device(): arrived = lax.all_to_all(sent, SEQ, 0, 0, tiled=True)]
    ppermute x2 -> x5, starting transfers between devices: 5.83 us -> 17.6 us  [the longest x1 7.72 us: on_device(): x2 = lax.ppermute(inputs, 'yh', SWAP)]
  transfers between devices with their start and end apart: 7 -> 7, of which waited for: 4 -> 5; matrix products, arithmetic and copies ran while one was open for 10% -> 4% of each run, Pallas kernels for 0% -> 6%
where the time goes in v1:
time: 109 us
  starting transfers between devices  44.7 us (41%)
  waiting for transfers between devices  37.4 us (34%)
  Pallas kernels  18.2 us (17%)
  local copies, waits for them, and re-layouts  6.36 us (6%)
  between operations  2.11 us (2%)
    all_to_all x1, starting transfers between devices, on_device(): arrived = lax.all_to_all(sent, SEQ, 0, 0, tiled=True)  20.5 us
    all_to_all x1, waiting for transfers between devices, on_device(): arrived = lax.all_to_all(sent, SEQ, 0, 0, tiled=True)  19.9 us
    ppermute x1, starting transfers between devices, on_device(): x2 = lax.ppermute(inputs, 'yh', SWAP)  7.72 us
    all_to_all x1, starting transfers between devices, on_device(): table = lax.all_to_all(chunk, SEQ, 0, 0, tiled=True)  6.58 us
    ppermute x1, waiting for transfers between devices, on_device(): x2 = lax.ppermute(inputs, 'yh', SWAP)  6.49 us
    pallas_call x1, Pallas kernels, on_device(): call(far_kernel, jax.ShapeDtypeStruct((tokens, HEADS * DH), bf16), 4, 24,...  5.26 us
    all_to_all x1, waiting for transfers between devices, on_device(): table = lax.all_to_all(chunk, SEQ, 0, 0, tiled=True)  5.2 us
    pallas_call x1, Pallas kernels, on_device(): call(near_kernel, [jax.ShapeDtypeStruct((tokens, HEADS * DH), f32), jax.S...  5.01 us
  transfers between devices with their start and end apart: 7, of which 5 were waited for; matrix products, arithmetic and copies ran while one was open for 4% of the time, Pallas kernels for 6%

profile of v1, /device:TPU:2, one launch (start us, length us, event | category | flops | bytes accessed | tf_op | source)
XLA Modules:
  0.0 108.8 jit_solution(1851789534828681376)
XLA Ops:
  0.0 7.7 %collective-permute-start.1 = (bf16[512,256]{1,0:T(8,128)(2,1)}, bf16[512,256]{1,0:T(8,128)(2,1)}, u32[]{:S(2)}, u32[]{:S(2)}) collective-permute-start(bf16[512,256]{1,0:T(8,128)(2,1)} %x0.1), channel_id=1, source_target_pairs={{0,2},{2,0},{1,3},{3,1},{4,6},{6,4},{5,7},{7,5},{8,10},{10,8},{9,1... | collective-permute-start | bytes 786440 | tf_op jit(solution)/shard_map/ppermute | solution.py:272
  7.7 1.9 %collective-permute-start = (bf16[512,256]{1,0:T(8,128)(2,1)}, bf16[512,256]{1,0:T(8,128)(2,1)}, u32[]{:S(2)}, u32[]{:S(2)}) collective-permute-start(bf16[512,256]{1,0:T(8,128)(2,1)} %x0.1), channel_id=1, source_target_pairs={{0,1},{1,0},{2,3},{3,2},{4,5},{5,4},{6,7},{7,6},{8,9},{9,8},{10,11... | collective-permute-start | bytes 786440 | tf_op jit(solution)/shard_map/ppermute | solution.py:273
  9.7 6.5 %collective-permute-done.1.x2 = bf16[512,256]{1,0:T(8,128)(2,1)} collective-permute-done((bf16[512,256]{1,0:T(8,128)(2,1)}, bf16[512,256]{1,0:T(8,128)(2,1)}, u32[]{:S(2)}, u32[]{:S(2)}) %collective-permute-start.1) | collective-permute-done | bytes 262176 | tf_op jit(solution)/shard_map/ppermute | solution.py:272
  16.2 1.9 %collective-permute-start.2 = (bf16[512,256]{1,0:T(8,128)(2,1)}, bf16[512,256]{1,0:T(8,128)(2,1)}, u32[]{:S(2)}, u32[]{:S(2)}) collective-permute-start(bf16[512,256]{1,0:T(8,128)(2,1)} %collective-permute-done.1.x2), channel_id=1, source_target_pairs={{0,1},{1,0},{2,3},{3,2},{4,5},{5,4},{6,7},{7,6},{8,9},{9,8},{10,11... | collective-permute-start | bytes 786440 | tf_op jit(solution)/shard_map/ppermute | solution.py:274
  18.1 0.0 copy-start
  18.1 0.0 copy-start.2
  18.1 2.9 %copy.8 = bf16[4,256,1024]{1,2,0:T(8,128)(2,1)S(1)} copy(bf16[4,256,1024]{2,1,0:T(8,128)(2,1)} %bitcast.12) | data formatting | bytes 4194304 | tf_op jit(solution)/shard_map/reshape | solution.py:280
  21.0 1.3 %fusion.1 = (s32[1,1]{1,0:T(1,128)}, s32[1,1]{1,0:T(1,128)}) fusion(s32[2,512]{1,0:T(2,128)} %param.13), kind=kLoop, calls=%fused_computation.4 | loop fusion | bytes 16 | tf_op jit(solution)/shard_map/slice | solution.py:256
  24.3 0.1 stack.33.scal
  24.4 0.0 copy-done
  24.4 0.0 copy-done.2
  24.4 1.2 %shard_map.73 = (bf16[4,512,128]{2,1,0:T(8,128)(2,1)S(1)}, bf16[4,512,256]{2,1,0:T(8,128)(2,1)S(1)}) custom-call(s32[7]{0:T(128)S(1)} %stack.33.scal, bf16[512,256]{1,0:T(8,128)(2,1)S(1)} %copy-done.2, bf16[2,512,256]{2,1,0:T(8,128)(2,1)S(1)} %copy-done), custom_call_target="tpu_custom_call" | custom-call | bytes 3145728 | tf_op jit(solution)/shard_map/pallas_call | solution.py:281
  25.5 0.0 collective-permute-done.x1
  25.5 0.0 collective-permute-done.2.x3
  25.6 0.0 copy-start.3
  25.6 0.9 copy-done.3
  26.5 0.0 copy-start.4
  26.5 0.0 copy-start.5
  26.5 4.4 %shard_map.74 = bf16[128,16,128]{2,1,0:T(8,128)(2,1)S(1)} custom-call(s32[7]{0:T(128)S(1)} %stack.33.scal, bf16[512,256]{1,0:T(8,128)(2,1)S(1)} %copy-done.3, bf16[512,256]{1,0:T(8,128)(2,1)} %collective-permute-done.x1, bf16[512,256]{1,0:T(8,128)(2,1)} %collective-permute-done.1.x2, bf16[512,256]{1,0:T(8,128)(2,1)} %collective-permute-done.2.x3, ...), custom_call_target="tpu_custom_call" | custom-call | flops 1342177280 | bytes 5242880 | tf_op jit(solution)/shard_map/pallas_call | solution.py:290
  31.0 0.0 copy-start.1
  31.0 0.8 copy-done.1
  31.8 20.5 %all-to-all-start = ((bf16[128,16,128]{2,1,0:T(8,128)(2,1)}), bf16[128,16,128]{2,1,0:T(8,128)(2,1)S(1)}, u32[]{:S(2)}, u32[]{:S(2)}) async-start(bf16[128,16,128]{2,1,0:T(8,128)(2,1)} %copy-done.1), calls=%async_computation | async-start | bytes 1048576 | tf_op jit(solution)/shard_map/all_to_all | solution.py:295
  52.3 0.0 copy-done.4
  52.3 0.0 copy-done.5
  52.3 0.1 constant_dynamic-slice_fusion
  52.4 0.1 reshape.10.gain_ref
  52.5 0.1 reshape.11.bias_ref
  52.6 0.1 pad_add_fusion.scal
  52.7 19.9 %all-to-all-done.in_ref = bf16[128,16,128]{2,1,0:T(8,128)(2,1)S(1)} async-done(((bf16[128,16,128]{2,1,0:T(8,128)(2,1)}), bf16[128,16,128]{2,1,0:T(8,128)(2,1)S(1)}, u32[]{:S(2)}, u32[]{:S(2)}) %all-to-all-start) | async-done | bytes 524320 | tf_op jit(solution)/shard_map/all_to_all | solution.py:295
  72.6 2.4 %shard_map.75 = bf16[128,16,128]{2,1,0:T(8,128)(2,1)} custom-call(s32[2]{0:T(128)S(1)} %pad_add_fusion.scal, bf16[128,16,128]{2,1,0:T(8,128)(2,1)S(1)} %all-to-all-done.in_ref, f32[1,128]{1,0:T(1,128)S(1)} %reshape.10.gain_ref, f32[1,128]{1,0:T(1,128)S(1)} %reshape.11.bias_ref), custom_call_target="tpu_custom_call" | custom-call | bytes 1048576 | tf_op jit(solution)/shard_map/pallas_call | solution.py:309
  75.0 6.6 %all-to-all-start.1 = ((bf16[128,16,128]{2,1,0:T(8,128)(2,1)}), bf16[128,16,128]{2,1,0:T(8,128)(2,1)S(1)}, u32[]{:S(2)}, u32[]{:S(2)}) async-start(bf16[128,16,128]{2,1,0:T(8,128)(2,1)} %shard_map.75), calls=%async_computation.1 | async-start | bytes 1048576 | tf_op jit(solution)/shard_map/all_to_all | solution.py:314
  81.6 3.4 %collective-permute-start.3 = (bf16[2,128,256]{2,1,0:T(8,128)(2,1)S(1)}, bf16[2,128,256]{2,1,0:T(8,128)(2,1)S(1)}, u32[]{:S(2)}, u32[]{:S(2)}) collective-permute-start(bf16[2,128,256]{2,1,0:T(8,128)(2,1)S(1)} %get-tuple-element.14), channel_id=1, source_target_pairs={{0,4},{4,8},{8,12},{12,16},{16,20},{20,24},{24,28},{28,32},{32,36}... | collective-permute-start | bytes 393224 | tf_op jit(solution)/shard_map/ppermute | solution.py:277
  85.0 2.6 %collective-permute-start.4 = (bf16[2,128,256]{2,1,0:T(8,128)(2,1)S(1)}, bf16[2,128,256]{2,1,0:T(8,128)(2,1)S(1)}, u32[]{:S(2)}, u32[]{:S(2)}) collective-permute-start(bf16[2,128,256]{2,1,0:T(8,128)(2,1)S(1)} %get-tuple-element.13), channel_id=1, source_target_pairs={{4,0},{8,4},{12,8},{16,12},{20,16},{24,20},{28,24},{32,28},{36,32}... | collective-permute-start | bytes 393224 | tf_op jit(solution)/shard_map/ppermute | solution.py:278
  87.6 2.5 %collective-permute-done.3.before_ref = bf16[2,128,256]{2,1,0:T(8,128)(2,1)S(1)} collective-permute-done((bf16[2,128,256]{2,1,0:T(8,128)(2,1)S(1)}, bf16[2,128,256]{2,1,0:T(8,128)(2,1)S(1)}, u32[]{:S(2)}, u32[]{:S(2)}) %collective-permute-start.3) | collective-permute-done | bytes 131104 | tf_op jit(solution)/shard_map/ppermute | solution.py:277
  90.1 3.3 %collective-permute-done.4.after_ref = bf16[2,128,256]{2,1,0:T(8,128)(2,1)S(1)} collective-permute-done((bf16[2,128,256]{2,1,0:T(8,128)(2,1)S(1)}, bf16[2,128,256]{2,1,0:T(8,128)(2,1)S(1)}, u32[]{:S(2)}, u32[]{:S(2)}) %collective-permute-start.4) | collective-permute-done | bytes 131104 | tf_op jit(solution)/shard_map/ppermute | solution.py:278
  93.4 5.0 %shard_map.76 = (f32[512,256]{1,0:T(8,128)S(1)}, f32[512,128]{1,0:T(8,128)S(1)}) custom-call(s32[7]{0:T(128)S(1)} %stack.33.scal, bf16[512,256]{1,0:T(8,128)(2,1)S(1)} %copy-done.2, bf16[2,512,256]{2,1,0:T(8,128)(2,1)S(1)} %copy-done, bf16[2,128,256]{2,1,0:T(8,128)(2,1)S(1)} %collective-permute-done.3.before_ref, ...), custom_call_target="tpu_custom_call" | custom-call | flops 402653184 | bytes 2097152 | tf_op jit(solution)/shard_map/pallas_call | solution.py:297
  98.4 5.2 %all-to-all-done.1.tab_ref = bf16[128,16,128]{2,1,0:T(8,128)(2,1)S(1)} async-done(((bf16[128,16,128]{2,1,0:T(8,128)(2,1)}), bf16[128,16,128]{2,1,0:T(8,128)(2,1)S(1)}, u32[]{:S(2)}, u32[]{:S(2)}) %all-to-all-start.1) | async-done | bytes 524320 | tf_op jit(solution)/shard_map/all_to_all | solution.py:314
  103.6 5.3 %shard_map.77 = bf16[512,256]{1,0:T(8,128)(2,1)} custom-call(s32[7]{0:T(128)S(1)} %stack.33.scal, bf16[4,512,128]{2,1,0:T(8,128)(2,1)S(1)} %get-tuple-element.9.q2_ref, bf16[128,16,128]{2,1,0:T(8,128)(2,1)S(1)} %all-to-all-done.1.tab_ref, f32[512,256]{1,0:T(8,128)S(1)} %get-tuple-element.11.o_ref, f32[512,128]{1,0:T(8,128)S(1)} %get-tuple-element.12.stat_ref), custom_call_target="tpu_custom_call" | custom-call | flops 268435456 | bytes 2097152 | tf_op jit(solution)/shard_map/pallas_call | solution.py:316
  (1 shorter events, 0.0 us)
Async XLA Ops:
  0.0 16.2 %collective-permute-start.1 = (bf16[512,256]{1,0:T(8,128)(2,1)}, bf16[512,256]{1,0:T(8,128)(2,1)}, u32[]{:S(2)}, u32[]{:S(2)}) collective-permute-start(bf16[512,256]{1,0:T(8,128)(2,1)} %x0.1), channel_id=1, source_target_pairs={{0,2},{2,0},{1,3},{3,1},{4,6},{6,4},{5,7},{7,5},{8,10},{10,8},{9,1... | collective-permute-start | bytes 786440 | tf_op jit(solution)/shard_map/ppermute | solution.py:272
  7.7 17.8 %collective-permute-start = (bf16[512,256]{1,0:T(8,128)(2,1)}, bf16[512,256]{1,0:T(8,128)(2,1)}, u32[]{:S(2)}, u32[]{:S(2)}) collective-permute-start(bf16[512,256]{1,0:T(8,128)(2,1)} %x0.1), channel_id=1, source_target_pairs={{0,1},{1,0},{2,3},{3,2},{4,5},{5,4},{6,7},{7,6},{8,9},{9,8},{10,11... | collective-permute-start | bytes 786440 | tf_op jit(solution)/shard_map/ppermute | solution.py:273
  16.2 9.4 %collective-permute-start.2 = (bf16[512,256]{1,0:T(8,128)(2,1)}, bf16[512,256]{1,0:T(8,128)(2,1)}, u32[]{:S(2)}, u32[]{:S(2)}) collective-permute-start(bf16[512,256]{1,0:T(8,128)(2,1)} %collective-permute-done.1.x2), channel_id=1, source_target_pairs={{0,1},{1,0},{2,3},{3,2},{4,5},{5,4},{6,7},{7,6},{8,9},{9,8},{10,11... | collective-permute-start | bytes 786440 | tf_op jit(solution)/shard_map/ppermute | solution.py:274
  18.1 6.3 %copy-start = (bf16[2,512,256]{2,1,0:T(8,128)(2,1)S(1)}, bf16[2,512,256]{2,1,0:T(8,128)(2,1)}, u32[]{:S(2)}) copy-start(bf16[2,512,256]{2,1,0:T(8,128)(2,1)} %kv_ref.3) | copy-start | bytes 1572868
  18.1 6.3 %copy-start.2 = (bf16[512,256]{1,0:T(8,128)(2,1)S(1)}, bf16[512,256]{1,0:T(8,128)(2,1)}, u32[]{:S(2)}) copy-start(bf16[512,256]{1,0:T(8,128)(2,1)} %q_ref.3) | copy-start | bytes 786436
  25.6 1.0 copy-start.3
  26.5 25.8 %copy-start.4 = (f32[2,256]{1,0:T(2,128)S(1)}, f32[2,256]{1,0:T(2,128)}, u32[]{:S(2)}) copy-start(f32[2,256]{1,0:T(2,128)} %param.12) | copy-start | bytes 6148
  26.5 25.8 %copy-start.5 = (f32[2,256]{1,0:T(2,128)S(1)}, f32[2,256]{1,0:T(2,128)}, u32[]{:S(2)}) copy-start(f32[2,256]{1,0:T(2,128)} %param.11) | copy-start | bytes 6148
  31.0 0.8 copy-start.1
  31.8 40.8 %all-to-all-start = ((bf16[128,16,128]{2,1,0:T(8,128)(2,1)}), bf16[128,16,128]{2,1,0:T(8,128)(2,1)S(1)}, u32[]{:S(2)}, u32[]{:S(2)}) async-start(bf16[128,16,128]{2,1,0:T(8,128)(2,1)} %copy-done.1), calls=%async_computation | async-start | bytes 1048576 | tf_op jit(solution)/shard_map/all_to_all | solution.py:295
  75.0 28.6 %all-to-all-start.1 = ((bf16[128,16,128]{2,1,0:T(8,128)(2,1)}), bf16[128,16,128]{2,1,0:T(8,128)(2,1)S(1)}, u32[]{:S(2)}, u32[]{:S(2)}) async-start(bf16[128,16,128]{2,1,0:T(8,128)(2,1)} %shard_map.75), calls=%async_computation.1 | async-start | bytes 1048576 | tf_op jit(solution)/shard_map/all_to_all | solution.py:314
  81.6 8.6 %collective-permute-start.3 = (bf16[2,128,256]{2,1,0:T(8,128)(2,1)S(1)}, bf16[2,128,256]{2,1,0:T(8,128)(2,1)S(1)}, u32[]{:S(2)}, u32[]{:S(2)}) collective-permute-start(bf16[2,128,256]{2,1,0:T(8,128)(2,1)S(1)} %get-tuple-element.14), channel_id=1, source_target_pairs={{0,4},{4,8},{8,12},{12,16},{16,20},{20,24},{24,28},{28,32},{32,36}... | collective-permute-start | bytes 393224 | tf_op jit(solution)/shard_map/ppermute | solution.py:277
  85.0 8.4 %collective-permute-start.4 = (bf16[2,128,256]{2,1,0:T(8,128)(2,1)S(1)}, bf16[2,128,256]{2,1,0:T(8,128)(2,1)S(1)}, u32[]{:S(2)}, u32[]{:S(2)}) collective-permute-start(bf16[2,128,256]{2,1,0:T(8,128)(2,1)S(1)} %get-tuple-element.13), channel_id=1, source_target_pairs={{4,0},{8,4},{12,8},{16,12},{20,16},{24,20},{28,24},{32,28},{36,32}... | collective-permute-start | bytes 393224 | tf_op jit(solution)/shard_map/ppermute | solution.py:278

commit v2 on v1

--- a/solution.py
+++ b/solution.py
@@ -1,5 +1,3 @@
-import functools
-
 import jax
 import jax.numpy as jnp
 from jax import lax
@@ -7,6 +5,7 @@
 from jax.experimental.pallas import tpu as pltpu
 from jax.sharding import Mesh
 from jax.sharding import PartitionSpec as P
+
 
 DH = 64
 R = 256
@@ -68,7 +67,7 @@
             kvh_ref[h, :, LANES:] = jnp.where(second, joined, 0.0).astype(bf16)
 
 
-def near_kernel(scal, q_ref, kv_ref, before_ref, after_ref, o_ref, stat_ref):
+def near_kernel(scal, q_ref, kv_ref, before_ref, after_ref, o_ref, top_ref, sum_ref):
     tokens = q_ref.shape[0]
     local, base, total = scal[0], scal[1], scal[2]
     blocks = tokens // W
@@ -77,7 +76,6 @@
     col = lax.broadcasted_iota(jnp.int32, (W, span), 1)
     band = (col >= row) & (col - row <= 2 * W)
     left = lanes_of((W, LANES)) < DH
-    lane = lanes_of((W, LANES))
 
     def piece(s, at, cols):
         if at < 0:
@@ -95,7 +93,6 @@
             & (key_pos + base >= 0)
             & (key_pos + base < total)
         )
-        stats = jnp.zeros((W, LANES), f32)
         for pair in range(HEADS // 2):
             cols = slice(pair * LANES, (pair + 1) * LANES)
             query = q_ref[b * W : (b + 1) * W, cols].astype(f32) * 0.125
@@ -110,10 +107,9 @@
                 weight = jnp.exp(scores - top)
                 total_w = jnp.sum(weight, axis=1, keepdims=True)
                 outs.append(jnp.dot(weight.astype(bf16), values, preferred_element_type=f32))
-                stats = jnp.where(lane == h, top, stats)
-                stats = jnp.where(lane == HEADS + h, total_w, stats)
+                top_ref[h, b * W : (b + 1) * W] = jnp.broadcast_to(top, (W, LANES))
+                sum_ref[h, b * W : (b + 1) * W] = jnp.broadcast_to(total_w, (W, LANES))
             o_ref[b * W : (b + 1) * W, cols] = jnp.where(left, outs[0], outs[1])
-        stat_ref[b * W : (b + 1) * W, :] = stats
 
 
 def pieces_of(top):
@@ -122,8 +118,16 @@
     return a, b, top - a - b
 
 
-def project_kernel(scal, x0, x1, x2, x3, wt_ref, kvh_ref, out_ref):
-    tokens = x0.shape[0]
+def partial_kernel(scal, x0, x1, wt_ref, acc_ref):
+    acc_ref[...] = dot_nt(wt_ref[scal[3]], x0[...]) + dot_nt(wt_ref[scal[4]], x1[...])
+
+
+def more_kernel(scal, x2, wt_ref, acc_ref, out_ref):
+    out_ref[...] = acc_ref[...] + dot_nt(wt_ref[scal[5]], x2[...])
+
+
+def project_kernel(scal, x3, wt_ref, acc_ref, kvh_ref, out_ref, held, sems):
+    tokens = x3.shape[0]
     local = scal[0]
     second = lax.broadcasted_iota(jnp.int32, (R, tokens), 1) >= local
     mixed = jnp.logical_and(local > 0, local < tokens)
@@ -131,12 +135,10 @@
     at_a = lane == 0
     at_b = lane == DH
     left = lane < DH
+    copies = []
     for h in range(HEADS):
         rows = slice(h * R, (h + 1) * R)
-        logits = dot_nt(wt_ref[scal[3], rows, :], x0[...])
-        logits += dot_nt(wt_ref[scal[4], rows, :], x1[...])
-        logits += dot_nt(wt_ref[scal[5], rows, :], x2[...])
-        logits += dot_nt(wt_ref[scal[6], rows, :], x3[...])
+        logits = acc_ref[rows, :] + dot_nt(wt_ref[scal[6], rows, :], x3[...])
         top0 = jnp.maximum(jnp.max(jnp.where(second, LOW, logits), axis=1, keepdims=True), LOW)
         top1 = jnp.maximum(jnp.max(jnp.where(second, logits, LOW), axis=1, keepdims=True), LOW)
         a0, b0, c0 = pieces_of(top0)
@@ -162,7 +164,14 @@
         packed = jnp.concatenate(
             [hi.reshape(parts, ROWS, LANES), rest.reshape(parts, ROWS, LANES)], axis=1
         )
-        out_ref[h * parts : (h + 1) * parts] = packed.astype(bf16)
+        held[h] = packed.astype(bf16)
+        copy = pltpu.make_async_copy(
+            held.at[h], out_ref.at[pl.ds(h * parts, parts)], sems.at[h]
+        )
+        copy.start()
+        copies.append(copy)
+    for copy in copies:
+        copy.wait()
 
 
 def combine_kernel(scal, in_ref, gain_ref, bias_ref, out_ref):
@@ -218,14 +227,13 @@
     out_ref[...] = jnp.broadcast_to(chunk, out_ref.shape).astype(bf16)
 
 
-def far_kernel(scal, q2_ref, tab_ref, o_ref, stat_ref, out_ref):
+def far_kernel(scal, q2_ref, tab_ref, o_ref, top_ref, sum_ref, out_ref):
     tokens = o_ref.shape[0]
     local = scal[0]
-    lane = lanes_of((tokens, LANES))
-    left = lane < DH
-    second = lax.broadcasted_iota(jnp.int32, (tokens, LANES), 0) >= local
+    shape = (tokens, LANES)
+    left = lanes_of(shape) < DH
+    second = lax.broadcasted_iota(jnp.int32, shape, 0) >= local
     parts = R // ROWS
-    stats = stat_ref[...]
     for pair in range(HEADS // 2):
         cols = slice(pair * LANES, (pair + 1) * LANES)
         near = o_ref[:, cols]
@@ -236,13 +244,17 @@
             keys = table[:, :ROWS].reshape(R, LANES).astype(bf16)
             values = table[:, ROWS:].reshape(R, LANES).astype(bf16)
             scores = dot_nt(q2_ref[h], keys)
-            near_top = stats[:, h : h + 1]
-            near_total = stats[:, HEADS + h : HEADS + h + 1]
-            top = jnp.maximum(jnp.max(scores, axis=1, keepdims=True), near_top)
-            weight = jnp.exp(scores - top)
+            low, high = scores[:, :LANES], scores[:, LANES:]
+            near_top = top_ref[h]
+            top = jnp.max(jnp.maximum(low, high), axis=1, keepdims=True)
+            top = jnp.maximum(jnp.broadcast_to(top, shape), near_top)
+            low = jnp.exp(low - top)
+            high = jnp.exp(high - top)
             scale = jnp.exp(near_top - top)
-            total = jnp.sum(weight, axis=1, keepdims=True) + near_total * scale
-            far = jnp.dot(weight.astype(bf16), values, preferred_element_type=f32)
+            total = jnp.broadcast_to(jnp.sum(low + high, axis=1, keepdims=True), shape)
+            total = total + sum_ref[h] * scale
+            weight = jnp.concatenate([low.astype(bf16), high.astype(bf16)], axis=1)
+            far = jnp.dot(weight, values, preferred_element_type=f32)
             swap = second if half == 0 else jnp.logical_not(second)
             far = jnp.where(swap, pltpu.roll(far, DH, 1), far)
             outs.append((near * scale + far) / total)
@@ -287,20 +299,34 @@
         2, 16, 0, 3 << 20,
     )(scal, queries, keys_values)
 
-    sent = call(
+    slots = HEADS * R
+    flops = 2 * tokens * slots * width
+    acc_shape = jax.ShapeDtypeStruct((slots, tokens), f32)
+    acc = call(partial_kernel, acc_shape, 3, 16, 2 * flops, 5 << 20)(
+        scal, inputs, x1, weight_t
+    )
+    acc = call(more_kernel, acc_shape, 3, 16, flops, 6 << 20)(scal, x2, weight_t, acc)
+    sent = pl.pallas_call(
         project_kernel,
-        jax.ShapeDtypeStruct((shards, 2 * ROWS, LANES), bf16),
-        6, 24, 2 * tokens * HEADS * R * (4 * width + 2 * LANES), 5 << 20, tokens * HEADS * R,
-    )(scal, inputs, x1, x2, x3, weight_t, kvh)
+        out_shape=jax.ShapeDtypeStruct((shards, 2 * ROWS, LANES), bf16),
+        in_specs=[SMEM] + [VMEM] * 4,
+        out_specs=pl.BlockSpec(memory_space=pltpu.HBM),
+        scratch_shapes=[
+            pltpu.VMEM((HEADS, R // ROWS, 2 * ROWS, LANES), bf16),
+            pltpu.SemaphoreType.DMA((HEADS,)),
+        ],
+        compiler_params=pltpu.CompilerParams(vmem_limit_bytes=24 << 20),
+        cost_estimate=pl.CostEstimate(
+            flops=2 * flops, bytes_accessed=5 << 20, transcendentals=tokens * slots
+        ),
+    )(scal, x3, weight_t, acc, kvh)
     arrived = lax.all_to_all(sent, SEQ, 0, 0, tiled=True)
 
-    near, stats = call(
+    rep = jax.ShapeDtypeStruct((HEADS, tokens, LANES), f32)
+    near, tops, sums = call(
         near_kernel,
-        [
-            jax.ShapeDtypeStruct((tokens, HEADS * DH), f32),
-            jax.ShapeDtypeStruct((tokens, LANES), f32),
-        ],
-        4, 16, 4 * tokens * 3 * W * HEADS * LANES, 2 << 20, tokens * 3 * W * HEADS,
+        [jax.ShapeDtypeStruct((tokens, HEADS * DH), f32), rep, rep],
+        4, 8, 4 * tokens * 3 * W * HEADS * LANES, 2 << 20, tokens * 3 * W * HEADS,
     )(scal, queries, keys_values, before, after)
 
     head = shard * ROWS // R
@@ -309,15 +335,15 @@
     chunk = call(
         combine_kernel,
         jax.ShapeDtypeStruct((shards, 2 * ROWS, LANES), bf16),
-        3, 16, 0, 1 << 20, 1 << 17,
+        3, 8, 0, 1 << 20, 1 << 17,
     )(scal2, arrived, gain, bias)
     table = lax.all_to_all(chunk, SEQ, 0, 0, tiled=True)
 
     return call(
         far_kernel,
         jax.ShapeDtypeStruct((tokens, HEADS * DH), bf16),
-        4, 24, 4 * tokens * R * HEADS * LANES, 2 << 20, tokens * R * HEADS,
-    )(scal, q2, table, near, stats)
+        5, 12, 4 * tokens * R * HEADS * LANES, 2 << 20, tokens * R * HEADS,
+    )(scal, q2, table, near, tops, sums)
 
 
 def solution(mesh):

time: 109 us -> 111 us (1.018)
  the two profiles are of different devices: /device:TPU:2 before, /device:TPU:16 now
where the time goes in v2:
time: 111 us
  starting transfers between devices  43.6 us (39%)
  waiting for transfers between devices  38 us (34%)
  Pallas kernels  19.3 us (17%)
  local copies, waits for them, and re-layouts  7.75 us (7%)
  between operations  2.18 us (2%)
    all_to_all x1, waiting for transfers between devices, on_device(): arrived = lax.all_to_all(sent, SEQ, 0, 0, tiled=True)  18.7 us
    all_to_all x1, starting transfers between devices, on_device(): arrived = lax.all_to_all(sent, SEQ, 0, 0, tiled=True)  17.9 us
    ppermute x1, waiting for transfers between devices, on_device(): x2 = lax.ppermute(inputs, 'yh', SWAP)  10.9 us
    ppermute x1, waiting for transfers between devices, on_device(): before = lax.ppermute(keys_values[:, tokens - W:], SEQ, up)  8.34 us
    all_to_all x1, starting transfers between devices, on_device(): table = lax.all_to_all(chunk, SEQ, 0, 0, tiled=True)  7.83 us
    ppermute x1, starting transfers between devices, on_device(): x2 = lax.ppermute(inputs, 'yh', SWAP)  5.92 us
    pallas_call x1, Pallas kernels, on_device(): call(near_kernel, [jax.ShapeDtypeStruct((tokens, HEADS * DH), f32), rep,...  4.97 us
    ppermute x1, starting transfers between devices, on_device(): after = lax.ppermute(keys_values[:, :W], SEQ, down)  4.75 us
  transfers between devices with their start and end apart: 7, of which 3 were waited for; matrix products, arithmetic and copies ran while one was open for 4% of the time, Pallas kernels for 8%

profile of v2, /device:TPU:16, one launch (start us, length us, event | category | flops | bytes accessed | tf_op | source)
XLA Modules:
  0.0 110.9 jit_solution(10421077356918808154)
XLA Ops:
  0.0 5.9 %collective-permute-start = (bf16[512,256]{1,0:T(8,128)(2,1)}, bf16[512,256]{1,0:T(8,128)(2,1)}, u32[]{:S(2)}, u32[]{:S(2)}) collective-permute-start(bf16[512,256]{1,0:T(8,128)(2,1)} %x0.1), channel_id=1, source_target_pairs={{0,2},{2,0},{1,3},{3,1},{4,6},{6,4},{5,7},{7,5},{8,10},{10,8},{9,1... | collective-permute-start | bytes 786440 | tf_op jit(solution)/shard_map/ppermute | solution.py:284
  5.9 1.9 %collective-permute-start.2 = (bf16[512,256]{1,0:T(8,128)(2,1)}, bf16[512,256]{1,0:T(8,128)(2,1)}, u32[]{:S(2)}, u32[]{:S(2)}) collective-permute-start(bf16[512,256]{1,0:T(8,128)(2,1)} %x0.1), channel_id=1, source_target_pairs={{0,1},{1,0},{2,3},{3,2},{4,5},{5,4},{6,7},{7,6},{8,9},{9,8},{10,11... | collective-permute-start | bytes 786440 | tf_op jit(solution)/shard_map/ppermute | solution.py:285
  7.9 10.9 %collective-permute-done.x2 = bf16[512,256]{1,0:T(8,128)(2,1)} collective-permute-done((bf16[512,256]{1,0:T(8,128)(2,1)}, bf16[512,256]{1,0:T(8,128)(2,1)}, u32[]{:S(2)}, u32[]{:S(2)}) %collective-permute-start) | collective-permute-done | bytes 262176 | tf_op jit(solution)/shard_map/ppermute | solution.py:284
  18.8 1.9 %collective-permute-start.1 = (bf16[512,256]{1,0:T(8,128)(2,1)}, bf16[512,256]{1,0:T(8,128)(2,1)}, u32[]{:S(2)}, u32[]{:S(2)}) collective-permute-start(bf16[512,256]{1,0:T(8,128)(2,1)} %collective-permute-done.x2), channel_id=1, source_target_pairs={{0,1},{1,0},{2,3},{3,2},{4,5},{5,4},{6,7},{7,6},{8,9},{9,8},{10,11... | collective-permute-start | bytes 786440 | tf_op jit(solution)/shard_map/ppermute | solution.py:286
  20.7 0.0 copy-start
  20.7 0.0 copy-start.3
  20.7 2.9 %copy.8 = bf16[4,256,1024]{1,2,0:T(8,128)(2,1)S(1)} copy(bf16[4,256,1024]{2,1,0:T(8,128)(2,1)} %bitcast.14) | data formatting | bytes 4194304 | tf_op jit(solution)/shard_map/reshape | solution.py:292
  23.7 1.3 %fusion.1 = (s32[1,1]{1,0:T(1,128)}, s32[1,1]{1,0:T(1,128)}) fusion(s32[2,512]{1,0:T(2,128)} %param.13), kind=kLoop, calls=%fused_computation.4 | loop fusion | bytes 16 | tf_op jit(solution)/shard_map/slice | solution.py:268
  26.9 0.1 stack.33.scal
  27.0 0.0 copy-done
  27.0 0.0 copy-start.4
  27.0 1.0 copy-done.4
  27.9 1.2 %shard_map.73 = (bf16[4,512,128]{2,1,0:T(8,128)(2,1)S(1)}, bf16[4,512,256]{2,1,0:T(8,128)(2,1)S(1)}) custom-call(s32[7]{0:T(128)S(1)} %stack.33.scal, bf16[512,256]{1,0:T(8,128)(2,1)S(1)} %copy-done.4, bf16[2,512,256]{2,1,0:T(8,128)(2,1)S(1)} %copy-done), custom_call_target="tpu_custom_call" | custom-call | bytes 3145728 | tf_op jit(solution)/shard_map/pallas_call | solution.py:293
  29.1 0.0 collective-permute-done.2.x1
  29.1 0.0 copy-done.3
  29.1 1.7 %shard_map.74.acc_ref = f32[1024,512]{1,0:T(8,128)S(1)} custom-call(s32[7]{0:T(128)S(1)} %stack.33.scal, bf16[512,256]{1,0:T(8,128)(2,1)S(1)} %copy-done.3, bf16[512,256]{1,0:T(8,128)(2,1)} %collective-permute-done.2.x1, bf16[4,1024,256]{2,1,0:T(8,128)(2,1)S(1)} %bitcast.11), custom_call_target="tpu_custom_call" | custom-call | flops 536870912 | bytes 5242880 | tf_op jit(solution)/shard_map/pallas_call | solution.py:305
  30.8 1.4 %shard_map.75.acc_ref = f32[1024,512]{1,0:T(8,128)S(1)} custom-call(s32[7]{0:T(128)S(1)} %stack.33.scal, bf16[512,256]{1,0:T(8,128)(2,1)} %collective-permute-done.x2, bf16[4,1024,256]{2,1,0:T(8,128)(2,1)S(1)} %bitcast.12, f32[1024,512]{1,0:T(8,128)S(1)} %shard_map.74.acc_ref), custom_call_target="tpu_custom_call" | custom-call | flops 268435456 | bytes 6291456 | tf_op jit(solution)/shard_map/pallas_call | solution.py:308
  32.2 0.0 collective-permute-done.1.x3
  32.2 0.0 copy-start.6
  32.3 0.0 copy-start.7
  32.3 4.1 %shard_map.76 = bf16[128,16,128]{2,1,0:T(8,128)(2,1)} custom-call(s32[7]{0:T(128)S(1)} %stack.33.scal, bf16[512,256]{1,0:T(8,128)(2,1)} %collective-permute-done.1.x3, bf16[4,1024,256]{2,1,0:T(8,128)(2,1)S(1)} %bitcast.13, f32[1024,512]{1,0:T(8,128)S(1)} %shard_map.75.acc_ref, bf16[4,512,256]{2,1,0:T(8,128)(2,1)S(1)} %get-tuple-element.11.kvh_ref), custom_call_target="tpu_custom_call" | custom-call | flops 536870912 | bytes 5242880 | tf_op jit(solution)/shard_map/pallas_call | solution.py:309
  36.4 0.0 copy-start.5
  36.4 17.9 %all-to-all-start = ((bf16[128,16,128]{2,1,0:T(8,128)(2,1)}), bf16[128,16,128]{2,1,0:T(8,128)(2,1)S(1)}, u32[]{:S(2)}, u32[]{:S(2)}) async-start(bf16[128,16,128]{2,1,0:T(8,128)(2,1)} %shard_map.76), calls=%async_computation | async-start | bytes 1048576 | tf_op jit(solution)/shard_map/all_to_all | solution.py:323
  54.3 0.0 copy-done.6
  54.3 0.0 copy-done.7
  54.3 0.1 constant_dynamic-slice_fusion
  54.4 0.1 reshape.10.gain_ref
  54.5 0.1 reshape.11.bias_ref
  54.6 0.1 pad_add_fusion.scal
  54.6 18.7 %all-to-all-done.in_ref = bf16[128,16,128]{2,1,0:T(8,128)(2,1)S(1)} async-done(((bf16[128,16,128]{2,1,0:T(8,128)(2,1)}), bf16[128,16,128]{2,1,0:T(8,128)(2,1)S(1)}, u32[]{:S(2)}, u32[]{:S(2)}) %all-to-all-start) | async-done | bytes 524320 | tf_op jit(solution)/shard_map/all_to_all | solution.py:323
  73.4 2.4 %shard_map.77 = bf16[128,16,128]{2,1,0:T(8,128)(2,1)} custom-call(s32[2]{0:T(128)S(1)} %pad_add_fusion.scal, bf16[128,16,128]{2,1,0:T(8,128)(2,1)S(1)} %all-to-all-done.in_ref, f32[1,128]{1,0:T(1,128)S(1)} %reshape.10.gain_ref, f32[1,128]{1,0:T(1,128)S(1)} %reshape.11.bias_ref), custom_call_target="tpu_custom_call" | custom-call | bytes 1048576 | tf_op jit(solution)/shard_map/pallas_call | solution.py:335
  75.7 7.8 %all-to-all-start.1 = ((bf16[128,16,128]{2,1,0:T(8,128)(2,1)}), bf16[128,16,128]{2,1,0:T(8,128)(2,1)S(1)}, u32[]{:S(2)}, u32[]{:S(2)}) async-start(bf16[128,16,128]{2,1,0:T(8,128)(2,1)} %shard_map.77), calls=%async_computation.1 | async-start | bytes 1048576 | tf_op jit(solution)/shard_map/all_to_all | solution.py:340
  83.6 3.4 %collective-permute-start.3 = (bf16[2,128,256]{2,1,0:T(8,128)(2,1)S(1)}, bf16[2,128,256]{2,1,0:T(8,128)(2,1)S(1)}, u32[]{:S(2)}, u32[]{:S(2)}) collective-permute-start(bf16[2,128,256]{2,1,0:T(8,128)(2,1)S(1)} %get-tuple-element.16), channel_id=1, source_target_pairs={{0,4},{4,8},{8,12},{12,16},{16,20},{20,24},{24,28},{28,32},{32,36}... | collective-permute-start | bytes 393224 | tf_op jit(solution)/shard_map/ppermute | solution.py:289
  87.0 4.8 %collective-permute-start.4 = (bf16[2,128,256]{2,1,0:T(8,128)(2,1)S(1)}, bf16[2,128,256]{2,1,0:T(8,128)(2,1)S(1)}, u32[]{:S(2)}, u32[]{:S(2)}) collective-permute-start(bf16[2,128,256]{2,1,0:T(8,128)(2,1)S(1)} %get-tuple-element.15), channel_id=1, source_target_pairs={{4,0},{8,4},{12,8},{16,12},{20,16},{24,20},{28,24},{32,28},{36,32}... | collective-permute-start | bytes 393224 | tf_op jit(solution)/shard_map/ppermute | solution.py:290
  91.7 8.3 %collective-permute-done.3.before_ref = bf16[2,128,256]{2,1,0:T(8,128)(2,1)S(1)} collective-permute-done((bf16[2,128,256]{2,1,0:T(8,128)(2,1)S(1)}, bf16[2,128,256]{2,1,0:T(8,128)(2,1)S(1)}, u32[]{:S(2)}, u32[]{:S(2)}) %collective-permute-start.3) | collective-permute-done | bytes 131104 | tf_op jit(solution)/shard_map/ppermute | solution.py:289
  100.1 0.0 collective-permute-done.4.after_ref
  100.1 0.0 copy-done.5
  100.1 5.0 %shard_map.78 = (f32[512,256]{1,0:T(8,128)S(1)}, f32[4,512,128]{2,1,0:T(8,128)S(1)}, f32[4,512,128]{2,1,0:T(8,128)S(1)}) custom-call(s32[7]{0:T(128)S(1)} %stack.33.scal, bf16[512,256]{1,0:T(8,128)(2,1)S(1)} %copy-done.5, bf16[2,512,256]{2,1,0:T(8,128)(2,1)S(1)} %copy-done, bf16[2,128,256]{2,1,0:T(8,128)(2,1)S(1)} %collective-permute-done.3.before_ref, ...), custom_call_target="tpu_custom_call" | custom-call | flops 402653184 | bytes 2097152 | tf_op jit(solution)/shard_map/pallas_call | solution.py:326
  105.1 0.0 copy-start.1
  105.1 1.0 copy-done.1
  106.0 0.0 all-to-all-done.1.tab_ref
  106.0 0.0 copy-start.2
  106.1 1.2 %copy-done.2 = f32[4,512,128]{2,1,0:T(8,128)S(1)} copy-done((f32[4,512,128]{2,1,0:T(8,128)S(1)}, f32[4,512,128]{2,1,0:T(8,128)}, u32[]{:S(2)}) %copy-start.2) | copy-done | bytes 1048600
  107.3 3.6 %shard_map.79 = bf16[512,256]{1,0:T(8,128)(2,1)} custom-call(s32[7]{0:T(128)S(1)} %stack.33.scal, bf16[4,512,128]{2,1,0:T(8,128)(2,1)S(1)} %get-tuple-element.10.q2_ref, bf16[128,16,128]{2,1,0:T(8,128)(2,1)S(1)} %all-to-all-done.1.tab_ref, f32[512,256]{1,0:T(8,128)S(1)} %get-tuple-element.12.o_ref, f32[4,512,128]{2,1,0:T(8,128)S(1)} %get-tuple-element.13.top_ref, ...), custom_call_target="tpu_custom_call" | custom-call | flops 268435456 | bytes 2097152 | tf_op jit(solution)/shard_map/pallas_call | solution.py:342
  (1 shorter events, 0.0 us)
Async XLA Ops:
  0.0 18.8 %collective-permute-start = (bf16[512,256]{1,0:T(8,128)(2,1)}, bf16[512,256]{1,0:T(8,128)(2,1)}, u32[]{:S(2)}, u32[]{:S(2)}) collective-permute-start(bf16[512,256]{1,0:T(8,128)(2,1)} %x0.1), channel_id=1, source_target_pairs={{0,2},{2,0},{1,3},{3,1},{4,6},{6,4},{5,7},{7,5},{8,10},{10,8},{9,1... | collective-permute-start | bytes 786440 | tf_op jit(solution)/shard_map/ppermute | solution.py:284
  5.9 23.1 %collective-permute-start.2 = (bf16[512,256]{1,0:T(8,128)(2,1)}, bf16[512,256]{1,0:T(8,128)(2,1)}, u32[]{:S(2)}, u32[]{:S(2)}) collective-permute-start(bf16[512,256]{1,0:T(8,128)(2,1)} %x0.1), channel_id=1, source_target_pairs={{0,1},{1,0},{2,3},{3,2},{4,5},{5,4},{6,7},{7,6},{8,9},{9,8},{10,11... | collective-permute-start | bytes 786440 | tf_op jit(solution)/shard_map/ppermute | solution.py:285
  18.8 13.5 %collective-permute-start.1 = (bf16[512,256]{1,0:T(8,128)(2,1)}, bf16[512,256]{1,0:T(8,128)(2,1)}, u32[]{:S(2)}, u32[]{:S(2)}) collective-permute-start(bf16[512,256]{1,0:T(8,128)(2,1)} %collective-permute-done.x2), channel_id=1, source_target_pairs={{0,1},{1,0},{2,3},{3,2},{4,5},{5,4},{6,7},{7,6},{8,9},{9,8},{10,11... | collective-permute-start | bytes 786440 | tf_op jit(solution)/shard_map/ppermute | solution.py:286
  20.7 6.3 %copy-start = (bf16[2,512,256]{2,1,0:T(8,128)(2,1)S(1)}, bf16[2,512,256]{2,1,0:T(8,128)(2,1)}, u32[]{:S(2)}) copy-start(bf16[2,512,256]{2,1,0:T(8,128)(2,1)} %kv_ref.3) | copy-start | bytes 1572868
  20.7 8.4 %copy-start.3 = (bf16[512,256]{1,0:T(8,128)(2,1)S(1)}, bf16[512,256]{1,0:T(8,128)(2,1)}, u32[]{:S(2)}) copy-start(bf16[512,256]{1,0:T(8,128)(2,1)} %x0.1) | copy-start | bytes 786436
  27.0 1.0 copy-start.4
  32.2 22.0 %copy-start.6 = (f32[2,256]{1,0:T(2,128)S(1)}, f32[2,256]{1,0:T(2,128)}, u32[]{:S(2)}) copy-start(f32[2,256]{1,0:T(2,128)} %param.12) | copy-start | bytes 6148
  32.3 22.0 %copy-start.7 = (f32[2,256]{1,0:T(2,128)S(1)}, f32[2,256]{1,0:T(2,128)}, u32[]{:S(2)}) copy-start(f32[2,256]{1,0:T(2,128)} %param.11) | copy-start | bytes 6148
  36.4 63.7 %copy-start.5 = (bf16[512,256]{1,0:T(8,128)(2,1)S(1)}, bf16[512,256]{1,0:T(8,128)(2,1)}, u32[]{:S(2)}) copy-start(bf16[512,256]{1,0:T(8,128)(2,1)} %q_ref.3) | copy-start | bytes 786436
  36.4 37.0 %all-to-all-start = ((bf16[128,16,128]{2,1,0:T(8,128)(2,1)}), bf16[128,16,128]{2,1,0:T(8,128)(2,1)S(1)}, u32[]{:S(2)}, u32[]{:S(2)}) async-start(bf16[128,16,128]{2,1,0:T(8,128)(2,1)} %shard_map.76), calls=%async_computation | async-start | bytes 1048576 | tf_op jit(solution)/shard_map/all_to_all | solution.py:323
  75.7 30.3 %all-to-all-start.1 = ((bf16[128,16,128]{2,1,0:T(8,128)(2,1)}), bf16[128,16,128]{2,1,0:T(8,128)(2,1)S(1)}, u32[]{:S(2)}, u32[]{:S(2)}) async-start(bf16[128,16,128]{2,1,0:T(8,128)(2,1)} %shard_map.77), calls=%async_computation.1 | async-start | bytes 1048576 | tf_op jit(solution)/shard_map/all_to_all | solution.py:340
  83.6 16.5 %collective-permute-start.3 = (bf16[2,128,256]{2,1,0:T(8,128)(2,1)S(1)}, bf16[2,128,256]{2,1,0:T(8,128)(2,1)S(1)}, u32[]{:S(2)}, u32[]{:S(2)}) collective-permute-start(bf16[2,128,256]{2,1,0:T(8,128)(2,1)S(1)} %get-tuple-element.16), channel_id=1, source_target_pairs={{0,4},{4,8},{8,12},{12,16},{16,20},{20,24},{24,28},{28,32},{32,36}... | collective-permute-start | bytes 393224 | tf_op jit(solution)/shard_map/ppermute | solution.py:289
  87.0 13.1 %collective-permute-start.4 = (bf16[2,128,256]{2,1,0:T(8,128)(2,1)S(1)}, bf16[2,128,256]{2,1,0:T(8,128)(2,1)S(1)}, u32[]{:S(2)}, u32[]{:S(2)}) collective-permute-start(bf16[2,128,256]{2,1,0:T(8,128)(2,1)S(1)} %get-tuple-element.15), channel_id=1, source_target_pairs={{4,0},{8,4},{12,8},{16,12},{20,16},{24,20},{28,24},{32,28},{36,32}... | collective-permute-start | bytes 393224 | tf_op jit(solution)/shard_map/ppermute | solution.py:290
  105.1 1.0 copy-start.1
  106.0 1.2 %copy-start.2 = (f32[4,512,128]{2,1,0:T(8,128)S(1)}, f32[4,512,128]{2,1,0:T(8,128)}, u32[]{:S(2)}) copy-start(f32[4,512,128]{2,1,0:T(8,128)} %copy-done.1) | copy-start | bytes 3145732

commit v3 on v2

--- a/solution.py
+++ b/solution.py
@@ -12,7 +12,9 @@
 W = 128
 HEADS = 4
 LANES = 128
-ROWS = 8
+ROWS = 32
+RING = ("z", "x")
+LINE = "yl"
 SEQ = ("z", "yl", "x")
 DOC = ("yh", "c")
 EPS = 1e-05
@@ -45,29 +47,25 @@
     return lax.broadcasted_iota(jnp.int32, shape, len(shape) - 1)
 
 
-def prep_kernel(scal, q_ref, kv_ref, q2_ref, kvh_ref):
-    tokens = q_ref.shape[0]
+def prep_kernel(scal, kv_ref, kvh_ref):
+    tokens = kv_ref.shape[1]
     local = scal[0]
     second = lax.broadcasted_iota(jnp.int32, (tokens, LANES), 0) >= local
     left = lanes_of((tokens, LANES)) < DH
     for pair in range(HEADS // 2):
         cols = slice(pair * LANES, (pair + 1) * LANES)
-        query = q_ref[:, cols].astype(f32) * 0.125
         keys = kv_ref[0, :, cols].astype(f32)
         values = kv_ref[1, :, cols].astype(f32)
-        query_r = pltpu.roll(query, DH, 1)
         keys_r = pltpu.roll(keys, DH, 1)
         values_r = pltpu.roll(values, DH, 1)
         for half in range(2):
             h = 2 * pair + half
-            both = jnp.where(left, query, query_r) if half == 0 else jnp.where(left, query_r, query)
-            q2_ref[h] = jnp.where(left == second, 0.0, both).astype(bf16)
             joined = jnp.where(left, keys, values_r) if half == 0 else jnp.where(left, keys_r, values)
             kvh_ref[h, :, :LANES] = jnp.where(second, 0.0, joined).astype(bf16)
             kvh_ref[h, :, LANES:] = jnp.where(second, joined, 0.0).astype(bf16)
 
 
-def near_kernel(scal, q_ref, kv_ref, before_ref, after_ref, o_ref, top_ref, sum_ref):
+def near_kernel(scal, q_ref, kv_ref, before_ref, after_ref, o_ref, stat_ref, q2_ref):
     tokens = q_ref.shape[0]
     local, base, total = scal[0], scal[1], scal[2]
     blocks = tokens // W
@@ -76,6 +74,7 @@
     col = lax.broadcasted_iota(jnp.int32, (W, span), 1)
     band = (col >= row) & (col - row <= 2 * W)
     left = lanes_of((W, LANES)) < DH
+    place = lax.broadcasted_iota(jnp.int32, (W, LANES), 0)
 
     def piece(s, at, cols):
         if at < 0:
@@ -96,19 +95,22 @@
         for pair in range(HEADS // 2):
             cols = slice(pair * LANES, (pair + 1) * LANES)
             query = q_ref[b * W : (b + 1) * W, cols].astype(f32) * 0.125
+            query_r = pltpu.roll(query, DH, 1)
+            second = place + b * W >= local
             keys = jnp.concatenate([piece(0, b + i, cols) for i in (-1, 0, 1)], axis=0)
             values = jnp.concatenate([piece(1, b + i, cols) for i in (-1, 0, 1)], axis=0)
             outs = []
             for half in range(2):
                 h = 2 * pair + half
-                mine = jnp.where(left == (half == 0), query, 0.0).astype(bf16)
+                both = jnp.where(left, query, query_r) if half == 0 else jnp.where(left, query_r, query)
+                q2_ref[h, b * W : (b + 1) * W] = jnp.where(left == second, 0.0, both).astype(bf16)
+                mine = jnp.where(left if half == 0 else jnp.logical_not(left), query, 0.0).astype(bf16)
                 scores = jnp.where(allowed, dot_nt(mine, keys), LOW)
                 top = jnp.max(scores, axis=1, keepdims=True)
                 weight = jnp.exp(scores - top)
                 total_w = jnp.sum(weight, axis=1, keepdims=True)
                 outs.append(jnp.dot(weight.astype(bf16), values, preferred_element_type=f32))
-                top_ref[h, b * W : (b + 1) * W] = jnp.broadcast_to(top, (W, LANES))
-                sum_ref[h, b * W : (b + 1) * W] = jnp.broadcast_to(total_w, (W, LANES))
+                stat_ref[h, b * W : (b + 1) * W] = jnp.where(left, top, total_w)
             o_ref[b * W : (b + 1) * W, cols] = jnp.where(left, outs[0], outs[1])
 
 
@@ -174,22 +176,26 @@
         copy.wait()
 
 
-def combine_kernel(scal, in_ref, gain_ref, bias_ref, out_ref):
+def combine_kernel(scal, in_ref, out_ref):
     senders = in_ref.shape[0]
-    split, tokens = scal[0], scal[1]
-    edge = split // tokens
-    has_edge = lax.rem(split, tokens) != 0
+    split, tokens, line, lines, ring = scal[0], scal[1], scal[2], scal[3], scal[4]
+    edge = lax.div(split, tokens)
+    has_edge = jnp.logical_and(
+        lax.rem(split, tokens) != 0, lax.rem(lax.div(edge, ring), lines) == line
+    )
+    slot = lax.div(edge, ring * lines) * ring + lax.rem(edge, ring)
+    slot = jnp.where(has_edge, slot, 0)
     shape = (senders, ROWS, LANES)
-    j = lax.broadcasted_iota(jnp.int32, shape, 0)
-    is_edge = jnp.logical_and(j == edge, has_edge)
+    k = lax.broadcasted_iota(jnp.int32, shape, 0)
+    is_edge = jnp.logical_and(k == slot, has_edge)
+    j = lax.div(k, ring) * (ring * lines) + line * ring + lax.rem(k, ring)
     late = j * tokens >= split
     first = in_ref[:, :ROWS, :].astype(f32)
     other = in_ref[:, ROWS:, :].astype(f32)
-    top = first[:, :, 0:1] + first[:, :, DH : DH + 1]
-    top = jnp.broadcast_to(top, shape)
+    top = jnp.broadcast_to(first[:, :, 0:1] + first[:, :, DH : DH + 1], shape)
     fine = jnp.where(is_edge, 0.0, jnp.broadcast_to(other[:, :, 0:1], shape))
     value = jnp.where(is_edge, first, first + other)
-    extra = in_ref[edge % senders].astype(f32)[ROWS:]
+    extra = in_ref[slot].astype(f32)[ROWS:]
     extra_top = jnp.broadcast_to(extra[:, 0:1] + extra[:, DH : DH + 1], (ROWS, LANES))
     extra_top = jnp.where(has_edge, extra_top, LOW)
     top0 = jnp.max(jnp.where(late, LOW, top), axis=0)
@@ -202,32 +208,40 @@
     n1 = jnp.sum(jnp.where(late, value, 0.0), axis=0)
     n1 = n1 + jnp.where(has_edge, extra * jnp.exp(extra_top - top1), 0.0)
     lane = lanes_of((ROWS, LANES))
+    n0 = jnp.where(lane == 0, top0, jnp.where(lane == DH, full0, n0))
+    n1 = jnp.where(lane == 0, top1, jnp.where(lane == DH, full1, n1))
+    out_ref[...] = jnp.broadcast_to(jnp.concatenate([n0, n1], axis=0)[None], out_ref.shape)
+
+
+def norm_kernel(scal, in_ref, gain_ref, bias_ref, out_ref):
+    got = in_ref[...]
+    top = jnp.broadcast_to(got[:, :, 0:1], got.shape)
+    whole = jnp.max(top, axis=0)
+    full = jnp.max(jnp.broadcast_to(got[:, :, DH : DH + 1], got.shape), axis=0)
+    n = jnp.sum(got * jnp.exp(top - whole[None]), axis=0)
+    lane = lanes_of((2 * ROWS, LANES))
     left = lane < DH
     used = jnp.logical_and(lane != 0, lane != DH)
-    gain = gain_ref[...]
-    bias = bias_ref[...]
 
     def halves(v):
         a = jnp.sum(jnp.where(left, v, 0.0), axis=1, keepdims=True)
         b = jnp.sum(jnp.where(left, 0.0, v), axis=1, keepdims=True)
         return jnp.where(left, a, b) * (1.0 / DH)
 
-    def norm(n, top_v, full_v):
-        n = jnp.where(used, n, 0.0)
-        centred = n - halves(n)
-        variance = halves(centred * centred)
-        scale = jnp.exp(2.0 * (full_v - top_v))
-        return centred * lax.rsqrt(variance + EPS * scale) * gain + bias
-
-    t0 = norm(n0, top0, full0)
-    t1 = norm(n1, top1, full1)
+    n = jnp.where(used, n, 0.0)
+    centred = n - halves(n)
+    variance = halves(centred * centred)
+    scale = jnp.exp(2.0 * (full - whole))
+    table = centred * lax.rsqrt(variance + EPS * scale) * gain_ref[...] + bias_ref[...]
+    t0, t1 = table[:ROWS], table[ROWS:]
+    left = left[:ROWS]
     keys = jnp.where(left, t0, pltpu.roll(t1, DH, 1))
     values = jnp.where(left, pltpu.roll(t0, DH, 1), t1)
-    chunk = jnp.concatenate([keys, values], axis=0)[None]
-    out_ref[...] = jnp.broadcast_to(chunk, out_ref.shape).astype(bf16)
-
-
-def far_kernel(scal, q2_ref, tab_ref, o_ref, top_ref, sum_ref, out_ref):
+    chunk = jnp.concatenate([keys, values], axis=0).astype(bf16)[None]
+    out_ref[...] = jnp.broadcast_to(chunk, out_ref.shape)
+
+
+def far_kernel(scal, q2_ref, tab_ref, o_ref, stat_ref, out_ref):
     tokens = o_ref.shape[0]
     local = scal[0]
     shape = (tokens, LANES)
@@ -240,19 +254,20 @@
         outs = []
         for half in range(2):
             h = 2 * pair + half
-            table = tab_ref[h * parts : (h + 1) * parts].astype(f32)
-            keys = table[:, :ROWS].reshape(R, LANES).astype(bf16)
-            values = table[:, ROWS:].reshape(R, LANES).astype(bf16)
+            keys = tab_ref[h * parts : (h + 1) * parts, :ROWS].reshape(R, LANES)
+            values = tab_ref[h * parts : (h + 1) * parts, ROWS:].reshape(R, LANES)
             scores = dot_nt(q2_ref[h], keys)
             low, high = scores[:, :LANES], scores[:, LANES:]
-            near_top = top_ref[h]
+            stat = stat_ref[h]
+            stat_r = pltpu.roll(stat, DH, 1)
+            near_top = jnp.where(left, stat, stat_r)
             top = jnp.max(jnp.maximum(low, high), axis=1, keepdims=True)
             top = jnp.maximum(jnp.broadcast_to(top, shape), near_top)
             low = jnp.exp(low - top)
             high = jnp.exp(high - top)
             scale = jnp.exp(near_top - top)
             total = jnp.broadcast_to(jnp.sum(low + high, axis=1, keepdims=True), shape)
-            total = total + sum_ref[h] * scale
+            total = total + jnp.where(left, stat_r, stat) * scale
             weight = jnp.concatenate([low.astype(bf16), high.astype(bf16)], axis=1)
             far = jnp.dot(weight, values, preferred_element_type=f32)
             swap = second if half == 0 else jnp.logical_not(second)
@@ -279,7 +294,13 @@
             (1 - yh) * 2 + 1 - c,
         ]
     ).astype(jnp.int32)
-    scal2 = jnp.stack([split, jnp.int32(tokens)]).astype(jnp.int32)
+    line = lax.axis_index(LINE)
+    slot = lax.axis_index(RING)
+    lines = lax.axis_size(LINE)
+    slots_held = lax.axis_size(RING)
+    scal2 = jnp.stack(
+        [split, jnp.int32(tokens), line, jnp.int32(lines), jnp.int32(lax.axis_size("x"))]
+    ).astype(jnp.int32)
 
     x2 = lax.ppermute(inputs, "yh", SWAP)
     x1 = lax.ppermute(inputs, "c", SWAP)
@@ -290,14 +311,11 @@
     after = lax.ppermute(keys_values[:, :W], SEQ, down)
 
     weight_t = jnp.swapaxes(slot_weight.reshape(4, width, HEADS * R), 1, 2)
-    q2, kvh = call(
+    kvh = call(
         prep_kernel,
-        [
-            jax.ShapeDtypeStruct((HEADS, tokens, LANES), bf16),
-            jax.ShapeDtypeStruct((HEADS, tokens, 2 * LANES), bf16),
-        ],
-        2, 16, 0, 3 << 20,
-    )(scal, queries, keys_values)
+        jax.ShapeDtypeStruct((HEADS, tokens, 2 * LANES), bf16),
+        1, 8, 0, 2 << 20,
+    )(scal, keys_values)
 
     slots = HEADS * R
     flops = 2 * tokens * slots * width
@@ -308,7 +326,7 @@
     acc = call(more_kernel, acc_shape, 3, 16, flops, 6 << 20)(scal, x2, weight_t, acc)
     sent = pl.pallas_call(
         project_kernel,
-        out_shape=jax.ShapeDtypeStruct((shards, 2 * ROWS, LANES), bf16),
+        out_shape=jax.ShapeDtypeStruct((slots_held, 2 * ROWS, LANES), bf16),
         in_specs=[SMEM] + [VMEM] * 4,
         out_specs=pl.BlockSpec(memory_space=pltpu.HBM),
         scratch_shapes=[
@@ -320,30 +338,39 @@
             flops=2 * flops, bytes_accessed=5 << 20, transcendentals=tokens * slots
         ),
     )(scal, x3, weight_t, acc, kvh)
-    arrived = lax.all_to_all(sent, SEQ, 0, 0, tiled=True)
-
-    rep = jax.ShapeDtypeStruct((HEADS, tokens, LANES), f32)
-    near, tops, sums = call(
+    arrived = lax.all_to_all(sent, RING, 0, 0, tiled=True)
+
+    near, stats, q2 = call(
         near_kernel,
-        [jax.ShapeDtypeStruct((tokens, HEADS * DH), f32), rep, rep],
+        [
+            jax.ShapeDtypeStruct((tokens, HEADS * DH), f32),
+            jax.ShapeDtypeStruct((HEADS, tokens, LANES), f32),
+            jax.ShapeDtypeStruct((HEADS, tokens, LANES), bf16),
+        ],
         4, 8, 4 * tokens * 3 * W * HEADS * LANES, 2 << 20, tokens * 3 * W * HEADS,
     )(scal, queries, keys_values, before, after)
 
-    head = shard * ROWS // R
+    held = call(
+        combine_kernel,
+        jax.ShapeDtypeStruct((lines, 2 * ROWS, LANES), f32),
+        1, 8, 0, 1 << 20, 1 << 17,
+    )(scal2, arrived)
+    shared = lax.all_to_all(held, LINE, 0, 0, tiled=True)
+    head = lax.div(slot * ROWS, R)
     gain = lax.dynamic_slice_in_dim(slot_gain, head * DH, DH, 1).reshape(1, 2 * DH)
     bias = lax.dynamic_slice_in_dim(slot_bias, head * DH, DH, 1).reshape(1, 2 * DH)
     chunk = call(
-        combine_kernel,
-        jax.ShapeDtypeStruct((shards, 2 * ROWS, LANES), bf16),
-        3, 8, 0, 1 << 20, 1 << 17,
-    )(scal2, arrived, gain, bias)
-    table = lax.all_to_all(chunk, SEQ, 0, 0, tiled=True)
+        norm_kernel,
+        jax.ShapeDtypeStruct((slots_held, 2 * ROWS, LANES), bf16),
+        3, 8, 0, 1 << 20, 1 << 15,
+    )(scal2, shared, gain, bias)
+    table = lax.all_to_all(chunk, RING, 0, 0, tiled=True)
 
     return call(
         far_kernel,
         jax.ShapeDtypeStruct((tokens, HEADS * DH), bf16),
-        5, 12, 4 * tokens * R * HEADS * LANES, 2 << 20, tokens * R * HEADS,
-    )(scal, q2, table, near, tops, sums)
+        4, 12, 4 * tokens * R * HEADS * LANES, 2 << 20, tokens * R * HEADS,
+    )(scal, q2, table, near, stats)
 
 
 def solution(mesh):

time: 111 us -> 114 us (1.027)
  the two profiles are of different devices: /device:TPU:16 before, /device:TPU:62 now
where the time goes in v3:
time: 114 us; the launch traced here: 113 us
  waiting for transfers between devices  43.4 us (38%)
  starting transfers between devices  41.2 us (36%)
  Pallas kernels  21.6 us (19%)
  local copies, waits for them, and re-layouts  4.62 us (4%)
  between operations  2.12 us (2%)
    all_to_all x1, waiting for transfers between devices, on_device(): arrived = lax.all_to_all(sent, RING, 0, 0, tiled=True)  17.4 us
    all_to_all x1, starting transfers between devices, on_device(): arrived = lax.all_to_all(sent, RING, 0, 0, tiled=True)  13.6 us
    ppermute x1, waiting for transfers between devices, on_device(): x2 = lax.ppermute(inputs, 'yh', SWAP)  13.2 us
    ppermute x1, waiting for transfers between devices, on_device(): after = lax.ppermute(keys_values[:, :W], SEQ, down)  8.34 us
    all_to_all x1, starting transfers between devices, on_device(): shared = lax.all_to_all(held, LINE, 0, 0, tiled=True)  6.19 us
    all_to_all x1, starting transfers between devices, on_device(): table = lax.all_to_all(chunk, RING, 0, 0, tiled=True)  5.57 us
    ppermute x1, starting transfers between devices, on_device(): before = lax.ppermute(keys_values[:, tokens - W:], SEQ, up)  5.21 us
    pallas_call x1, Pallas kernels, on_device(): call(near_kernel, [jax.ShapeDtypeStruct((tokens, HEADS * DH), f32), jax.S...  5.07 us
  transfers between devices with their start and end apart: 8, of which 5 were waited for; matrix products, arithmetic and copies ran while one was open for 4% of the time, Pallas kernels for 8%

profile of v3, /device:TPU:62, one launch (start us, length us, event | category | flops | bytes accessed | tf_op | source)
XLA Modules:
  0.0 113.0 jit_solution(16828743653089496539)
XLA Ops:
  0.0 4.7 %collective-permute-start.2 = (bf16[512,256]{1,0:T(8,128)(2,1)}, bf16[512,256]{1,0:T(8,128)(2,1)}, u32[]{:S(2)}, u32[]{:S(2)}) collective-permute-start(bf16[512,256]{1,0:T(8,128)(2,1)} %x0.1), channel_id=1, source_target_pairs={{0,2},{2,0},{1,3},{3,1},{4,6},{6,4},{5,7},{7,5},{8,10},{10,8},{9,1... | collective-permute-start | bytes 786440 | tf_op jit(solution)/shard_map/ppermute | solution.py:305
  4.7 1.9 %collective-permute-start.4 = (bf16[512,256]{1,0:T(8,128)(2,1)}, bf16[512,256]{1,0:T(8,128)(2,1)S(1)}, u32[]{:S(2)}, u32[]{:S(2)}) collective-permute-start(bf16[512,256]{1,0:T(8,128)(2,1)} %x0.1), channel_id=1, source_target_pairs={{0,1},{1,0},{2,3},{3,2},{4,5},{5,4},{6,7},{7,6},{8,9},{9,8},{10,11... | collective-permute-start | bytes 786440 | tf_op jit(solution)/shard_map/ppermute | solution.py:306
  6.6 13.2 %collective-permute-done.2.x2 = bf16[512,256]{1,0:T(8,128)(2,1)} collective-permute-done((bf16[512,256]{1,0:T(8,128)(2,1)}, bf16[512,256]{1,0:T(8,128)(2,1)}, u32[]{:S(2)}, u32[]{:S(2)}) %collective-permute-start.2) | collective-permute-done | bytes 262176 | tf_op jit(solution)/shard_map/ppermute | solution.py:305
  19.8 1.9 %collective-permute-start.3 = (bf16[512,256]{1,0:T(8,128)(2,1)}, bf16[512,256]{1,0:T(8,128)(2,1)S(1)}, u32[]{:S(2)}, u32[]{:S(2)}) collective-permute-start(bf16[512,256]{1,0:T(8,128)(2,1)} %collective-permute-done.2.x2), channel_id=1, source_target_pairs={{0,1},{1,0},{2,3},{3,2},{4,5},{5,4},{6,7},{7,6},{8,9},{9,8},{10,11... | collective-permute-start | bytes 786440 | tf_op jit(solution)/shard_map/ppermute | solution.py:307
  21.8 0.0 copy-start
  21.8 0.0 copy-start.1
  21.8 2.9 %copy.8 = bf16[4,256,1024]{1,2,0:T(8,128)(2,1)S(1)} copy(bf16[4,256,1024]{2,1,0:T(8,128)(2,1)} %bitcast.15) | data formatting | bytes 4194304 | tf_op jit(solution)/shard_map/reshape | solution.py:313
  24.7 1.3 %fusion.1 = (s32[1,1]{1,0:T(1,128)}, s32[1,1]{1,0:T(1,128)}) fusion(s32[2,512]{1,0:T(2,128)} %param.13), kind=kLoop, calls=%fused_computation.4 | loop fusion | bytes 16 | tf_op jit(solution)/shard_map/slice | solution.py:283
  27.9 0.1 stack.36.scal
  28.0 0.0 copy-done
  28.0 0.9 shard_map.76.kvh_ref
  29.0 0.0 collective-permute-done.4.x1
  29.0 0.0 copy-done.1
  29.0 1.3 %shard_map.74.acc_ref = f32[1024,512]{1,0:T(8,128)S(1)} custom-call(s32[7]{0:T(128)S(1)} %stack.36.scal, bf16[512,256]{1,0:T(8,128)(2,1)S(1)} %copy-done.1, bf16[512,256]{1,0:T(8,128)(2,1)S(1)} %collective-permute-done.4.x1, bf16[4,1024,256]{2,1,0:T(8,128)(2,1)S(1)} %bitcast.12), custom_call_target="tpu_custom_call" | custom-call | flops 536870912 | bytes 5242880 | tf_op jit(solution)/shard_map/pallas_call | solution.py:323
  30.3 1.4 %shard_map.75.acc_ref = f32[1024,512]{1,0:T(8,128)S(1)} custom-call(s32[7]{0:T(128)S(1)} %stack.36.scal, bf16[512,256]{1,0:T(8,128)(2,1)} %collective-permute-done.2.x2, bf16[4,1024,256]{2,1,0:T(8,128)(2,1)S(1)} %bitcast.13, f32[1024,512]{1,0:T(8,128)S(1)} %shard_map.74.acc_ref), custom_call_target="tpu_custom_call" | custom-call | flops 268435456 | bytes 6291456 | tf_op jit(solution)/shard_map/pallas_call | solution.py:326
  31.7 0.0 copy-start.3
  31.7 0.0 copy-start.4
  31.7 0.0 collective-permute-done.3.x3
  31.7 3.7 %shard_map.77 = bf16[32,64,128]{2,1,0:T(8,128)(2,1)} custom-call(s32[7]{0:T(128)S(1)} %stack.36.scal, bf16[512,256]{1,0:T(8,128)(2,1)S(1)} %collective-permute-done.3.x3, bf16[4,1024,256]{2,1,0:T(8,128)(2,1)S(1)} %bitcast.14, f32[1024,512]{1,0:T(8,128)S(1)} %shard_map.75.acc_ref, bf16[4,512,256]{2,1,0:T(8,128)(2,1)S(1)} %shard_map.76.kvh_ref), custom_call_target="tpu_custom_call" | custom-call | flops 536870912 | bytes 5242880 | tf_op jit(solution)/shard_map/pallas_call | solution.py:327
  35.4 0.0 copy-start.2
  35.4 13.6 %all-to-all-start = ((bf16[32,64,128]{2,1,0:T(8,128)(2,1)}), bf16[32,64,128]{2,1,0:T(8,128)(2,1)S(1)}, u32[]{:S(2)}, u32[]{:S(2)}) async-start(bf16[32,64,128]{2,1,0:T(8,128)(2,1)} %shard_map.77), calls=%async_computation | async-start | bytes 1048576 | tf_op jit(solution)/shard_map/all_to_all | solution.py:341
  49.0 0.1 pad_add_fusion.scal
  49.1 17.4 %all-to-all-done.in_ref = bf16[32,64,128]{2,1,0:T(8,128)(2,1)S(1)} async-done(((bf16[32,64,128]{2,1,0:T(8,128)(2,1)}), bf16[32,64,128]{2,1,0:T(8,128)(2,1)S(1)}, u32[]{:S(2)}, u32[]{:S(2)}) %all-to-all-start) | async-done | bytes 524320 | tf_op jit(solution)/shard_map/all_to_all | solution.py:341
  66.5 3.0 %shard_map.78 = f32[4,64,128]{2,1,0:T(8,128)} custom-call(s32[5]{0:T(128)S(1)} %pad_add_fusion.scal, bf16[32,64,128]{2,1,0:T(8,128)(2,1)S(1)} %all-to-all-done.in_ref), custom_call_target="tpu_custom_call" | custom-call | bytes 1048576 | tf_op jit(solution)/shard_map/pallas_call | solution.py:353
  69.5 6.2 %all-to-all-start.1 = ((f32[4,64,128]{2,1,0:T(8,128)}), f32[4,64,128]{2,1,0:T(8,128)S(1)}, u32[]{:S(2)}, u32[]{:S(2)}) async-start(f32[4,64,128]{2,1,0:T(8,128)} %shard_map.78), calls=%async_computation.1 | async-start | bytes 262144 | tf_op jit(solution)/shard_map/all_to_all | solution.py:358
  75.7 0.0 copy-done.3
  75.7 0.0 copy-done.4
  75.7 0.1 constant_dynamic-slice_fusion
  75.8 0.1 reshape.10.gain_ref
  75.8 0.1 reshape.11.bias_ref
  75.9 3.3 %all-to-all-done.1.in_ref = f32[4,64,128]{2,1,0:T(8,128)S(1)} async-done(((f32[4,64,128]{2,1,0:T(8,128)}), f32[4,64,128]{2,1,0:T(8,128)S(1)}, u32[]{:S(2)}, u32[]{:S(2)}) %all-to-all-start.1) | async-done | bytes 131104 | tf_op jit(solution)/shard_map/all_to_all | solution.py:358
  79.2 1.8 %shard_map.79 = bf16[32,64,128]{2,1,0:T(8,128)(2,1)} custom-call(s32[5]{0:T(128)S(1)} %pad_add_fusion.scal, f32[4,64,128]{2,1,0:T(8,128)S(1)} %all-to-all-done.1.in_ref, f32[1,128]{1,0:T(1,128)S(1)} %reshape.10.gain_ref, f32[1,128]{1,0:T(1,128)S(1)} %reshape.11.bias_ref), custom_call_target="tpu_custom_call" | custom-call | bytes 1048576 | tf_op jit(solution)/shard_map/pallas_call | solution.py:362
  81.0 5.6 %all-to-all-start.2 = ((bf16[32,64,128]{2,1,0:T(8,128)(2,1)}), bf16[32,64,128]{2,1,0:T(8,128)(2,1)S(1)}, u32[]{:S(2)}, u32[]{:S(2)}) async-start(bf16[32,64,128]{2,1,0:T(8,128)(2,1)} %shard_map.79), calls=%async_computation.2 | async-start | bytes 1048576 | tf_op jit(solution)/shard_map/all_to_all | solution.py:367
  86.6 5.2 %collective-permute-start = (bf16[2,128,256]{2,1,0:T(8,128)(2,1)S(1)}, bf16[2,128,256]{2,1,0:T(8,128)(2,1)S(1)}, u32[]{:S(2)}, u32[]{:S(2)}) collective-permute-start(bf16[2,128,256]{2,1,0:T(8,128)(2,1)S(1)} %get-tuple-element.12), channel_id=1, source_target_pairs={{0,4},{4,8},{8,12},{12,16},{16,20},{20,24},{24,28},{28,32},{32,36}... | collective-permute-start | bytes 393224 | tf_op jit(solution)/shard_map/ppermute | solution.py:310
  91.8 2.1 %collective-permute-start.1 = (bf16[2,128,256]{2,1,0:T(8,128)(2,1)S(1)}, bf16[2,128,256]{2,1,0:T(8,128)(2,1)S(1)}, u32[]{:S(2)}, u32[]{:S(2)}) collective-permute-start(bf16[2,128,256]{2,1,0:T(8,128)(2,1)S(1)} %get-tuple-element.11), channel_id=1, source_target_pairs={{4,0},{8,4},{12,8},{16,12},{20,16},{24,20},{28,24},{32,28},{36,32}... | collective-permute-start | bytes 393224 | tf_op jit(solution)/shard_map/ppermute | solution.py:311
  93.9 1.2 %collective-permute-done.before_ref = bf16[2,128,256]{2,1,0:T(8,128)(2,1)S(1)} collective-permute-done((bf16[2,128,256]{2,1,0:T(8,128)(2,1)S(1)}, bf16[2,128,256]{2,1,0:T(8,128)(2,1)S(1)}, u32[]{:S(2)}, u32[]{:S(2)}) %collective-permute-start) | collective-permute-done | bytes 131104 | tf_op jit(solution)/shard_map/ppermute | solution.py:310
  95.1 8.3 %collective-permute-done.1.after_ref = bf16[2,128,256]{2,1,0:T(8,128)(2,1)S(1)} collective-permute-done((bf16[2,128,256]{2,1,0:T(8,128)(2,1)S(1)}, bf16[2,128,256]{2,1,0:T(8,128)(2,1)S(1)}, u32[]{:S(2)}, u32[]{:S(2)}) %collective-permute-start.1) | collective-permute-done | bytes 131104 | tf_op jit(solution)/shard_map/ppermute | solution.py:311
  103.5 0.0 copy-done.2
  103.5 5.1 %shard_map.73 = (f32[512,256]{1,0:T(8,128)S(1)}, f32[4,512,128]{2,1,0:T(8,128)S(1)}, bf16[4,512,128]{2,1,0:T(8,128)(2,1)S(1)}) custom-call(s32[7]{0:T(128)S(1)} %stack.36.scal, bf16[512,256]{1,0:T(8,128)(2,1)S(1)} %copy-done.2, bf16[2,512,256]{2,1,0:T(8,128)(2,1)S(1)} %copy-done, bf16[2,128,256]{2,1,0:T(8,128)(2,1)S(1)} %collective-permute-done.before_ref, ...), custom_call_target="tpu_custom_call" | custom-call | flops 402653184 | bytes 2097152 | tf_op jit(solution)/shard_map/pallas_call | solution.py:343
  108.5 0.0 all-to-all-done.2.tab_ref
  108.6 4.4 %shard_map.80 = bf16[512,256]{1,0:T(8,128)(2,1)} custom-call(s32[7]{0:T(128)S(1)} %stack.36.scal, bf16[4,512,128]{2,1,0:T(8,128)(2,1)S(1)} %get-tuple-element.8.q2_ref, bf16[32,64,128]{2,1,0:T(8,128)(2,1)S(1)} %all-to-all-done.2.tab_ref, f32[512,256]{1,0:T(8,128)S(1)} %get-tuple-element.9.o_ref, f32[4,512,128]{2,1,0:T(8,128)S(1)} %get-tuple-element.10.stat_ref), custom_call_target="tpu_custom_call" | custom-call | flops 268435456 | bytes 2097152 | tf_op jit(solution)/shard_map/pallas_call | solution.py:369
  (2 shorter events, 0.0 us)
Async XLA Ops:
  0.0 19.8 %collective-permute-start.2 = (bf16[512,256]{1,0:T(8,128)(2,1)}, bf16[512,256]{1,0:T(8,128)(2,1)}, u32[]{:S(2)}, u32[]{:S(2)}) collective-permute-start(bf16[512,256]{1,0:T(8,128)(2,1)} %x0.1), channel_id=1, source_target_pairs={{0,2},{2,0},{1,3},{3,1},{4,6},{6,4},{5,7},{7,5},{8,10},{10,8},{9,1... | collective-permute-start | bytes 786440 | tf_op jit(solution)/shard_map/ppermute | solution.py:305
  4.7 24.3 %collective-permute-start.4 = (bf16[512,256]{1,0:T(8,128)(2,1)}, bf16[512,256]{1,0:T(8,128)(2,1)S(1)}, u32[]{:S(2)}, u32[]{:S(2)}) collective-permute-start(bf16[512,256]{1,0:T(8,128)(2,1)} %x0.1), channel_id=1, source_target_pairs={{0,1},{1,0},{2,3},{3,2},{4,5},{5,4},{6,7},{7,6},{8,9},{9,8},{10,11... | collective-permute-start | bytes 786440 | tf_op jit(solution)/shard_map/ppermute | solution.py:306
  19.8 11.9 %collective-permute-start.3 = (bf16[512,256]{1,0:T(8,128)(2,1)}, bf16[512,256]{1,0:T(8,128)(2,1)S(1)}, u32[]{:S(2)}, u32[]{:S(2)}) collective-permute-start(bf16[512,256]{1,0:T(8,128)(2,1)} %collective-permute-done.2.x2), channel_id=1, source_target_pairs={{0,1},{1,0},{2,3},{3,2},{4,5},{5,4},{6,7},{7,6},{8,9},{9,8},{10,11... | collective-permute-start | bytes 786440 | tf_op jit(solution)/shard_map/ppermute | solution.py:307
  21.8 6.3 %copy-start = (bf16[2,512,256]{2,1,0:T(8,128)(2,1)S(1)}, bf16[2,512,256]{2,1,0:T(8,128)(2,1)}, u32[]{:S(2)}) copy-start(bf16[2,512,256]{2,1,0:T(8,128)(2,1)} %kv_ref.3) | copy-start | bytes 1572868
  21.8 7.2 %copy-start.1 = (bf16[512,256]{1,0:T(8,128)(2,1)S(1)}, bf16[512,256]{1,0:T(8,128)(2,1)}, u32[]{:S(2)}) copy-start(bf16[512,256]{1,0:T(8,128)(2,1)} %x0.1) | copy-start | bytes 786436
  31.7 44.0 %copy-start.3 = (f32[2,256]{1,0:T(2,128)S(1)}, f32[2,256]{1,0:T(2,128)}, u32[]{:S(2)}) copy-start(f32[2,256]{1,0:T(2,128)} %param.12) | copy-start | bytes 6148
  31.7 44.0 %copy-start.4 = (f32[2,256]{1,0:T(2,128)S(1)}, f32[2,256]{1,0:T(2,128)}, u32[]{:S(2)}) copy-start(f32[2,256]{1,0:T(2,128)} %param.11) | copy-start | bytes 6148
  35.4 68.1 %copy-start.2 = (bf16[512,256]{1,0:T(8,128)(2,1)S(1)}, bf16[512,256]{1,0:T(8,128)(2,1)}, u32[]{:S(2)}) copy-start(bf16[512,256]{1,0:T(8,128)(2,1)} %q_ref.1) | copy-start | bytes 786436
  35.4 31.1 %all-to-all-start = ((bf16[32,64,128]{2,1,0:T(8,128)(2,1)}), bf16[32,64,128]{2,1,0:T(8,128)(2,1)S(1)}, u32[]{:S(2)}, u32[]{:S(2)}) async-start(bf16[32,64,128]{2,1,0:T(8,128)(2,1)} %shard_map.77), calls=%async_computation | async-start | bytes 1048576 | tf_op jit(solution)/shard_map/all_to_all | solution.py:341
  69.5 9.7 %all-to-all-start.1 = ((f32[4,64,128]{2,1,0:T(8,128)}), f32[4,64,128]{2,1,0:T(8,128)S(1)}, u32[]{:S(2)}, u32[]{:S(2)}) async-start(f32[4,64,128]{2,1,0:T(8,128)} %shard_map.78), calls=%async_computation.1 | async-start | bytes 262144 | tf_op jit(solution)/shard_map/all_to_all | solution.py:358
  81.0 27.6 %all-to-all-start.2 = ((bf16[32,64,128]{2,1,0:T(8,128)(2,1)}), bf16[32,64,128]{2,1,0:T(8,128)(2,1)S(1)}, u32[]{:S(2)}, u32[]{:S(2)}) async-start(bf16[32,64,128]{2,1,0:T(8,128)(2,1)} %shard_map.79), calls=%async_computation.2 | async-start | bytes 1048576 | tf_op jit(solution)/shard_map/all_to_all | solution.py:367
  86.6 8.6 %collective-permute-start = (bf16[2,128,256]{2,1,0:T(8,128)(2,1)S(1)}, bf16[2,128,256]{2,1,0:T(8,128)(2,1)S(1)}, u32[]{:S(2)}, u32[]{:S(2)}) collective-permute-start(bf16[2,128,256]{2,1,0:T(8,128)(2,1)S(1)} %get-tuple-element.12), channel_id=1, source_target_pairs={{0,4},{4,8},{8,12},{12,16},{16,20},{20,24},{24,28},{28,32},{32,36}... | collective-permute-start | bytes 393224 | tf_op jit(solution)/shard_map/ppermute | solution.py:310
  91.8 11.7 %collective-permute-start.1 = (bf16[2,128,256]{2,1,0:T(8,128)(2,1)S(1)}, bf16[2,128,256]{2,1,0:T(8,128)(2,1)S(1)}, u32[]{:S(2)}, u32[]{:S(2)}) collective-permute-start(bf16[2,128,256]{2,1,0:T(8,128)(2,1)S(1)} %get-tuple-element.11), channel_id=1, source_target_pairs={{4,0},{8,4},{12,8},{16,12},{20,16},{24,20},{28,24},{32,28},{36,32}... | collective-permute-start | bytes 393224 | tf_op jit(solution)/shard_map/ppermute | solution.py:311

commit v4 on v3

v4 whole, which is shorter than its diff:
```python
import functools

import jax
import jax.numpy as jnp
from jax import lax
from jax.experimental import pallas as pl
from jax.experimental.pallas import tpu as pltpu
from jax.sharding import Mesh
from jax.sharding import PartitionSpec as P


DH = 64
R = 256
W = 128
HEADS = 4
LANES = 128
ROWS = 32
RING = ("z", "x")
LINE = "yl"
SEQ = ("z", "yl", "x")
DOC = ("yh", "c")
EPS = 1e-05
LOW = -1e30
SWAP = [(0, 1), (1, 0)]

f32 = jnp.float32
bf16 = jnp.bfloat16
VMEM = pl.BlockSpec(memory_space=pltpu.VMEM)
SMEM = pl.BlockSpec(memory_space=pltpu.SMEM)


def call(kernel, out_shape, n_in, vmem_mib, flops, nbytes, exps=0, scalars=1, scratch=()):
    single = not isinstance(out_shape, (list, tuple))
    return pl.pallas_call(
        kernel,
        out_shape=out_shape,
        in_specs=[SMEM] * scalars + [VMEM] * n_in,
        out_specs=VMEM if single else [VMEM] * len(out_shape),
        scratch_shapes=list(scratch),
        compiler_params=pltpu.CompilerParams(vmem_limit_bytes=vmem_mib << 20),
        cost_estimate=pl.CostEstimate(flops=flops, bytes_accessed=nbytes, transcendentals=exps),
    )


def dot_nt(a, b):
    return lax.dot_general(a, b, (((1,), (1,)), ((), ())), preferred_element_type=f32)


def dot_tn(a, b):
    return lax.dot_general(a, b, (((0,), (0,)), ((), ())), preferred_element_type=f32)


def lanes_of(shape):
    return lax.broadcasted_iota(jnp.int32, shape, len(shape) - 1)


def prep_kernel(scal, kv_ref, kvh_ref):
    tokens = kv_ref.shape[1]
    local = scal[0]
    second = lax.broadcasted_iota(jnp.int32, (tokens, LANES), 0) >= local
    left = lanes_of((tokens, LANES)) < DH
    for pair in range(HEADS // 2):
        cols = slice(pair * LANES, (pair + 1) * LANES)
        keys = kv_ref[0, :, cols].astype(f32)
        values = kv_ref[1, :, cols].astype(f32)
        keys_r = pltpu.roll(keys, DH, 1)
        values_r = pltpu.roll(values, DH, 1)
        for half in range(2):
            h = 2 * pair + half
            joined = jnp.where(left, keys, values_r) if half == 0 else jnp.where(left, keys_r, values)
            kvh_ref[h, :, :LANES] = jnp.where(second, 0.0, joined).astype(bf16)
            kvh_ref[h, :, LANES:] = jnp.where(second, joined, 0.0).astype(bf16)


def near_kernel(scal, q_ref, kv_ref, before_ref, after_ref, o_ref, stat_ref, q2_ref):
    tokens = q_ref.shape[0]
    local, base, total = scal[0], scal[1], scal[2]
    blocks = tokens // W
    span = 3 * W
    key = lax.broadcasted_iota(jnp.int32, (span, W), 0)
    query_at = lax.broadcasted_iota(jnp.int32, (span, W), 1)
    band = (key >= query_at) & (key - query_at <= 2 * W)
    left = lanes_of((W, LANES)) < DH
    place = lax.broadcasted_iota(jnp.int32, (W, LANES), 0)
    stat_ref[...] = jnp.zeros_like(stat_ref)

    def piece(s, at, cols):
        if at < 0:
            return before_ref[s, :, cols]
        if at >= blocks:
            return after_ref[s, :, cols]
        return kv_ref[s, at * W : (at + 1) * W, cols]

    for b in range(blocks):
        here = slice(b * W, (b + 1) * W)
        query_pos = query_at + b * W
        key_pos = key + (b - 1) * W
        allowed = (
            band
            & ((query_pos >= local) == (key_pos >= local))
            & (key_pos + base >= 0)
            & (key_pos + base < total)
        )
        second = place + b * W >= local
        stat_ref[HEADS : HEADS + 1, here] = jnp.where(query_pos[:1] >= local, 1.0, 0.0)
        for pair in range(HEADS // 2):
            cols = slice(pair * LANES, (pair + 1) * LANES)
            query = q_ref[here, cols].astype(f32) * 0.125
            query_r = pltpu.roll(query, DH, 1)
            keys = jnp.concatenate([piece(0, b + i, cols) for i in (-1, 0, 1)], axis=0)
            values = jnp.concatenate([piece(1, b + i, cols) for i in (-1, 0, 1)], axis=0)
            for half in range(2):
                h = 2 * pair + half
                both = jnp.where(left, query, query_r) if half == 0 else jnp.where(left, query_r, query)
                q2_ref[h, here] = jnp.where(left == second, 0.0, both).astype(bf16)
                mine = jnp.where(left if half == 0 else jnp.logical_not(left), query, 0.0).astype(bf16)
                scores = jnp.where(allowed, dot_nt(keys, mine), LOW)
                top = jnp.max(scores, axis=0, keepdims=True)
                weight = jnp.exp(scores - top)
                stat_ref[h : h + 1, here] = top
                stat_ref[2 * HEADS + h : 2 * HEADS + h + 1, here] = jnp.sum(
                    weight, axis=0, keepdims=True
                )
                out = dot_tn(values, weight.astype(bf16))
                o_ref[h * DH : (h + 1) * DH, here] = out[half * DH : (half + 1) * DH]


def pieces_of(top):
    a = top.astype(bf16).astype(f32)
    b = (top - a).astype(bf16).astype(f32)
    return a, b, top - a - b


def partial_kernel(scal, x0, x1, wt_ref, acc_ref):
    acc_ref[...] = dot_nt(wt_ref[scal[3]], x0[...]) + dot_nt(wt_ref[scal[4]], x1[...])


def more_kernel(scal, x2, wt_ref, acc_ref, out_ref):
    out_ref[...] = acc_ref[...] + dot_nt(wt_ref[scal[5]], x2[...])


def project_kernel(scal, x3, wt_ref, acc_ref, kvh_ref, out_ref, held, sems):
    tokens = x3.shape[0]
    local = scal[0]
    mixed = jnp.logical_and(local > 0, local < tokens)
    lane = lanes_of((R, LANES))
    at_a = lane == 0
    at_b = lane == DH
    left = lane < DH
    parts = R // ROWS

    def logits_of(h):
        rows = slice(h * R, (h + 1) * R)
        return acc_ref[rows, :] + dot_nt(wt_ref[scal[6], rows, :], x3[...])

    def from_first(n):
        return n - jnp.where(left, n[:, 0:1], n[:, DH : DH + 1])

    def put(h, hi, rest):
        packed = jnp.concatenate(
            [hi.reshape(parts, ROWS, LANES), rest.reshape(parts, ROWS, LANES)], axis=1
        )
        held[h] = packed.astype(bf16)
        copy = pltpu.make_async_copy(
            held.at[h], out_ref.at[pl.ds(h * parts, parts)], sems.at[h]
        )
        copy.start()
        return copy

    @pl.when(jnp.logical_not(mixed))
    def _():
        side = pl.multiple_of(jnp.where(local <= 0, LANES, 0), LANES)
        copies = []
        for h in range(HEADS):
            logits = logits_of(h)
            a, b, c = pieces_of(jnp.max(logits, axis=1, keepdims=True))
            proj = jnp.exp(logits - (a + b)).astype(bf16)
            n = from_first(
                jnp.dot(proj, kvh_ref[h, :, pl.ds(side, LANES)], preferred_element_type=f32)
            )
            hi = n.astype(bf16).astype(f32)
            rest = jnp.where(at_a, c, jnp.where(at_b, 0.0, n - hi))
            hi = jnp.where(at_a, a, jnp.where(at_b, b, hi))
            copies.append(put(h, hi, rest))
        for copy in copies:
            copy.wait()

    @pl.when(mixed)
    def _():
        second = lax.broadcasted_iota(jnp.int32, (R, tokens), 1) >= local
        copies = []
        for h in range(HEADS):
            logits = logits_of(h)
            a0, b0, _ = pieces_of(jnp.max(jnp.where(second, LOW, logits), axis=1, keepdims=True))
            a1, b1, _ = pieces_of(jnp.max(jnp.where(second, logits, LOW), axis=1, keepdims=True))
            proj = jnp.exp(logits - jnp.where(second, a1 + b1, a0 + b0)).astype(bf16)
            sums = jnp.dot(proj, kvh_ref[h], preferred_element_type=f32)
            n0 = from_first(sums[:, :LANES])
            n1 = from_first(sums[:, LANES:])
            n0 = jnp.where(at_a, a0, jnp.where(at_b, b0, n0))
            n1 = jnp.where(at_a, a1, jnp.where(at_b, b1, n1))
            copies.append(put(h, n0, n1))
        for copy in copies:
            copy.wait()


def combine_kernel(lines, ring, tokens, scal, in_ref, out_ref, tops):
    senders = in_ref.shape[0]
    split, line = scal[0], scal[1]
    edge = lax.div(split, tokens)
    has_edge = jnp.logical_and(
        lax.rem(split, tokens) != 0, lax.rem(lax.div(edge, ring), lines) == line
    )
    slot = lax.div(edge, ring * lines) * ring + lax.rem(edge, ring)
    slot = jnp.where(has_edge, slot, 0)
    shape = (ROWS, LANES)
    low = jnp.full(shape, LOW, f32)
    extra = in_ref[slot, ROWS:].astype(f32)
    extra_top = jnp.broadcast_to(extra[:, 0:1] + extra[:, DH : DH + 1], shape)
    extra_top = jnp.where(has_edge, extra_top, low)
    top0, full0, top1, full1 = low, low, extra_top, extra_top
    late, is_edge = [], []
    for k in range(senders):
        j = (k // ring) * (ring * lines) + k % ring + line * ring
        late.append(j * tokens >= split)
        is_edge.append(jnp.logical_and(has_edge, slot == k))
        first = in_ref[k, :ROWS].astype(f32)
        other = in_ref[k, ROWS:].astype(f32)
        top = jnp.broadcast_to(first[:, 0:1] + first[:, DH : DH + 1], shape)
        full = top + jnp.where(is_edge[k], 0.0, jnp.broadcast_to(other[:, 0:1], shape))
        tops[k] = top
        top0 = jnp.maximum(top0, jnp.where(late[k], low, top))
        full0 = jnp.maximum(full0, jnp.where(late[k], low, full))
        top1 = jnp.maximum(top1, jnp.where(late[k], top, low))
        full1 = jnp.maximum(full1, jnp.where(late[k], full, low))
    n0 = jnp.zeros(shape, f32)
    n1 = jnp.where(has_edge, extra * jnp.exp(extra_top - top1), 0.0)
    for k in range(senders):
        first = in_ref[k, :ROWS].astype(f32)
        other = in_ref[k, ROWS:].astype(f32)
        value = first + jnp.where(is_edge[k], 0.0, other)
        value = value * jnp.exp(tops[k] - jnp.where(late[k], top1, top0))
        n0 = n0 + jnp.where(late[k], 0.0, value)
        n1 = n1 + jnp.where(late[k], value, 0.0)
    lane = lanes_of(shape)
    n0 = jnp.where(lane == 0, top0, jnp.where(lane == DH, full0, n0))
    n1 = jnp.where(lane == 0, top1, jnp.where(lane == DH, full1, n1))
    out_ref[...] = jnp.broadcast_to(jnp.concatenate([n0, n1], axis=0)[None], out_ref.shape)


def norm_kernel(in_ref, gain_ref, bias_ref, out_ref):
    got = in_ref[...]
    top = jnp.broadcast_to(got[:, :, 0:1], got.shape)
    whole = jnp.max(top, axis=0)
    full = jnp.max(jnp.broadcast_to(got[:, :, DH : DH + 1], got.shape), axis=0)
    n = jnp.sum(got * jnp.exp(top - whole[None]), axis=0)
    lane = lanes_of((2 * ROWS, LANES))
    left = lane < DH
    used = jnp.logical_and(lane != 0, lane != DH)

    def halves(v):
        a = jnp.sum(jnp.where(left, v, 0.0), axis=1, keepdims=True)
        b = jnp.sum(jnp.where(left, 0.0, v), axis=1, keepdims=True)
        return jnp.where(left, a, b) * (1.0 / DH)

    n = jnp.where(used, n, 0.0)
    centred = n - halves(n)
    variance = halves(centred * centred)
    scale = jnp.exp(2.0 * (full - whole))
    table = centred * lax.rsqrt(variance + EPS * scale) * gain_ref[...] + bias_ref[...]
    t0, t1 = table[:ROWS], table[ROWS:]
    left = left[:ROWS]
    keys = jnp.where(left, t0, pltpu.roll(t1, DH, 1))
    values = jnp.where(left, pltpu.roll(t0, DH, 1), t1)
    chunk = jnp.concatenate([keys, values], axis=0).astype(bf16)[None]
    out_ref[...] = jnp.broadcast_to(chunk, out_ref.shape)


def far_kernel(q2_ref, tab_ref, o_ref, stat_ref, out_ref):
    parts = R // ROWS
    second = stat_ref[HEADS : HEADS + 1, :] > 0.5
    for pair in range(HEADS // 2):
        outs = []
        for half in range(2):
            h = 2 * pair + half
            keys = tab_ref[h * parts : (h + 1) * parts, :ROWS].reshape(R, LANES)
            values = tab_ref[h * parts : (h + 1) * parts, ROWS:].reshape(R, LANES)
            scores = dot_nt(keys, q2_ref[h])
            near_top = stat_ref[h : h + 1, :]
            near_total = stat_ref[2 * HEADS + h : 2 * HEADS + h + 1, :]
            top = jnp.maximum(jnp.max(scores, axis=0, keepdims=True), near_top)
            weight = jnp.exp(scores - top)
            scale = jnp.exp(near_top - top)
            total = jnp.sum(weight, axis=0, keepdims=True) + near_total * scale
            far = dot_tn(values, weight.astype(bf16))
            far = jnp.where(second, far[DH:], far[:DH])
            outs.append((o_ref[h * DH : (h + 1) * DH] * scale + far) / total)
        both = jnp.concatenate(outs, axis=0)
        out_ref[:, pair * LANES : (pair + 1) * LANES] = jnp.transpose(both).astype(bf16)


def on_device(inputs, queries, keys_values, slot_weight, slot_gain, slot_bias, bounds):
    tokens, width = inputs.shape
    shards = lax.axis_size(SEQ)
    shard = lax.axis_index(SEQ)
    split = jnp.where(bounds[0, 0] > 0, bounds[0, 0], bounds[1, 0])
    base = shard * tokens
    yh, c = lax.axis_index("yh"), lax.axis_index("c")
    scal = jnp.stack(
        [
            split - base,
            base,
            jnp.int32(shards * tokens),
            yh * 2 + c,
            yh * 2 + 1 - c,
            (1 - yh) * 2 + c,
            (1 - yh) * 2 + 1 - c,
        ]
    ).astype(jnp.int32)
    line = lax.axis_index(LINE)
    slot = lax.axis_index(RING)
    lines = lax.axis_size(LINE)
    slots_held = lax.axis_size(RING)
    scal2 = jnp.stack([split, line]).astype(jnp.int32)

    x2 = lax.ppermute(inputs, "yh", SWAP)
    x1 = lax.ppermute(inputs, "c", SWAP)
    x3 = lax.ppermute(x2, "c", SWAP)
    up = [(i, i + 1) for i in range(shards - 1)]
    down = [(j, i) for i, j in up]
    before = lax.ppermute(keys_values[:, tokens - W :], SEQ, up)
    after = lax.ppermute(keys_values[:, :W], SEQ, down)

    weight_t = jnp.swapaxes(slot_weight.reshape(4, width, HEADS * R), 1, 2)
    kvh = call(
        prep_kernel,
        jax.ShapeDtypeStruct((HEADS, tokens, 2 * LANES), bf16),
        1, 8, 0, 2 << 20,
    )(scal, keys_values)

    slots = HEADS * R
    flops = 2 * tokens * slots * width
    acc_shape = jax.ShapeDtypeStruct((slots, tokens), f32)
    acc = call(partial_kernel, acc_shape, 3, 16, 2 * flops, 5 << 20)(
        scal, inputs, x1, weight_t
    )
    acc = call(more_kernel, acc_shape, 3, 16, flops, 6 << 20)(scal, x2, weight_t, acc)
    sent = pl.pallas_call(
        project_kernel,
        out_shape=jax.ShapeDtypeStruct((slots_held, 2 * ROWS, LANES), bf16),
        in_specs=[SMEM] + [VMEM] * 4,
        out_specs=pl.BlockSpec(memory_space=pltpu.HBM),
        scratch_shapes=[
            pltpu.VMEM((HEADS, R // ROWS, 2 * ROWS, LANES), bf16),
            pltpu.SemaphoreType.DMA((HEADS,)),
        ],
        compiler_params=pltpu.CompilerParams(vmem_limit_bytes=24 << 20),
        cost_estimate=pl.CostEstimate(
            flops=2 * flops, bytes_accessed=5 << 20, transcendentals=tokens * slots
        ),
    )(scal, x3, weight_t, acc, kvh)
    arrived = lax.all_to_all(sent, RING, 0, 0, tiled=True)

    near, stats, q2 = call(
        near_kernel,
        [
            jax.ShapeDtypeStruct((HEADS * DH, tokens), f32),
            jax.ShapeDtypeStruct((4 * HEADS, tokens), f32),
            jax.ShapeDtypeStruct((HEADS, tokens, LANES), bf16),
        ],
        4, 8, 4 * tokens * 3 * W * HEADS * LANES, 2 << 20, tokens * 3 * W * HEADS,
    )(scal, queries, keys_values, before, after)

    held = call(
        functools.partial(combine_kernel, lines, lax.axis_size("x"), tokens),
        jax.ShapeDtypeStruct((lines, 2 * ROWS, LANES), f32),
        1, 8, 0, 1 << 20, 1 << 17,
        scratch=[pltpu.VMEM((slots_held, ROWS, LANES), f32)],
    )(scal2, arrived)
    shared = lax.all_to_all(held, LINE, 0, 0, tiled=True)
    head = lax.div(slot * ROWS, R)
    gain = lax.dynamic_slice_in_dim(slot_gain, head * DH, DH, 1).reshape(1, 2 * DH)
    bias = lax.dynamic_slice_in_dim(slot_bias, head * DH, DH, 1).reshape(1, 2 * DH)
    chunk = call(
        norm_kernel,
        jax.ShapeDtypeStruct((slots_held, 2 * ROWS, LANES), bf16),
        3, 8, 0, 1 << 20, 1 << 15, 0,
    )(shared, gain, bias)
    table = lax.all_to_all(chunk, RING, 0, 0, tiled=True)

    return call(
        far_kernel,
        jax.ShapeDtypeStruct((tokens, HEADS * DH), bf16),
        4, 12, 4 * tokens * R * HEADS * LANES, 2 << 20, tokens * R * HEADS, 0,
    )(q2, table, near, stats)


def solution(mesh):
    finer = Mesh(mesh.devices.reshape(8, 4, 4, 2, 2), SEQ + DOC)
    return jax.shard_map(
        on_device,
        mesh=finer,
        in_specs=(
            P(SEQ, DOC),
            P(SEQ, DOC),
            P(None, SEQ, DOC),
            P(None, DOC),
            P(None, DOC),
            P(None, DOC),
            P(None, SEQ),
        ),
        out_specs=P(SEQ, DOC),
        check_vma=False,
    )
```

time: 114 us -> 108 us (0.947)
  Pallas kernels: 21.6 us -> 15.6 us
    pallas_call x2, Pallas kernels: 8.07 us -> 5.46 us  [the longest x1 3.21 us: on_device(): call(functools.partial(combine_kernel, lines, lax.axis_size('x'), tokens)...]
    pallas_call x1, Pallas kernels: 4.4 us -> 2.34 us  [on_device(): call(far_kernel, jax.ShapeDtypeStruct((tokens, HEADS * DH), bf16), 4, 12,...]
  transfers between devices with their start and end apart: 8 -> 8, of which waited for: 5 -> 5; matrix products, arithmetic and copies ran while one was open for 4% -> 4% of each run, Pallas kernels for 8% -> 5%
where the time goes in v4:
time: 108 us; the launch traced here: 107 us
  waiting for transfers between devices  43.6 us (40%)
  starting transfers between devices  41 us (38%)
  Pallas kernels  15.6 us (14%)
  local copies, waits for them, and re-layouts  4.62 us (4%)
  between operations  2.11 us (2%)
    all_to_all x1, waiting for transfers between devices, on_device(): arrived = lax.all_to_all(sent, RING, 0, 0, tiled=True)  17.4 us
    all_to_all x1, starting transfers between devices, on_device(): arrived = lax.all_to_all(sent, RING, 0, 0, tiled=True)  13.6 us
    ppermute x1, waiting for transfers between devices, on_device(): x2 = lax.ppermute(inputs, 'yh', SWAP)  13.2 us
    ppermute x1, waiting for transfers between devices, on_device(): after = lax.ppermute(keys_values[:, :W], SEQ, down)  8.34 us
    all_to_all x1, starting transfers between devices, on_device(): shared = lax.all_to_all(held, LINE, 0, 0, tiled=True)  6.19 us
    all_to_all x1, starting transfers between devices, on_device(): table = lax.all_to_all(chunk, RING, 0, 0, tiled=True)  5.56 us
    ppermute x1, starting transfers between devices, on_device(): before = lax.ppermute(keys_values[:, tokens - W:], SEQ, up)  5.21 us
    ppermute x1, starting transfers between devices, on_device(): x2 = lax.ppermute(inputs, 'yh', SWAP)  4.7 us
  transfers between devices with their start and end apart: 8, of which 5 were waited for; matrix products, arithmetic and copies ran while one was open for 4% of the time, Pallas kernels for 5%

profile of v4, /device:TPU:62, one launch (start us, length us, event | category | flops | bytes accessed | tf_op | source)
XLA Modules:
  0.0 107.0 jit_solution(7852219741638095365)
XLA Ops:
  0.0 4.7 %collective-permute-start.2 = (bf16[512,256]{1,0:T(8,128)(2,1)}, bf16[512,256]{1,0:T(8,128)(2,1)}, u32[]{:S(2)}, u32[]{:S(2)}) collective-permute-start(bf16[512,256]{1,0:T(8,128)(2,1)} %x0.1), channel_id=1, source_target_pairs={{0,2},{2,0},{1,3},{3,1},{4,6},{6,4},{5,7},{7,5},{8,10},{10,8},{9,1... | collective-permute-start | bytes 786440 | tf_op jit(solution)/shard_map/ppermute | solution.py:326
  4.7 1.9 %collective-permute-start.4 = (bf16[512,256]{1,0:T(8,128)(2,1)}, bf16[512,256]{1,0:T(8,128)(2,1)S(1)}, u32[]{:S(2)}, u32[]{:S(2)}) collective-permute-start(bf16[512,256]{1,0:T(8,128)(2,1)} %x0.1), channel_id=1, source_target_pairs={{0,1},{1,0},{2,3},{3,2},{4,5},{5,4},{6,7},{7,6},{8,9},{9,8},{10,11... | collective-permute-start | bytes 786440 | tf_op jit(solution)/shard_map/ppermute | solution.py:327
  6.6 13.2 %collective-permute-done.2.x2 = bf16[512,256]{1,0:T(8,128)(2,1)} collective-permute-done((bf16[512,256]{1,0:T(8,128)(2,1)}, bf16[512,256]{1,0:T(8,128)(2,1)}, u32[]{:S(2)}, u32[]{:S(2)}) %collective-permute-start.2) | collective-permute-done | bytes 262176 | tf_op jit(solution)/shard_map/ppermute | solution.py:326
  19.8 1.9 %collective-permute-start.3 = (bf16[512,256]{1,0:T(8,128)(2,1)}, bf16[512,256]{1,0:T(8,128)(2,1)S(1)}, u32[]{:S(2)}, u32[]{:S(2)}) collective-permute-start(bf16[512,256]{1,0:T(8,128)(2,1)} %collective-permute-done.2.x2), channel_id=1, source_target_pairs={{0,1},{1,0},{2,3},{3,2},{4,5},{5,4},{6,7},{7,6},{8,9},{9,8},{10,11... | collective-permute-start | bytes 786440 | tf_op jit(solution)/shard_map/ppermute | solution.py:328
  21.8 0.0 copy-start
  21.8 0.0 copy-start.1
  21.8 2.9 %copy.8 = bf16[4,256,1024]{1,2,0:T(8,128)(2,1)S(1)} copy(bf16[4,256,1024]{2,1,0:T(8,128)(2,1)} %bitcast.15) | data formatting | bytes 4194304 | tf_op jit(solution)/shard_map/reshape | solution.py:334
  24.7 1.3 %fusion.1 = (s32[1,1]{1,0:T(1,128)}, s32[1,1]{1,0:T(1,128)}) fusion(s32[2,512]{1,0:T(2,128)} %param.13), kind=kLoop, calls=%fused_computation.4 | loop fusion | bytes 16 | tf_op jit(solution)/shard_map/slice | solution.py:306
  27.9 0.1 stack.36.scal
  28.0 0.0 copy-done
  28.0 0.9 shard_map.76.kvh_ref
  29.0 0.0 collective-permute-done.4.x1
  29.0 0.0 copy-done.1
  29.0 1.3 %shard_map.74.acc_ref = f32[1024,512]{1,0:T(8,128)S(1)} custom-call(s32[7]{0:T(128)S(1)} %stack.36.scal, bf16[512,256]{1,0:T(8,128)(2,1)S(1)} %copy-done.1, bf16[512,256]{1,0:T(8,128)(2,1)S(1)} %collective-permute-done.4.x1, bf16[4,1024,256]{2,1,0:T(8,128)(2,1)S(1)} %bitcast.12), custom_call_target="tpu_custom_call" | custom-call | flops 536870912 | bytes 5242880 | tf_op jit(solution)/shard_map/pallas_call | solution.py:344
  30.3 1.4 %shard_map.75.acc_ref = f32[1024,512]{1,0:T(8,128)S(1)} custom-call(s32[7]{0:T(128)S(1)} %stack.36.scal, bf16[512,256]{1,0:T(8,128)(2,1)} %collective-permute-done.2.x2, bf16[4,1024,256]{2,1,0:T(8,128)(2,1)S(1)} %bitcast.13, f32[1024,512]{1,0:T(8,128)S(1)} %shard_map.74.acc_ref), custom_call_target="tpu_custom_call" | custom-call | flops 268435456 | bytes 6291456 | tf_op jit(solution)/shard_map/pallas_call | solution.py:347
  31.7 0.0 copy-start.3
  31.7 0.0 copy-start.4
  31.7 0.0 collective-permute-done.3.x3
  31.7 2.9 %shard_map.77 = bf16[32,64,128]{2,1,0:T(8,128)(2,1)} custom-call(s32[7]{0:T(128)S(1)} %stack.36.scal, bf16[512,256]{1,0:T(8,128)(2,1)S(1)} %collective-permute-done.3.x3, bf16[4,1024,256]{2,1,0:T(8,128)(2,1)S(1)} %bitcast.14, f32[1024,512]{1,0:T(8,128)S(1)} %shard_map.75.acc_ref, bf16[4,512,256]{2,1,0:T(8,128)(2,1)S(1)} %shard_map.76.kvh_ref), custom_call_target="tpu_custom_call" | custom-call | flops 536870912 | bytes 5242880 | tf_op jit(solution)/shard_map/pallas_call | solution.py:348
  34.7 0.0 copy-start.2
  34.7 13.6 %all-to-all-start = ((bf16[32,64,128]{2,1,0:T(8,128)(2,1)}), bf16[32,64,128]{2,1,0:T(8,128)(2,1)S(1)}, u32[]{:S(2)}, u32[]{:S(2)}) async-start(bf16[32,64,128]{2,1,0:T(8,128)(2,1)} %shard_map.77), calls=%async_computation | async-start | bytes 1048576 | tf_op jit(solution)/shard_map/all_to_all | solution.py:362
  48.2 0.1 pad_add_fusion.scal
  48.3 17.4 %all-to-all-done.in_ref = bf16[32,64,128]{2,1,0:T(8,128)(2,1)S(1)} async-done(((bf16[32,64,128]{2,1,0:T(8,128)(2,1)}), bf16[32,64,128]{2,1,0:T(8,128)(2,1)S(1)}, u32[]{:S(2)}, u32[]{:S(2)}) %all-to-all-start) | async-done | bytes 524320 | tf_op jit(solution)/shard_map/all_to_all | solution.py:362
  65.7 3.2 %shard_map.78 = f32[4,64,128]{2,1,0:T(8,128)} custom-call(s32[2]{0:T(128)S(1)} %pad_add_fusion.scal, bf16[32,64,128]{2,1,0:T(8,128)(2,1)S(1)} %all-to-all-done.in_ref), custom_call_target="tpu_custom_call" | custom-call | bytes 1048576 | tf_op jit(solution)/shard_map/pallas_call | solution.py:374
  69.0 6.2 %all-to-all-start.1 = ((f32[4,64,128]{2,1,0:T(8,128)}), f32[4,64,128]{2,1,0:T(8,128)S(1)}, u32[]{:S(2)}, u32[]{:S(2)}) async-start(f32[4,64,128]{2,1,0:T(8,128)} %shard_map.78), calls=%async_computation.1 | async-start | bytes 262144 | tf_op jit(solution)/shard_map/all_to_all | solution.py:380
  75.1 0.0 copy-done.3
  75.2 0.0 copy-done.4
  75.2 0.1 constant_dynamic-slice_fusion
  75.2 0.1 reshape.10.gain_ref
  75.3 0.1 reshape.11.bias_ref
  75.4 3.3 %all-to-all-done.1.in_ref = f32[4,64,128]{2,1,0:T(8,128)S(1)} async-done(((f32[4,64,128]{2,1,0:T(8,128)}), f32[4,64,128]{2,1,0:T(8,128)S(1)}, u32[]{:S(2)}, u32[]{:S(2)}) %all-to-all-start.1) | async-done | bytes 131104 | tf_op jit(solution)/shard_map/all_to_all | solution.py:380
  78.7 1.2 %shard_map.79 = bf16[32,64,128]{2,1,0:T(8,128)(2,1)} custom-call(f32[4,64,128]{2,1,0:T(8,128)S(1)} %all-to-all-done.1.in_ref, f32[1,128]{1,0:T(1,128)S(1)} %reshape.10.gain_ref, f32[1,128]{1,0:T(1,128)S(1)} %reshape.11.bias_ref), custom_call_target="tpu_custom_call" | custom-call | bytes 1048576 | tf_op jit(solution)/shard_map/pallas_call | solution.py:384
  79.9 5.6 %all-to-all-start.2 = ((bf16[32,64,128]{2,1,0:T(8,128)(2,1)}), bf16[32,64,128]{2,1,0:T(8,128)(2,1)S(1)}, u32[]{:S(2)}, u32[]{:S(2)}) async-start(bf16[32,64,128]{2,1,0:T(8,128)(2,1)} %shard_map.79), calls=%async_computation.2 | async-start | bytes 1048576 | tf_op jit(solution)/shard_map/all_to_all | solution.py:389
  85.5 5.2 %collective-permute-start = (bf16[2,128,256]{2,1,0:T(8,128)(2,1)S(1)}, bf16[2,128,256]{2,1,0:T(8,128)(2,1)S(1)}, u32[]{:S(2)}, u32[]{:S(2)}) collective-permute-start(bf16[2,128,256]{2,1,0:T(8,128)(2,1)S(1)} %get-tuple-element.12), channel_id=1, source_target_pairs={{0,4},{4,8},{8,12},{12,16},{16,20},{20,24},{24,28},{28,32},{32,36}... | collective-permute-start | bytes 393224 | tf_op jit(solution)/shard_map/ppermute | solution.py:331
  90.7 1.9 %collective-permute-start.1 = (bf16[2,128,256]{2,1,0:T(8,128)(2,1)S(1)}, bf16[2,128,256]{2,1,0:T(8,128)(2,1)S(1)}, u32[]{:S(2)}, u32[]{:S(2)}) collective-permute-start(bf16[2,128,256]{2,1,0:T(8,128)(2,1)S(1)} %get-tuple-element.11), channel_id=1, source_target_pairs={{4,0},{8,4},{12,8},{16,12},{20,16},{24,20},{28,24},{32,28},{36,32}... | collective-permute-start | bytes 393224 | tf_op jit(solution)/shard_map/ppermute | solution.py:332
  92.7 1.4 %collective-permute-done.before_ref = bf16[2,128,256]{2,1,0:T(8,128)(2,1)S(1)} collective-permute-done((bf16[2,128,256]{2,1,0:T(8,128)(2,1)S(1)}, bf16[2,128,256]{2,1,0:T(8,128)(2,1)S(1)}, u32[]{:S(2)}, u32[]{:S(2)}) %collective-permute-start) | collective-permute-done | bytes 131104 | tf_op jit(solution)/shard_map/ppermute | solution.py:331
  94.1 8.3 %collective-permute-done.1.after_ref = bf16[2,128,256]{2,1,0:T(8,128)(2,1)S(1)} collective-permute-done((bf16[2,128,256]{2,1,0:T(8,128)(2,1)S(1)}, bf16[2,128,256]{2,1,0:T(8,128)(2,1)S(1)}, u32[]{:S(2)}, u32[]{:S(2)}) %collective-permute-start.1) | collective-permute-done | bytes 131104 | tf_op jit(solution)/shard_map/ppermute | solution.py:332
  102.4 0.0 copy-done.2
  102.4 2.2 %shard_map.73 = (f32[256,512]{1,0:T(8,128)S(1)}, f32[16,512]{1,0:T(8,128)S(1)}, bf16[4,512,128]{2,1,0:T(8,128)(2,1)S(1)}) custom-call(s32[7]{0:T(128)S(1)} %stack.36.scal, bf16[512,256]{1,0:T(8,128)(2,1)S(1)} %copy-done.2, bf16[2,512,256]{2,1,0:T(8,128)(2,1)S(1)} %copy-done, bf16[2,128,256]{2,1,0:T(8,128)(2,1)S(1)} %collective-permute-done.before_ref, ...), custom_call_target="tpu_custom_call" | custom-call | flops 402653184 | bytes 2097152 | tf_op jit(solution)/shard_map/pallas_call | solution.py:364
  104.7 0.0 all-to-all-done.2.tab_ref
  104.7 2.3 %shard_map.80 = bf16[512,256]{1,0:T(8,128)(2,1)} custom-call(bf16[4,512,128]{2,1,0:T(8,128)(2,1)S(1)} %get-tuple-element.8.q2_ref, bf16[32,64,128]{2,1,0:T(8,128)(2,1)S(1)} %all-to-all-done.2.tab_ref, f32[256,512]{1,0:T(8,128)S(1)} %get-tuple-element.9.o_ref, f32[16,512]{1,0:T(8,128)S(1)} %get-tuple-element.10.stat_ref), custom_call_target="tpu_custom_call" | custom-call | flops 268435456 | bytes 2097152 | tf_op jit(solution)/shard_map/pallas_call | solution.py:391
  (1 shorter events, 0.0 us)
Async XLA Ops:
  0.0 19.8 %collective-permute-start.2 = (bf16[512,256]{1,0:T(8,128)(2,1)}, bf16[512,256]{1,0:T(8,128)(2,1)}, u32[]{:S(2)}, u32[]{:S(2)}) collective-permute-start(bf16[512,256]{1,0:T(8,128)(2,1)} %x0.1), channel_id=1, source_target_pairs={{0,2},{2,0},{1,3},{3,1},{4,6},{6,4},{5,7},{7,5},{8,10},{10,8},{9,1... | collective-permute-start | bytes 786440 | tf_op jit(solution)/shard_map/ppermute | solution.py:326
  4.7 24.3 %collective-permute-start.4 = (bf16[512,256]{1,0:T(8,128)(2,1)}, bf16[512,256]{1,0:T(8,128)(2,1)S(1)}, u32[]{:S(2)}, u32[]{:S(2)}) collective-permute-start(bf16[512,256]{1,0:T(8,128)(2,1)} %x0.1), channel_id=1, source_target_pairs={{0,1},{1,0},{2,3},{3,2},{4,5},{5,4},{6,7},{7,6},{8,9},{9,8},{10,11... | collective-permute-start | bytes 786440 | tf_op jit(solution)/shard_map/ppermute | solution.py:327
  19.8 11.9 %collective-permute-start.3 = (bf16[512,256]{1,0:T(8,128)(2,1)}, bf16[512,256]{1,0:T(8,128)(2,1)S(1)}, u32[]{:S(2)}, u32[]{:S(2)}) collective-permute-start(bf16[512,256]{1,0:T(8,128)(2,1)} %collective-permute-done.2.x2), channel_id=1, source_target_pairs={{0,1},{1,0},{2,3},{3,2},{4,5},{5,4},{6,7},{7,6},{8,9},{9,8},{10,11... | collective-permute-start | bytes 786440 | tf_op jit(solution)/shard_map/ppermute | solution.py:328
  21.8 6.3 %copy-start = (bf16[2,512,256]{2,1,0:T(8,128)(2,1)S(1)}, bf16[2,512,256]{2,1,0:T(8,128)(2,1)}, u32[]{:S(2)}) copy-start(bf16[2,512,256]{2,1,0:T(8,128)(2,1)} %kv_ref.3) | copy-start | bytes 1572868
  21.8 7.2 %copy-start.1 = (bf16[512,256]{1,0:T(8,128)(2,1)S(1)}, bf16[512,256]{1,0:T(8,128)(2,1)}, u32[]{:S(2)}) copy-start(bf16[512,256]{1,0:T(8,128)(2,1)} %x0.1) | copy-start | bytes 786436
  31.7 43.5 %copy-start.3 = (f32[2,256]{1,0:T(2,128)S(1)}, f32[2,256]{1,0:T(2,128)}, u32[]{:S(2)}) copy-start(f32[2,256]{1,0:T(2,128)} %param.12) | copy-start | bytes 6148
  31.7 43.4 %copy-start.4 = (f32[2,256]{1,0:T(2,128)S(1)}, f32[2,256]{1,0:T(2,128)}, u32[]{:S(2)}) copy-start(f32[2,256]{1,0:T(2,128)} %param.11) | copy-start | bytes 6148
  34.7 67.7 %copy-start.2 = (bf16[512,256]{1,0:T(8,128)(2,1)S(1)}, bf16[512,256]{1,0:T(8,128)(2,1)}, u32[]{:S(2)}) copy-start(bf16[512,256]{1,0:T(8,128)(2,1)} %q_ref.1) | copy-start | bytes 786436
  34.7 31.1 %all-to-all-start = ((bf16[32,64,128]{2,1,0:T(8,128)(2,1)}), bf16[32,64,128]{2,1,0:T(8,128)(2,1)S(1)}, u32[]{:S(2)}, u32[]{:S(2)}) async-start(bf16[32,64,128]{2,1,0:T(8,128)(2,1)} %shard_map.77), calls=%async_computation | async-start | bytes 1048576 | tf_op jit(solution)/shard_map/all_to_all | solution.py:362
  69.0 9.7 %all-to-all-start.1 = ((f32[4,64,128]{2,1,0:T(8,128)}), f32[4,64,128]{2,1,0:T(8,128)S(1)}, u32[]{:S(2)}, u32[]{:S(2)}) async-start(f32[4,64,128]{2,1,0:T(8,128)} %shard_map.78), calls=%async_computation.1 | async-start | bytes 262144 | tf_op jit(solution)/shard_map/all_to_all | solution.py:380
  79.9 24.8 %all-to-all-start.2 = ((bf16[32,64,128]{2,1,0:T(8,128)(2,1)}), bf16[32,64,128]{2,1,0:T(8,128)(2,1)S(1)}, u32[]{:S(2)}, u32[]{:S(2)}) async-start(bf16[32,64,128]{2,1,0:T(8,128)(2,1)} %shard_map.79), calls=%async_computation.2 | async-start | bytes 1048576 | tf_op jit(solution)/shard_map/all_to_all | solution.py:389
  85.5 8.6 %collective-permute-start = (bf16[2,128,256]{2,1,0:T(8,128)(2,1)S(1)}, bf16[2,128,256]{2,1,0:T(8,128)(2,1)S(1)}, u32[]{:S(2)}, u32[]{:S(2)}) collective-permute-start(bf16[2,128,256]{2,1,0:T(8,128)(2,1)S(1)} %get-tuple-element.12), channel_id=1, source_target_pairs={{0,4},{4,8},{8,12},{12,16},{16,20},{20,24},{24,28},{28,32},{32,36}... | collective-permute-start | bytes 393224 | tf_op jit(solution)/shard_map/ppermute | solution.py:331
  90.7 11.7 %collective-permute-start.1 = (bf16[2,128,256]{2,1,0:T(8,128)(2,1)S(1)}, bf16[2,128,256]{2,1,0:T(8,128)(2,1)S(1)}, u32[]{:S(2)}, u32[]{:S(2)}) collective-permute-start(bf16[2,128,256]{2,1,0:T(8,128)(2,1)S(1)} %get-tuple-element.11), channel_id=1, source_target_pairs={{4,0},{8,4},{12,8},{16,12},{20,16},{24,20},{28,24},{32,28},{36,32}... | collective-permute-start | bytes 393224 | tf_op jit(solution)/shard_map/ppermute | solution.py:332

commit v5 on v4

--- a/solution.py
+++ b/solution.py
@@ -171,8 +171,11 @@
     def _():
         side = pl.multiple_of(jnp.where(local <= 0, LANES, 0), LANES)
         copies = []
+        after = logits_of(0)
         for h in range(HEADS):
-            logits = logits_of(h)
+            logits = after
+            if h + 1 < HEADS:
+                after = logits_of(h + 1)
             a, b, c = pieces_of(jnp.max(logits, axis=1, keepdims=True))
             proj = jnp.exp(logits - (a + b)).astype(bf16)
             n = from_first(
@@ -204,7 +207,7 @@
             copy.wait()
 
 
-def combine_kernel(lines, ring, tokens, scal, in_ref, out_ref, tops):
+def combine_kernel(lines, ring, tokens, scal, in_ref, out_ref, tops, held):
     senders = in_ref.shape[0]
     split, line = scal[0], scal[1]
     edge = lax.div(split, tokens)
@@ -213,39 +216,44 @@
     )
     slot = lax.div(edge, ring * lines) * ring + lax.rem(edge, ring)
     slot = jnp.where(has_edge, slot, 0)
-    shape = (ROWS, LANES)
+    half = ROWS // 2
+    shape = (half, LANES)
     low = jnp.full(shape, LOW, f32)
-    extra = in_ref[slot, ROWS:].astype(f32)
-    extra_top = jnp.broadcast_to(extra[:, 0:1] + extra[:, DH : DH + 1], shape)
-    extra_top = jnp.where(has_edge, extra_top, low)
-    top0, full0, top1, full1 = low, low, extra_top, extra_top
-    late, is_edge = [], []
-    for k in range(senders):
-        j = (k // ring) * (ring * lines) + k % ring + line * ring
-        late.append(j * tokens >= split)
-        is_edge.append(jnp.logical_and(has_edge, slot == k))
-        first = in_ref[k, :ROWS].astype(f32)
-        other = in_ref[k, ROWS:].astype(f32)
-        top = jnp.broadcast_to(first[:, 0:1] + first[:, DH : DH + 1], shape)
-        full = top + jnp.where(is_edge[k], 0.0, jnp.broadcast_to(other[:, 0:1], shape))
-        tops[k] = top
-        top0 = jnp.maximum(top0, jnp.where(late[k], low, top))
-        full0 = jnp.maximum(full0, jnp.where(late[k], low, full))
-        top1 = jnp.maximum(top1, jnp.where(late[k], top, low))
-        full1 = jnp.maximum(full1, jnp.where(late[k], full, low))
-    n0 = jnp.zeros(shape, f32)
-    n1 = jnp.where(has_edge, extra * jnp.exp(extra_top - top1), 0.0)
-    for k in range(senders):
-        first = in_ref[k, :ROWS].astype(f32)
-        other = in_ref[k, ROWS:].astype(f32)
-        value = first + jnp.where(is_edge[k], 0.0, other)
-        value = value * jnp.exp(tops[k] - jnp.where(late[k], top1, top0))
-        n0 = n0 + jnp.where(late[k], 0.0, value)
-        n1 = n1 + jnp.where(late[k], value, 0.0)
+    border = jnp.full(shape, split - line * (ring * tokens), jnp.int32)
     lane = lanes_of(shape)
-    n0 = jnp.where(lane == 0, top0, jnp.where(lane == DH, full0, n0))
-    n1 = jnp.where(lane == 0, top1, jnp.where(lane == DH, full1, n1))
-    out_ref[...] = jnp.broadcast_to(jnp.concatenate([n0, n1], axis=0)[None], out_ref.shape)
+    starts = [((k // ring) * (ring * lines) + k % ring) * tokens for k in range(senders)]
+    for part in range(2):
+        hi = slice(part * half, (part + 1) * half)
+        lo = slice(ROWS + part * half, ROWS + (part + 1) * half)
+        extra = in_ref[slot, lo].astype(f32)
+        extra_top = jnp.broadcast_to(extra[:, 0:1] + extra[:, DH : DH + 1], shape)
+        extra_top = jnp.where(has_edge, extra_top, low)
+        top0, full0, top1, full1 = low, low, extra_top, extra_top
+        for k in range(senders):
+            late = border <= starts[k]
+            is_edge = jnp.logical_and(border > starts[k], border < starts[k] + tokens)
+            first = in_ref[k, hi].astype(f32)
+            other = jnp.where(is_edge, 0.0, in_ref[k, lo].astype(f32))
+            top = jnp.broadcast_to(first[:, 0:1] + first[:, DH : DH + 1], shape)
+            full = top + jnp.broadcast_to(other[:, 0:1], shape)
+            tops[part, k] = top
+            held[part, k] = first + other
+            top0 = jnp.maximum(top0, jnp.where(late, low, top))
+            full0 = jnp.maximum(full0, jnp.where(late, low, full))
+            top1 = jnp.maximum(top1, jnp.where(late, top, low))
+            full1 = jnp.maximum(full1, jnp.where(late, full, low))
+        n0 = jnp.zeros(shape, f32)
+        n1 = jnp.where(has_edge, extra * jnp.exp(extra_top - top1), 0.0)
+        for k in range(senders):
+            late = border <= starts[k]
+            value = held[part, k] * jnp.exp(tops[part, k] - jnp.where(late, top1, top0))
+            n0 = n0 + jnp.where(late, 0.0, value)
+            n1 = n1 + jnp.where(late, value, 0.0)
+        n0 = jnp.where(lane == 0, top0, jnp.where(lane == DH, full0, n0))
+        n1 = jnp.where(lane == 0, top1, jnp.where(lane == DH, full1, n1))
+        for line_at in range(lines):
+            out_ref[line_at, hi] = n0
+            out_ref[line_at, lo] = n1
 
 
 def norm_kernel(in_ref, gain_ref, bias_ref, out_ref):
@@ -279,24 +287,34 @@
 def far_kernel(q2_ref, tab_ref, o_ref, stat_ref, out_ref):
     parts = R // ROWS
     second = stat_ref[HEADS : HEADS + 1, :] > 0.5
-    for pair in range(HEADS // 2):
-        outs = []
-        for half in range(2):
-            h = 2 * pair + half
-            keys = tab_ref[h * parts : (h + 1) * parts, :ROWS].reshape(R, LANES)
-            values = tab_ref[h * parts : (h + 1) * parts, ROWS:].reshape(R, LANES)
-            scores = dot_nt(keys, q2_ref[h])
-            near_top = stat_ref[h : h + 1, :]
-            near_total = stat_ref[2 * HEADS + h : 2 * HEADS + h + 1, :]
-            top = jnp.maximum(jnp.max(scores, axis=0, keepdims=True), near_top)
-            weight = jnp.exp(scores - top)
-            scale = jnp.exp(near_top - top)
-            total = jnp.sum(weight, axis=0, keepdims=True) + near_total * scale
-            far = dot_tn(values, weight.astype(bf16))
-            far = jnp.where(second, far[DH:], far[:DH])
-            outs.append((o_ref[h * DH : (h + 1) * DH] * scale + far) / total)
-        both = jnp.concatenate(outs, axis=0)
-        out_ref[:, pair * LANES : (pair + 1) * LANES] = jnp.transpose(both).astype(bf16)
+
+    def rows_of(h, part):
+        return tab_ref[h * parts : (h + 1) * parts, part * ROWS : (part + 1) * ROWS].reshape(R, LANES)
+
+    def scores_of(h):
+        return dot_nt(rows_of(h, 0), q2_ref[h])
+
+    after = scores_of(0)
+    outs = []
+    for h in range(HEADS):
+        scores = after
+        if h + 1 < HEADS:
+            after = scores_of(h + 1)
+        near_top = stat_ref[h : h + 1, :]
+        near_total = stat_ref[2 * HEADS + h : 2 * HEADS + h + 1, :]
+        top = jnp.maximum(jnp.max(scores, axis=0, keepdims=True), near_top)
+        weight = jnp.exp(scores - top)
+        scale = jnp.exp(near_top - top)
+        total = jnp.sum(weight, axis=0, keepdims=True) + near_total * scale
+        far = dot_tn(rows_of(h, 1), weight.astype(bf16))
+        far = jnp.where(second, far[DH:], far[:DH])
+        share = 1.0 / total
+        outs.append(o_ref[h * DH : (h + 1) * DH] * (scale * share) + far * share)
+        if h % 2 == 1:
+            both = jnp.concatenate(outs, axis=0)
+            outs = []
+            at = (h // 2) * LANES
+            out_ref[:, at : at + LANES] = jnp.transpose(both).astype(bf16)
 
 
 def on_device(inputs, queries, keys_values, slot_weight, slot_gain, slot_bias, bounds):
@@ -375,7 +393,7 @@
         functools.partial(combine_kernel, lines, lax.axis_size("x"), tokens),
         jax.ShapeDtypeStruct((lines, 2 * ROWS, LANES), f32),
         1, 8, 0, 1 << 20, 1 << 17,
-        scratch=[pltpu.VMEM((slots_held, ROWS, LANES), f32)],
+        scratch=[pltpu.VMEM((2, slots_held, ROWS // 2, LANES), f32)] * 2,
     )(scal2, arrived)
     shared = lax.all_to_all(held, LINE, 0, 0, tiled=True)
     head = lax.div(slot * ROWS, R)

time: 108 us -> 108 us (level)
  no operation moved by 1% of the time
where the time goes in v5:
time: 108 us; the launch traced here: 107 us
  waiting for transfers between devices  43.6 us (40%)
  starting transfers between devices  41 us (38%)
  Pallas kernels  15.6 us (14%)
  local copies, waits for them, and re-layouts  4.62 us (4%)
  between operations  2.11 us (2%)
    all_to_all x1, waiting for transfers between devices, on_device(): arrived = lax.all_to_all(sent, RING, 0, 0, tiled=True)  17.4 us
    all_to_all x1, starting transfers between devices, on_device(): arrived = lax.all_to_all(sent, RING, 0, 0, tiled=True)  13.6 us
    ppermute x1, waiting for transfers between devices, on_device(): x2 = lax.ppermute(inputs, 'yh', SWAP)  13.2 us
    ppermute x1, waiting for transfers between devices, on_device(): after = lax.ppermute(keys_values[:, :W], SEQ, down)  8.34 us
    all_to_all x1, starting transfers between devices, on_device(): shared = lax.all_to_all(held, LINE, 0, 0, tiled=True)  6.19 us
    all_to_all x1, starting transfers between devices, on_device(): table = lax.all_to_all(chunk, RING, 0, 0, tiled=True)  5.56 us
    ppermute x1, starting transfers between devices, on_device(): before = lax.ppermute(keys_values[:, tokens - W:], SEQ, up)  5.21 us
    ppermute x1, starting transfers between devices, on_device(): x2 = lax.ppermute(inputs, 'yh', SWAP)  4.7 us
  transfers between devices with their start and end apart: 8, of which 5 were waited for; matrix products, arithmetic and copies ran while one was open for 4% of the time, Pallas kernels for 5%

profile of v5, /device:TPU:62, one launch (start us, length us, event | category | flops | bytes accessed | tf_op | source)
XLA Modules:
  0.0 107.0 jit_solution(649272110345855318)
XLA Ops:
  0.0 4.7 %collective-permute-start.2 = (bf16[512,256]{1,0:T(8,128)(2,1)}, bf16[512,256]{1,0:T(8,128)(2,1)}, u32[]{:S(2)}, u32[]{:S(2)}) collective-permute-start(bf16[512,256]{1,0:T(8,128)(2,1)} %x0.1), channel_id=1, source_target_pairs={{0,2},{2,0},{1,3},{3,1},{4,6},{6,4},{5,7},{7,5},{8,10},{10,8},{9,1... | collective-permute-start | bytes 786440 | tf_op jit(solution)/shard_map/ppermute | solution.py:344
  4.7 1.9 %collective-permute-start.4 = (bf16[512,256]{1,0:T(8,128)(2,1)}, bf16[512,256]{1,0:T(8,128)(2,1)S(1)}, u32[]{:S(2)}, u32[]{:S(2)}) collective-permute-start(bf16[512,256]{1,0:T(8,128)(2,1)} %x0.1), channel_id=1, source_target_pairs={{0,1},{1,0},{2,3},{3,2},{4,5},{5,4},{6,7},{7,6},{8,9},{9,8},{10,11... | collective-permute-start | bytes 786440 | tf_op jit(solution)/shard_map/ppermute | solution.py:345
  6.6 13.2 %collective-permute-done.2.x2 = bf16[512,256]{1,0:T(8,128)(2,1)} collective-permute-done((bf16[512,256]{1,0:T(8,128)(2,1)}, bf16[512,256]{1,0:T(8,128)(2,1)}, u32[]{:S(2)}, u32[]{:S(2)}) %collective-permute-start.2) | collective-permute-done | bytes 262176 | tf_op jit(solution)/shard_map/ppermute | solution.py:344
  19.8 1.9 %collective-permute-start.3 = (bf16[512,256]{1,0:T(8,128)(2,1)}, bf16[512,256]{1,0:T(8,128)(2,1)S(1)}, u32[]{:S(2)}, u32[]{:S(2)}) collective-permute-start(bf16[512,256]{1,0:T(8,128)(2,1)} %collective-permute-done.2.x2), channel_id=1, source_target_pairs={{0,1},{1,0},{2,3},{3,2},{4,5},{5,4},{6,7},{7,6},{8,9},{9,8},{10,11... | collective-permute-start | bytes 786440 | tf_op jit(solution)/shard_map/ppermute | solution.py:346
  21.8 0.0 copy-start
  21.8 0.0 copy-start.1
  21.8 2.9 %copy.8 = bf16[4,256,1024]{1,2,0:T(8,128)(2,1)S(1)} copy(bf16[4,256,1024]{2,1,0:T(8,128)(2,1)} %bitcast.15) | data formatting | bytes 4194304 | tf_op jit(solution)/shard_map/reshape | solution.py:352
  24.7 1.3 %fusion.1 = (s32[1,1]{1,0:T(1,128)}, s32[1,1]{1,0:T(1,128)}) fusion(s32[2,512]{1,0:T(2,128)} %param.13), kind=kLoop, calls=%fused_computation.4 | loop fusion | bytes 16 | tf_op jit(solution)/shard_map/slice | solution.py:324
  27.9 0.1 stack.36.scal
  28.0 0.0 copy-done
  28.0 0.9 shard_map.76.kvh_ref
  29.0 0.0 collective-permute-done.4.x1
  29.0 0.0 copy-done.1
  29.0 1.3 %shard_map.74.acc_ref = f32[1024,512]{1,0:T(8,128)S(1)} custom-call(s32[7]{0:T(128)S(1)} %stack.36.scal, bf16[512,256]{1,0:T(8,128)(2,1)S(1)} %copy-done.1, bf16[512,256]{1,0:T(8,128)(2,1)S(1)} %collective-permute-done.4.x1, bf16[4,1024,256]{2,1,0:T(8,128)(2,1)S(1)} %bitcast.12), custom_call_target="tpu_custom_call" | custom-call | flops 536870912 | bytes 5242880 | tf_op jit(solution)/shard_map/pallas_call | solution.py:362
  30.3 1.4 %shard_map.75.acc_ref = f32[1024,512]{1,0:T(8,128)S(1)} custom-call(s32[7]{0:T(128)S(1)} %stack.36.scal, bf16[512,256]{1,0:T(8,128)(2,1)} %collective-permute-done.2.x2, bf16[4,1024,256]{2,1,0:T(8,128)(2,1)S(1)} %bitcast.13, f32[1024,512]{1,0:T(8,128)S(1)} %shard_map.74.acc_ref), custom_call_target="tpu_custom_call" | custom-call | flops 268435456 | bytes 6291456 | tf_op jit(solution)/shard_map/pallas_call | solution.py:365
  31.7 0.0 copy-start.3
  31.7 0.0 copy-start.4
  31.7 0.0 collective-permute-done.3.x3
  31.7 2.4 %shard_map.77 = bf16[32,64,128]{2,1,0:T(8,128)(2,1)} custom-call(s32[7]{0:T(128)S(1)} %stack.36.scal, bf16[512,256]{1,0:T(8,128)(2,1)S(1)} %collective-permute-done.3.x3, bf16[4,1024,256]{2,1,0:T(8,128)(2,1)S(1)} %bitcast.14, f32[1024,512]{1,0:T(8,128)S(1)} %shard_map.75.acc_ref, bf16[4,512,256]{2,1,0:T(8,128)(2,1)S(1)} %shard_map.76.kvh_ref), custom_call_target="tpu_custom_call" | custom-call | flops 536870912 | bytes 5242880 | tf_op jit(solution)/shard_map/pallas_call | solution.py:366
  34.2 0.0 copy-start.2
  34.2 13.6 %all-to-all-start = ((bf16[32,64,128]{2,1,0:T(8,128)(2,1)}), bf16[32,64,128]{2,1,0:T(8,128)(2,1)S(1)}, u32[]{:S(2)}, u32[]{:S(2)}) async-start(bf16[32,64,128]{2,1,0:T(8,128)(2,1)} %shard_map.77), calls=%async_computation | async-start | bytes 1048576 | tf_op jit(solution)/shard_map/all_to_all | solution.py:380
  47.8 0.1 pad_add_fusion.scal
  47.8 17.4 %all-to-all-done.in_ref = bf16[32,64,128]{2,1,0:T(8,128)(2,1)S(1)} async-done(((bf16[32,64,128]{2,1,0:T(8,128)(2,1)}), bf16[32,64,128]{2,1,0:T(8,128)(2,1)S(1)}, u32[]{:S(2)}, u32[]{:S(2)}) %all-to-all-start) | async-done | bytes 524320 | tf_op jit(solution)/shard_map/all_to_all | solution.py:380
  65.3 4.2 %shard_map.78 = f32[4,64,128]{2,1,0:T(8,128)} custom-call(s32[2]{0:T(128)S(1)} %pad_add_fusion.scal, bf16[32,64,128]{2,1,0:T(8,128)(2,1)S(1)} %all-to-all-done.in_ref), custom_call_target="tpu_custom_call" | custom-call | bytes 1048576 | tf_op jit(solution)/shard_map/pallas_call | solution.py:392
  69.5 6.2 %all-to-all-start.1 = ((f32[4,64,128]{2,1,0:T(8,128)}), f32[4,64,128]{2,1,0:T(8,128)S(1)}, u32[]{:S(2)}, u32[]{:S(2)}) async-start(f32[4,64,128]{2,1,0:T(8,128)} %shard_map.78), calls=%async_computation.1 | async-start | bytes 262144 | tf_op jit(solution)/shard_map/all_to_all | solution.py:398
  75.7 0.0 copy-done.3
  75.7 0.0 copy-done.4
  75.7 0.1 constant_dynamic-slice_fusion
  75.7 0.1 reshape.10.gain_ref
  75.8 0.1 reshape.11.bias_ref
  75.9 3.3 %all-to-all-done.1.in_ref = f32[4,64,128]{2,1,0:T(8,128)S(1)} async-done(((f32[4,64,128]{2,1,0:T(8,128)}), f32[4,64,128]{2,1,0:T(8,128)S(1)}, u32[]{:S(2)}, u32[]{:S(2)}) %all-to-all-start.1) | async-done | bytes 131104 | tf_op jit(solution)/shard_map/all_to_all | solution.py:398
  79.2 1.2 %shard_map.79 = bf16[32,64,128]{2,1,0:T(8,128)(2,1)} custom-call(f32[4,64,128]{2,1,0:T(8,128)S(1)} %all-to-all-done.1.in_ref, f32[1,128]{1,0:T(1,128)S(1)} %reshape.10.gain_ref, f32[1,128]{1,0:T(1,128)S(1)} %reshape.11.bias_ref), custom_call_target="tpu_custom_call" | custom-call | bytes 1048576 | tf_op jit(solution)/shard_map/pallas_call | solution.py:402
  80.4 5.6 %all-to-all-start.2 = ((bf16[32,64,128]{2,1,0:T(8,128)(2,1)}), bf16[32,64,128]{2,1,0:T(8,128)(2,1)S(1)}, u32[]{:S(2)}, u32[]{:S(2)}) async-start(bf16[32,64,128]{2,1,0:T(8,128)(2,1)} %shard_map.79), calls=%async_computation.2 | async-start | bytes 1048576 | tf_op jit(solution)/shard_map/all_to_all | solution.py:407
  86.0 5.2 %collective-permute-start = (bf16[2,128,256]{2,1,0:T(8,128)(2,1)S(1)}, bf16[2,128,256]{2,1,0:T(8,128)(2,1)S(1)}, u32[]{:S(2)}, u32[]{:S(2)}) collective-permute-start(bf16[2,128,256]{2,1,0:T(8,128)(2,1)S(1)} %get-tuple-element.12), channel_id=1, source_target_pairs={{0,4},{4,8},{8,12},{12,16},{16,20},{20,24},{24,28},{28,32},{32,36}... | collective-permute-start | bytes 393224 | tf_op jit(solution)/shard_map/ppermute | solution.py:349
  91.2 1.9 %collective-permute-start.1 = (bf16[2,128,256]{2,1,0:T(8,128)(2,1)S(1)}, bf16[2,128,256]{2,1,0:T(8,128)(2,1)S(1)}, u32[]{:S(2)}, u32[]{:S(2)}) collective-permute-start(bf16[2,128,256]{2,1,0:T(8,128)(2,1)S(1)} %get-tuple-element.11), channel_id=1, source_target_pairs={{4,0},{8,4},{12,8},{16,12},{20,16},{24,20},{28,24},{32,28},{36,32}... | collective-permute-start | bytes 393224 | tf_op jit(solution)/shard_map/ppermute | solution.py:350
  93.2 1.4 %collective-permute-done.before_ref = bf16[2,128,256]{2,1,0:T(8,128)(2,1)S(1)} collective-permute-done((bf16[2,128,256]{2,1,0:T(8,128)(2,1)S(1)}, bf16[2,128,256]{2,1,0:T(8,128)(2,1)S(1)}, u32[]{:S(2)}, u32[]{:S(2)}) %collective-permute-start) | collective-permute-done | bytes 131104 | tf_op jit(solution)/shard_map/ppermute | solution.py:349
  94.6 8.3 %collective-permute-done.1.after_ref = bf16[2,128,256]{2,1,0:T(8,128)(2,1)S(1)} collective-permute-done((bf16[2,128,256]{2,1,0:T(8,128)(2,1)S(1)}, bf16[2,128,256]{2,1,0:T(8,128)(2,1)S(1)}, u32[]{:S(2)}, u32[]{:S(2)}) %collective-permute-start.1) | collective-permute-done | bytes 131104 | tf_op jit(solution)/shard_map/ppermute | solution.py:350
  102.9 0.0 copy-done.2
  102.9 2.2 %shard_map.73 = (f32[256,512]{1,0:T(8,128)S(1)}, f32[16,512]{1,0:T(8,128)S(1)}, bf16[4,512,128]{2,1,0:T(8,128)(2,1)S(1)}) custom-call(s32[7]{0:T(128)S(1)} %stack.36.scal, bf16[512,256]{1,0:T(8,128)(2,1)S(1)} %copy-done.2, bf16[2,512,256]{2,1,0:T(8,128)(2,1)S(1)} %copy-done, bf16[2,128,256]{2,1,0:T(8,128)(2,1)S(1)} %collective-permute-done.before_ref, ...), custom_call_target="tpu_custom_call" | custom-call | flops 402653184 | bytes 2097152 | tf_op jit(solution)/shard_map/pallas_call | solution.py:382
  105.2 0.0 all-to-all-done.2.tab_ref
  105.2 1.9 %shard_map.80 = bf16[512,256]{1,0:T(8,128)(2,1)} custom-call(bf16[4,512,128]{2,1,0:T(8,128)(2,1)S(1)} %get-tuple-element.8.q2_ref, bf16[32,64,128]{2,1,0:T(8,128)(2,1)S(1)} %all-to-all-done.2.tab_ref, f32[256,512]{1,0:T(8,128)S(1)} %get-tuple-element.9.o_ref, f32[16,512]{1,0:T(8,128)S(1)} %get-tuple-element.10.stat_ref), custom_call_target="tpu_custom_call" | custom-call | flops 268435456 | bytes 2097152 | tf_op jit(solution)/shard_map/pallas_call | solution.py:409
  (1 shorter events, 0.0 us)
Async XLA Ops:
  0.0 19.8 %collective-permute-start.2 = (bf16[512,256]{1,0:T(8,128)(2,1)}, bf16[512,256]{1,0:T(8,128)(2,1)}, u32[]{:S(2)}, u32[]{:S(2)}) collective-permute-start(bf16[512,256]{1,0:T(8,128)(2,1)} %x0.1), channel_id=1, source_target_pairs={{0,2},{2,0},{1,3},{3,1},{4,6},{6,4},{5,7},{7,5},{8,10},{10,8},{9,1... | collective-permute-start | bytes 786440 | tf_op jit(solution)/shard_map/ppermute | solution.py:344
  4.7 24.3 %collective-permute-start.4 = (bf16[512,256]{1,0:T(8,128)(2,1)}, bf16[512,256]{1,0:T(8,128)(2,1)S(1)}, u32[]{:S(2)}, u32[]{:S(2)}) collective-permute-start(bf16[512,256]{1,0:T(8,128)(2,1)} %x0.1), channel_id=1, source_target_pairs={{0,1},{1,0},{2,3},{3,2},{4,5},{5,4},{6,7},{7,6},{8,9},{9,8},{10,11... | collective-permute-start | bytes 786440 | tf_op jit(solution)/shard_map/ppermute | solution.py:345
  19.8 11.9 %collective-permute-start.3 = (bf16[512,256]{1,0:T(8,128)(2,1)}, bf16[512,256]{1,0:T(8,128)(2,1)S(1)}, u32[]{:S(2)}, u32[]{:S(2)}) collective-permute-start(bf16[512,256]{1,0:T(8,128)(2,1)} %collective-permute-done.2.x2), channel_id=1, source_target_pairs={{0,1},{1,0},{2,3},{3,2},{4,5},{5,4},{6,7},{7,6},{8,9},{9,8},{10,11... | collective-permute-start | bytes 786440 | tf_op jit(solution)/shard_map/ppermute | solution.py:346
  21.8 6.3 %copy-start = (bf16[2,512,256]{2,1,0:T(8,128)(2,1)S(1)}, bf16[2,512,256]{2,1,0:T(8,128)(2,1)}, u32[]{:S(2)}) copy-start(bf16[2,512,256]{2,1,0:T(8,128)(2,1)} %kv_ref.3) | copy-start | bytes 1572868
  21.8 7.2 %copy-start.1 = (bf16[512,256]{1,0:T(8,128)(2,1)S(1)}, bf16[512,256]{1,0:T(8,128)(2,1)}, u32[]{:S(2)}) copy-start(bf16[512,256]{1,0:T(8,128)(2,1)} %x0.1) | copy-start | bytes 786436
  31.7 44.0 %copy-start.3 = (f32[2,256]{1,0:T(2,128)S(1)}, f32[2,256]{1,0:T(2,128)}, u32[]{:S(2)}) copy-start(f32[2,256]{1,0:T(2,128)} %param.12) | copy-start | bytes 6148
  31.7 43.9 %copy-start.4 = (f32[2,256]{1,0:T(2,128)S(1)}, f32[2,256]{1,0:T(2,128)}, u32[]{:S(2)}) copy-start(f32[2,256]{1,0:T(2,128)} %param.11) | copy-start | bytes 6148
  34.2 68.7 %copy-start.2 = (bf16[512,256]{1,0:T(8,128)(2,1)S(1)}, bf16[512,256]{1,0:T(8,128)(2,1)}, u32[]{:S(2)}) copy-start(bf16[512,256]{1,0:T(8,128)(2,1)} %q_ref.1) | copy-start | bytes 786436
  34.2 31.1 %all-to-all-start = ((bf16[32,64,128]{2,1,0:T(8,128)(2,1)}), bf16[32,64,128]{2,1,0:T(8,128)(2,1)S(1)}, u32[]{:S(2)}, u32[]{:S(2)}) async-start(bf16[32,64,128]{2,1,0:T(8,128)(2,1)} %shard_map.77), calls=%async_computation | async-start | bytes 1048576 | tf_op jit(solution)/shard_map/all_to_all | solution.py:380
  69.5 9.7 %all-to-all-start.1 = ((f32[4,64,128]{2,1,0:T(8,128)}), f32[4,64,128]{2,1,0:T(8,128)S(1)}, u32[]{:S(2)}, u32[]{:S(2)}) async-start(f32[4,64,128]{2,1,0:T(8,128)} %shard_map.78), calls=%async_computation.1 | async-start | bytes 262144 | tf_op jit(solution)/shard_map/all_to_all | solution.py:398
  80.4 24.8 %all-to-all-start.2 = ((bf16[32,64,128]{2,1,0:T(8,128)(2,1)}), bf16[32,64,128]{2,1,0:T(8,128)(2,1)S(1)}, u32[]{:S(2)}, u32[]{:S(2)}) async-start(bf16[32,64,128]{2,1,0:T(8,128)(2,1)} %shard_map.79), calls=%async_computation.2 | async-start | bytes 1048576 | tf_op jit(solution)/shard_map/all_to_all | solution.py:407
  86.0 8.6 %collective-permute-start = (bf16[2,128,256]{2,1,0:T(8,128)(2,1)S(1)}, bf16[2,128,256]{2,1,0:T(8,128)(2,1)S(1)}, u32[]{:S(2)}, u32[]{:S(2)}) collective-permute-start(bf16[2,128,256]{2,1,0:T(8,128)(2,1)S(1)} %get-tuple-element.12), channel_id=1, source_target_pairs={{0,4},{4,8},{8,12},{12,16},{16,20},{20,24},{24,28},{28,32},{32,36}... | collective-permute-start | bytes 393224 | tf_op jit(solution)/shard_map/ppermute | solution.py:349
  91.2 11.7 %collective-permute-start.1 = (bf16[2,128,256]{2,1,0:T(8,128)(2,1)S(1)}, bf16[2,128,256]{2,1,0:T(8,128)(2,1)S(1)}, u32[]{:S(2)}, u32[]{:S(2)}) collective-permute-start(bf16[2,128,256]{2,1,0:T(8,128)(2,1)S(1)} %get-tuple-element.11), channel_id=1, source_target_pairs={{4,0},{8,4},{12,8},{16,12},{20,16},{24,20},{28,24},{32,28},{36,32}... | collective-permute-start | bytes 393224 | tf_op jit(solution)/shard_map/ppermute | solution.py:350

commit v6 on v5

--- a/solution.py
+++ b/solution.py
@@ -44,6 +44,10 @@
 
 def dot_nt(a, b):
     return lax.dot_general(a, b, (((1,), (1,)), ((), ())), preferred_element_type=f32)
+
+
+def dot_nn(a, b):
+    return jnp.dot(a, b, preferred_element_type=f32)
 
 
 def dot_tn(a, b):
@@ -207,53 +211,47 @@
             copy.wait()
 
 
-def combine_kernel(lines, ring, tokens, scal, in_ref, out_ref, tops, held):
+def combine_kernel(lines, ring, tokens, scal, in_ref, out_ref, tops, fine):
     senders = in_ref.shape[0]
-    split, line = scal[0], scal[1]
-    edge = lax.div(split, tokens)
-    has_edge = jnp.logical_and(
-        lax.rem(split, tokens) != 0, lax.rem(lax.div(edge, ring), lines) == line
-    )
-    slot = lax.div(edge, ring * lines) * ring + lax.rem(edge, ring)
-    slot = jnp.where(has_edge, slot, 0)
-    half = ROWS // 2
-    shape = (half, LANES)
+    slot = scal[1]
+    has_edge = scal[2] > 0
+    shape = (ROWS, LANES)
+    flat = (senders * ROWS, LANES)
+    row = lax.broadcasted_iota(jnp.int32, (LANES, LANES), 0)
+    pick_both = jnp.where((row == 0) | (row == DH), 1.0, 0.0).astype(bf16)
+    pick_first = jnp.where(row == 0, 1.0, 0.0).astype(bf16)
+    tops[...] = dot_nn(in_ref[:, :ROWS].reshape(flat), pick_both).reshape(tops.shape)
+    fine[...] = dot_nn(in_ref[:, ROWS:].reshape(flat), pick_first).reshape(fine.shape)
     low = jnp.full(shape, LOW, f32)
-    border = jnp.full(shape, split - line * (ring * tokens), jnp.int32)
+    border = jnp.full(shape, scal[0], jnp.int32)
+    starts = [((k // ring) * (ring * lines) + k % ring) * tokens for k in range(senders)]
+    extra = in_ref[slot, ROWS:]
+    extra_top = jnp.where(has_edge, dot_nn(extra, pick_both), low)
+    top0, full0, top1, full1 = low, low, extra_top, extra_top
+    for k in range(senders):
+        late = border <= starts[k]
+        is_edge = jnp.logical_and(border > starts[k], border < starts[k] + tokens)
+        top = tops[k]
+        full = top + jnp.where(is_edge, 0.0, fine[k])
+        top0 = jnp.maximum(top0, jnp.where(late, low, top))
+        full0 = jnp.maximum(full0, jnp.where(late, low, full))
+        top1 = jnp.maximum(top1, jnp.where(late, top, low))
+        full1 = jnp.maximum(full1, jnp.where(late, full, low))
+    n0 = jnp.zeros(shape, f32)
+    n1 = jnp.where(has_edge, extra.astype(f32) * jnp.exp(extra_top - top1), 0.0)
+    for k in range(senders):
+        late = border <= starts[k]
+        is_edge = jnp.logical_and(border > starts[k], border < starts[k] + tokens)
+        value = in_ref[k, :ROWS].astype(f32) + jnp.where(is_edge, 0.0, in_ref[k, ROWS:].astype(f32))
+        value = value * jnp.exp(tops[k] - jnp.where(late, top1, top0))
+        n0 = n0 + jnp.where(late, 0.0, value)
+        n1 = n1 + jnp.where(late, value, 0.0)
     lane = lanes_of(shape)
-    starts = [((k // ring) * (ring * lines) + k % ring) * tokens for k in range(senders)]
-    for part in range(2):
-        hi = slice(part * half, (part + 1) * half)
-        lo = slice(ROWS + part * half, ROWS + (part + 1) * half)
-        extra = in_ref[slot, lo].astype(f32)
-        extra_top = jnp.broadcast_to(extra[:, 0:1] + extra[:, DH : DH + 1], shape)
-        extra_top = jnp.where(has_edge, extra_top, low)
-        top0, full0, top1, full1 = low, low, extra_top, extra_top
-        for k in range(senders):
-            late = border <= starts[k]
-            is_edge = jnp.logical_and(border > starts[k], border < starts[k] + tokens)
-            first = in_ref[k, hi].astype(f32)
-            other = jnp.where(is_edge, 0.0, in_ref[k, lo].astype(f32))
-            top = jnp.broadcast_to(first[:, 0:1] + first[:, DH : DH + 1], shape)
-            full = top + jnp.broadcast_to(other[:, 0:1], shape)
-            tops[part, k] = top
-            held[part, k] = first + other
-            top0 = jnp.maximum(top0, jnp.where(late, low, top))
-            full0 = jnp.maximum(full0, jnp.where(late, low, full))
-            top1 = jnp.maximum(top1, jnp.where(late, top, low))
-            full1 = jnp.maximum(full1, jnp.where(late, full, low))
-        n0 = jnp.zeros(shape, f32)
-        n1 = jnp.where(has_edge, extra * jnp.exp(extra_top - top1), 0.0)
-        for k in range(senders):
-            late = border <= starts[k]
-            value = held[part, k] * jnp.exp(tops[part, k] - jnp.where(late, top1, top0))
-            n0 = n0 + jnp.where(late, 0.0, value)
-            n1 = n1 + jnp.where(late, value, 0.0)
-        n0 = jnp.where(lane == 0, top0, jnp.where(lane == DH, full0, n0))
-        n1 = jnp.where(lane == 0, top1, jnp.where(lane == DH, full1, n1))
-        for line_at in range(lines):
-            out_ref[line_at, hi] = n0
-            out_ref[line_at, lo] = n1
+    n0 = jnp.where(lane == 0, top0, jnp.where(lane == DH, full0, n0))
+    n1 = jnp.where(lane == 0, top1, jnp.where(lane == DH, full1, n1))
+    for at in range(lines):
+        out_ref[at, :ROWS] = n0
+        out_ref[at, ROWS:] = n1
 
 
 def norm_kernel(in_ref, gain_ref, bias_ref, out_ref):
@@ -339,7 +337,11 @@
     slot = lax.axis_index(RING)
     lines = lax.axis_size(LINE)
     slots_held = lax.axis_size(RING)
-    scal2 = jnp.stack([split, line]).astype(jnp.int32)
+    ring = lax.axis_size("x")
+    edge = split // tokens
+    has_edge = (split % tokens != 0) & ((edge // ring) % lines == line)
+    edge_slot = jnp.where(has_edge, edge // (ring * lines) * ring + edge % ring, 0)
+    scal2 = jnp.stack([split - line * (ring * tokens), edge_slot, has_edge]).astype(jnp.int32)
 
     x2 = lax.ppermute(inputs, "yh", SWAP)
     x1 = lax.ppermute(inputs, "c", SWAP)
@@ -393,7 +395,7 @@
         functools.partial(combine_kernel, lines, lax.axis_size("x"), tokens),
         jax.ShapeDtypeStruct((lines, 2 * ROWS, LANES), f32),
         1, 8, 0, 1 << 20, 1 << 17,
-        scratch=[pltpu.VMEM((2, slots_held, ROWS // 2, LANES), f32)] * 2,
+        scratch=[pltpu.VMEM((slots_held, ROWS, LANES), f32)] * 2,
     )(scal2, arrived)
     shared = lax.all_to_all(held, LINE, 0, 0, tiled=True)
     head = lax.div(slot * ROWS, R)

time: 108 us -> 105 us (0.972)
  Pallas kernels: 15.6 us -> 13.2 us
    pallas_call x1, Pallas kernels: 4.2 us -> 1.76 us  [on_device(): call(functools.partial(combine_kernel, lines, lax.axis_size('x'), tokens)...]
  transfers between devices with their start and end apart: 8 -> 8, of which waited for: 5 -> 5; matrix products, arithmetic and copies ran while one was open for 4% -> 4% of each run, Pallas kernels for 5% -> 6%
where the time goes in v6:
time: 105 us
  waiting for transfers between devices  43.5 us (41%)
  starting transfers between devices  41 us (39%)
  Pallas kernels  13.2 us (13%)
  local copies, waits for them, and re-layouts  4.62 us (4%)
  between operations  2.21 us (2%)
    all_to_all x1, waiting for transfers between devices, on_device(): arrived = lax.all_to_all(sent, RING, 0, 0, tiled=True)  17.3 us
    all_to_all x1, starting transfers between devices, on_device(): arrived = lax.all_to_all(sent, RING, 0, 0, tiled=True)  13.6 us
    ppermute x1, waiting for transfers between devices, on_device(): x2 = lax.ppermute(inputs, 'yh', SWAP)  13.2 us
    ppermute x1, waiting for transfers between devices, on_device(): after = lax.ppermute(keys_values[:, :W], SEQ, down)  8.34 us
    all_to_all x1, starting transfers between devices, on_device(): shared = lax.all_to_all(held, LINE, 0, 0, tiled=True)  6.19 us
    all_to_all x1, starting transfers between devices, on_device(): table = lax.all_to_all(chunk, RING, 0, 0, tiled=True)  5.56 us
    ppermute x1, starting transfers between devices, on_device(): before = lax.ppermute(keys_values[:, tokens - W:], SEQ, up)  5.21 us
    ppermute x1, starting transfers between devices, on_device(): x2 = lax.ppermute(inputs, 'yh', SWAP)  4.7 us
  transfers between devices with their start and end apart: 8, of which 5 were waited for; matrix products, arithmetic and copies ran while one was open for 4% of the time, Pallas kernels for 6%

profile of v6, /device:TPU:62, one launch (start us, length us, event | category | flops | bytes accessed | tf_op | source)
XLA Modules:
  0.0 104.6 jit_solution(10004424983498363059)
XLA Ops:
  0.0 4.7 %collective-permute-start.2 = (bf16[512,256]{1,0:T(8,128)(2,1)}, bf16[512,256]{1,0:T(8,128)(2,1)}, u32[]{:S(2)}, u32[]{:S(2)}) collective-permute-start(bf16[512,256]{1,0:T(8,128)(2,1)} %x0.1), channel_id=1, source_target_pairs={{0,2},{2,0},{1,3},{3,1},{4,6},{6,4},{5,7},{7,5},{8,10},{10,8},{9,1... | collective-permute-start | bytes 786440 | tf_op jit(solution)/shard_map/ppermute | solution.py:346
  4.7 1.9 %collective-permute-start.4 = (bf16[512,256]{1,0:T(8,128)(2,1)}, bf16[512,256]{1,0:T(8,128)(2,1)S(1)}, u32[]{:S(2)}, u32[]{:S(2)}) collective-permute-start(bf16[512,256]{1,0:T(8,128)(2,1)} %x0.1), channel_id=1, source_target_pairs={{0,1},{1,0},{2,3},{3,2},{4,5},{5,4},{6,7},{7,6},{8,9},{9,8},{10,11... | collective-permute-start | bytes 786440 | tf_op jit(solution)/shard_map/ppermute | solution.py:347
  6.6 13.2 %collective-permute-done.2.x2 = bf16[512,256]{1,0:T(8,128)(2,1)} collective-permute-done((bf16[512,256]{1,0:T(8,128)(2,1)}, bf16[512,256]{1,0:T(8,128)(2,1)}, u32[]{:S(2)}, u32[]{:S(2)}) %collective-permute-start.2) | collective-permute-done | bytes 262176 | tf_op jit(solution)/shard_map/ppermute | solution.py:346
  19.8 1.9 %collective-permute-start.3 = (bf16[512,256]{1,0:T(8,128)(2,1)}, bf16[512,256]{1,0:T(8,128)(2,1)S(1)}, u32[]{:S(2)}, u32[]{:S(2)}) collective-permute-start(bf16[512,256]{1,0:T(8,128)(2,1)} %collective-permute-done.2.x2), channel_id=1, source_target_pairs={{0,1},{1,0},{2,3},{3,2},{4,5},{5,4},{6,7},{7,6},{8,9},{9,8},{10,11... | collective-permute-start | bytes 786440 | tf_op jit(solution)/shard_map/ppermute | solution.py:348
  21.8 0.0 copy-start
  21.8 0.0 copy-start.1
  21.8 2.9 %copy.8 = bf16[4,256,1024]{1,2,0:T(8,128)(2,1)S(1)} copy(bf16[4,256,1024]{2,1,0:T(8,128)(2,1)} %bitcast.16) | data formatting | bytes 4194304 | tf_op jit(solution)/shard_map/reshape | solution.py:354
  24.7 1.3 %fusion.1 = (s32[1,1]{1,0:T(1,128)}, s32[1,1]{1,0:T(1,128)}) fusion(s32[2,512]{1,0:T(2,128)} %param.13), kind=kLoop, calls=%fused_computation.4 | loop fusion | bytes 16 | tf_op jit(solution)/shard_map/slice | solution.py:322
  27.9 0.1 stack.42.scal
  28.0 0.0 copy-done
  28.0 0.9 shard_map.76.kvh_ref
  29.0 0.0 collective-permute-done.4.x1
  29.0 0.0 copy-done.1
  29.0 1.3 %shard_map.74.acc_ref = f32[1024,512]{1,0:T(8,128)S(1)} custom-call(s32[7]{0:T(128)S(1)} %stack.42.scal, bf16[512,256]{1,0:T(8,128)(2,1)S(1)} %copy-done.1, bf16[512,256]{1,0:T(8,128)(2,1)S(1)} %collective-permute-done.4.x1, bf16[4,1024,256]{2,1,0:T(8,128)(2,1)S(1)} %bitcast.13), custom_call_target="tpu_custom_call" | custom-call | flops 536870912 | bytes 5242880 | tf_op jit(solution)/shard_map/pallas_call | solution.py:364
  30.3 1.4 %shard_map.75.acc_ref = f32[1024,512]{1,0:T(8,128)S(1)} custom-call(s32[7]{0:T(128)S(1)} %stack.42.scal, bf16[512,256]{1,0:T(8,128)(2,1)} %collective-permute-done.2.x2, bf16[4,1024,256]{2,1,0:T(8,128)(2,1)S(1)} %bitcast.14, f32[1024,512]{1,0:T(8,128)S(1)} %shard_map.74.acc_ref), custom_call_target="tpu_custom_call" | custom-call | flops 268435456 | bytes 6291456 | tf_op jit(solution)/shard_map/pallas_call | solution.py:367
  31.7 0.0 collective-permute-done.3.x3
  31.7 2.5 %shard_map.77 = bf16[32,64,128]{2,1,0:T(8,128)(2,1)} custom-call(s32[7]{0:T(128)S(1)} %stack.42.scal, bf16[512,256]{1,0:T(8,128)(2,1)S(1)} %collective-permute-done.3.x3, bf16[4,1024,256]{2,1,0:T(8,128)(2,1)S(1)} %bitcast.15, f32[1024,512]{1,0:T(8,128)S(1)} %shard_map.75.acc_ref, bf16[4,512,256]{2,1,0:T(8,128)(2,1)S(1)} %shard_map.76.kvh_ref), custom_call_target="tpu_custom_call" | custom-call | flops 536870912 | bytes 5242880 | tf_op jit(solution)/shard_map/pallas_call | solution.py:368
  34.2 0.0 copy-start.3
  34.2 0.0 copy-start.4
  34.2 0.0 copy-start.2
  34.3 13.6 %all-to-all-start = ((bf16[32,64,128]{2,1,0:T(8,128)(2,1)}), bf16[32,64,128]{2,1,0:T(8,128)(2,1)S(1)}, u32[]{:S(2)}, u32[]{:S(2)}) async-start(bf16[32,64,128]{2,1,0:T(8,128)(2,1)} %shard_map.77), calls=%async_computation | async-start | bytes 1048576 | tf_op jit(solution)/shard_map/all_to_all | solution.py:382
  47.9 0.1 pad_add_fusion.scal
  48.0 17.3 %all-to-all-done.in_ref = bf16[32,64,128]{2,1,0:T(8,128)(2,1)S(1)} async-done(((bf16[32,64,128]{2,1,0:T(8,128)(2,1)}), bf16[32,64,128]{2,1,0:T(8,128)(2,1)S(1)}, u32[]{:S(2)}, u32[]{:S(2)}) %all-to-all-start) | async-done | bytes 524320 | tf_op jit(solution)/shard_map/all_to_all | solution.py:382
  65.3 1.8 %shard_map.78 = f32[4,64,128]{2,1,0:T(8,128)} custom-call(s32[3]{0:T(128)S(1)} %pad_add_fusion.scal, bf16[32,64,128]{2,1,0:T(8,128)(2,1)S(1)} %all-to-all-done.in_ref), custom_call_target="tpu_custom_call" | custom-call | bytes 1048576 | tf_op jit(solution)/shard_map/pallas_call | solution.py:394
  67.1 6.2 %all-to-all-start.1 = ((f32[4,64,128]{2,1,0:T(8,128)}), f32[4,64,128]{2,1,0:T(8,128)S(1)}, u32[]{:S(2)}, u32[]{:S(2)}) async-start(f32[4,64,128]{2,1,0:T(8,128)} %shard_map.78), calls=%async_computation.1 | async-start | bytes 262144 | tf_op jit(solution)/shard_map/all_to_all | solution.py:400
  73.3 0.0 copy-done.3
  73.3 0.0 copy-done.4
  73.3 0.1 constant_dynamic-slice_fusion
  73.3 0.1 reshape.10.gain_ref
  73.4 0.1 reshape.11.bias_ref
  73.5 3.3 %all-to-all-done.1.in_ref = f32[4,64,128]{2,1,0:T(8,128)S(1)} async-done(((f32[4,64,128]{2,1,0:T(8,128)}), f32[4,64,128]{2,1,0:T(8,128)S(1)}, u32[]{:S(2)}, u32[]{:S(2)}) %all-to-all-start.1) | async-done | bytes 131104 | tf_op jit(solution)/shard_map/all_to_all | solution.py:400
  76.8 1.2 %shard_map.79 = bf16[32,64,128]{2,1,0:T(8,128)(2,1)} custom-call(f32[4,64,128]{2,1,0:T(8,128)S(1)} %all-to-all-done.1.in_ref, f32[1,128]{1,0:T(1,128)S(1)} %reshape.10.gain_ref, f32[1,128]{1,0:T(1,128)S(1)} %reshape.11.bias_ref), custom_call_target="tpu_custom_call" | custom-call | bytes 1048576 | tf_op jit(solution)/shard_map/pallas_call | solution.py:404
  78.0 5.6 %all-to-all-start.2 = ((bf16[32,64,128]{2,1,0:T(8,128)(2,1)}), bf16[32,64,128]{2,1,0:T(8,128)(2,1)S(1)}, u32[]{:S(2)}, u32[]{:S(2)}) async-start(bf16[32,64,128]{2,1,0:T(8,128)(2,1)} %shard_map.79), calls=%async_computation.2 | async-start | bytes 1048576 | tf_op jit(solution)/shard_map/all_to_all | solution.py:409
  83.6 5.2 %collective-permute-start = (bf16[2,128,256]{2,1,0:T(8,128)(2,1)S(1)}, bf16[2,128,256]{2,1,0:T(8,128)(2,1)S(1)}, u32[]{:S(2)}, u32[]{:S(2)}) collective-permute-start(bf16[2,128,256]{2,1,0:T(8,128)(2,1)S(1)} %get-tuple-element.12), channel_id=1, source_target_pairs={{0,4},{4,8},{8,12},{12,16},{16,20},{20,24},{24,28},{28,32},{32,36}... | collective-permute-start | bytes 393224 | tf_op jit(solution)/shard_map/ppermute | solution.py:351
  88.8 1.9 %collective-permute-start.1 = (bf16[2,128,256]{2,1,0:T(8,128)(2,1)S(1)}, bf16[2,128,256]{2,1,0:T(8,128)(2,1)S(1)}, u32[]{:S(2)}, u32[]{:S(2)}) collective-permute-start(bf16[2,128,256]{2,1,0:T(8,128)(2,1)S(1)} %get-tuple-element.11), channel_id=1, source_target_pairs={{4,0},{8,4},{12,8},{16,12},{20,16},{24,20},{28,24},{32,28},{36,32}... | collective-permute-start | bytes 393224 | tf_op jit(solution)/shard_map/ppermute | solution.py:352
  90.8 1.4 %collective-permute-done.before_ref = bf16[2,128,256]{2,1,0:T(8,128)(2,1)S(1)} collective-permute-done((bf16[2,128,256]{2,1,0:T(8,128)(2,1)S(1)}, bf16[2,128,256]{2,1,0:T(8,128)(2,1)S(1)}, u32[]{:S(2)}, u32[]{:S(2)}) %collective-permute-start) | collective-permute-done | bytes 131104 | tf_op jit(solution)/shard_map/ppermute | solution.py:351
  92.2 8.3 %collective-permute-done.1.after_ref = bf16[2,128,256]{2,1,0:T(8,128)(2,1)S(1)} collective-permute-done((bf16[2,128,256]{2,1,0:T(8,128)(2,1)S(1)}, bf16[2,128,256]{2,1,0:T(8,128)(2,1)S(1)}, u32[]{:S(2)}, u32[]{:S(2)}) %collective-permute-start.1) | collective-permute-done | bytes 131104 | tf_op jit(solution)/shard_map/ppermute | solution.py:352
  100.5 0.0 copy-done.2
  100.5 2.3 %shard_map.73 = (f32[256,512]{1,0:T(8,128)S(1)}, f32[16,512]{1,0:T(8,128)S(1)}, bf16[4,512,128]{2,1,0:T(8,128)(2,1)S(1)}) custom-call(s32[7]{0:T(128)S(1)} %stack.42.scal, bf16[512,256]{1,0:T(8,128)(2,1)S(1)} %copy-done.2, bf16[2,512,256]{2,1,0:T(8,128)(2,1)S(1)} %copy-done, bf16[2,128,256]{2,1,0:T(8,128)(2,1)S(1)} %collective-permute-done.before_ref, ...), custom_call_target="tpu_custom_call" | custom-call | flops 402653184 | bytes 2097152 | tf_op jit(solution)/shard_map/pallas_call | solution.py:384
  102.8 0.0 all-to-all-done.2.tab_ref
  102.8 1.9 %shard_map.80 = bf16[512,256]{1,0:T(8,128)(2,1)} custom-call(bf16[4,512,128]{2,1,0:T(8,128)(2,1)S(1)} %get-tuple-element.8.q2_ref, bf16[32,64,128]{2,1,0:T(8,128)(2,1)S(1)} %all-to-all-done.2.tab_ref, f32[256,512]{1,0:T(8,128)S(1)} %get-tuple-element.9.o_ref, f32[16,512]{1,0:T(8,128)S(1)} %get-tuple-element.10.stat_ref), custom_call_target="tpu_custom_call" | custom-call | flops 268435456 | bytes 2097152 | tf_op jit(solution)/shard_map/pallas_call | solution.py:411
  (1 shorter events, 0.0 us)
Async XLA Ops:
  0.0 19.8 %collective-permute-start.2 = (bf16[512,256]{1,0:T(8,128)(2,1)}, bf16[512,256]{1,0:T(8,128)(2,1)}, u32[]{:S(2)}, u32[]{:S(2)}) collective-permute-start(bf16[512,256]{1,0:T(8,128)(2,1)} %x0.1), channel_id=1, source_target_pairs={{0,2},{2,0},{1,3},{3,1},{4,6},{6,4},{5,7},{7,5},{8,10},{10,8},{9,1... | collective-permute-start | bytes 786440 | tf_op jit(solution)/shard_map/ppermute | solution.py:346
  4.7 24.3 %collective-permute-start.4 = (bf16[512,256]{1,0:T(8,128)(2,1)}, bf16[512,256]{1,0:T(8,128)(2,1)S(1)}, u32[]{:S(2)}, u32[]{:S(2)}) collective-permute-start(bf16[512,256]{1,0:T(8,128)(2,1)} %x0.1), channel_id=1, source_target_pairs={{0,1},{1,0},{2,3},{3,2},{4,5},{5,4},{6,7},{7,6},{8,9},{9,8},{10,11... | collective-permute-start | bytes 786440 | tf_op jit(solution)/shard_map/ppermute | solution.py:347
  19.8 11.9 %collective-permute-start.3 = (bf16[512,256]{1,0:T(8,128)(2,1)}, bf16[512,256]{1,0:T(8,128)(2,1)S(1)}, u32[]{:S(2)}, u32[]{:S(2)}) collective-permute-start(bf16[512,256]{1,0:T(8,128)(2,1)} %collective-permute-done.2.x2), channel_id=1, source_target_pairs={{0,1},{1,0},{2,3},{3,2},{4,5},{5,4},{6,7},{7,6},{8,9},{9,8},{10,11... | collective-permute-start | bytes 786440 | tf_op jit(solution)/shard_map/ppermute | solution.py:348
  21.8 6.3 %copy-start = (bf16[2,512,256]{2,1,0:T(8,128)(2,1)S(1)}, bf16[2,512,256]{2,1,0:T(8,128)(2,1)}, u32[]{:S(2)}) copy-start(bf16[2,512,256]{2,1,0:T(8,128)(2,1)} %kv_ref.3) | copy-start | bytes 1572868
  21.8 7.2 %copy-start.1 = (bf16[512,256]{1,0:T(8,128)(2,1)S(1)}, bf16[512,256]{1,0:T(8,128)(2,1)}, u32[]{:S(2)}) copy-start(bf16[512,256]{1,0:T(8,128)(2,1)} %x0.1) | copy-start | bytes 786436
  34.2 39.1 %copy-start.3 = (f32[2,256]{1,0:T(2,128)S(1)}, f32[2,256]{1,0:T(2,128)}, u32[]{:S(2)}) copy-start(f32[2,256]{1,0:T(2,128)} %param.12) | copy-start | bytes 6148
  34.2 39.0 %copy-start.4 = (f32[2,256]{1,0:T(2,128)S(1)}, f32[2,256]{1,0:T(2,128)}, u32[]{:S(2)}) copy-start(f32[2,256]{1,0:T(2,128)} %param.11) | copy-start | bytes 6148
  34.2 66.3 %copy-start.2 = (bf16[512,256]{1,0:T(8,128)(2,1)S(1)}, bf16[512,256]{1,0:T(8,128)(2,1)}, u32[]{:S(2)}) copy-start(bf16[512,256]{1,0:T(8,128)(2,1)} %q_ref.1) | copy-start | bytes 786436
  34.3 31.1 %all-to-all-start = ((bf16[32,64,128]{2,1,0:T(8,128)(2,1)}), bf16[32,64,128]{2,1,0:T(8,128)(2,1)S(1)}, u32[]{:S(2)}, u32[]{:S(2)}) async-start(bf16[32,64,128]{2,1,0:T(8,128)(2,1)} %shard_map.77), calls=%async_computation | async-start | bytes 1048576 | tf_op jit(solution)/shard_map/all_to_all | solution.py:382
  67.1 9.7 %all-to-all-start.1 = ((f32[4,64,128]{2,1,0:T(8,128)}), f32[4,64,128]{2,1,0:T(8,128)S(1)}, u32[]{:S(2)}, u32[]{:S(2)}) async-start(f32[4,64,128]{2,1,0:T(8,128)} %shard_map.78), calls=%async_computation.1 | async-start | bytes 262144 | tf_op jit(solution)/shard_map/all_to_all | solution.py:400
  78.0 24.8 %all-to-all-start.2 = ((bf16[32,64,128]{2,1,0:T(8,128)(2,1)}), bf16[32,64,128]{2,1,0:T(8,128)(2,1)S(1)}, u32[]{:S(2)}, u32[]{:S(2)}) async-start(bf16[32,64,128]{2,1,0:T(8,128)(2,1)} %shard_map.79), calls=%async_computation.2 | async-start | bytes 1048576 | tf_op jit(solution)/shard_map/all_to_all | solution.py:409
  83.6 8.6 %collective-permute-start = (bf16[2,128,256]{2,1,0:T(8,128)(2,1)S(1)}, bf16[2,128,256]{2,1,0:T(8,128)(2,1)S(1)}, u32[]{:S(2)}, u32[]{:S(2)}) collective-permute-start(bf16[2,128,256]{2,1,0:T(8,128)(2,1)S(1)} %get-tuple-element.12), channel_id=1, source_target_pairs={{0,4},{4,8},{8,12},{12,16},{16,20},{20,24},{24,28},{28,32},{32,36}... | collective-permute-start | bytes 393224 | tf_op jit(solution)/shard_map/ppermute | solution.py:351
  88.8 11.7 %collective-permute-start.1 = (bf16[2,128,256]{2,1,0:T(8,128)(2,1)S(1)}, bf16[2,128,256]{2,1,0:T(8,128)(2,1)S(1)}, u32[]{:S(2)}, u32[]{:S(2)}) collective-permute-start(bf16[2,128,256]{2,1,0:T(8,128)(2,1)S(1)} %get-tuple-element.11), channel_id=1, source_target_pairs={{4,0},{8,4},{12,8},{16,12},{20,16},{24,20},{28,24},{32,28},{36,32}... | collective-permute-start | bytes 393224 | tf_op jit(solution)/shard_map/ppermute | solution.py:352

commit v7 on v6

--- a/solution.py
+++ b/solution.py
@@ -14,9 +14,9 @@
 W = 128
 HEADS = 4
 LANES = 128
-ROWS = 32
-RING = ("z", "x")
-LINE = "yl"
+GROUP = 4
+GATHER = (("z", "yl"),)
+SHARE = ("x",)
 SEQ = ("z", "yl", "x")
 DOC = ("yh", "c")
 EPS = 1e-05
@@ -143,7 +143,7 @@
     out_ref[...] = acc_ref[...] + dot_nt(wt_ref[scal[5]], x2[...])
 
 
-def project_kernel(scal, x3, wt_ref, acc_ref, kvh_ref, out_ref, held, sems):
+def project_kernel(group, count, scal, x3, wt_ref, acc_ref, kvh_ref, out_ref, held, sems):
     tokens = x3.shape[0]
     local = scal[0]
     mixed = jnp.logical_and(local > 0, local < tokens)
@@ -151,22 +151,23 @@
     at_a = lane == 0
     at_b = lane == DH
     left = lane < DH
-    parts = R // ROWS
-
-    def logits_of(h):
-        rows = slice(h * R, (h + 1) * R)
+    parts = R // count
+
+    def logits_of(i):
+        at = (group * GROUP + i) * R
+        rows = slice(at, at + R)
         return acc_ref[rows, :] + dot_nt(wt_ref[scal[6], rows, :], x3[...])
 
     def from_first(n):
         return n - jnp.where(left, n[:, 0:1], n[:, DH : DH + 1])
 
-    def put(h, hi, rest):
+    def put(i, hi, rest):
         packed = jnp.concatenate(
-            [hi.reshape(parts, ROWS, LANES), rest.reshape(parts, ROWS, LANES)], axis=1
+            [hi.reshape(parts, count, LANES), rest.reshape(parts, count, LANES)], axis=1
         )
-        held[h] = packed.astype(bf16)
+        held[i] = packed.astype(bf16)
         copy = pltpu.make_async_copy(
-            held.at[h], out_ref.at[pl.ds(h * parts, parts)], sems.at[h]
+            held.at[i], out_ref.at[pl.ds(i * parts, parts)], sems.at[i]
         )
         copy.start()
         return copy
@@ -176,19 +177,18 @@
         side = pl.multiple_of(jnp.where(local <= 0, LANES, 0), LANES)
         copies = []
         after = logits_of(0)
-        for h in range(HEADS):
+        for i in range(GROUP):
+            h = group * GROUP + i
             logits = after
-            if h + 1 < HEADS:
-                after = logits_of(h + 1)
+            if i + 1 < GROUP:
+                after = logits_of(i + 1)
             a, b, c = pieces_of(jnp.max(logits, axis=1, keepdims=True))
             proj = jnp.exp(logits - (a + b)).astype(bf16)
-            n = from_first(
-                jnp.dot(proj, kvh_ref[h, :, pl.ds(side, LANES)], preferred_element_type=f32)
-            )
+            n = from_first(dot_nn(proj, kvh_ref[h, :, pl.ds(side, LANES)]))
             hi = n.astype(bf16).astype(f32)
             rest = jnp.where(at_a, c, jnp.where(at_b, 0.0, n - hi))
             hi = jnp.where(at_a, a, jnp.where(at_b, b, hi))
-            copies.append(put(h, hi, rest))
+            copies.append(put(i, hi, rest))
         for copy in copies:
             copy.wait()
 
@@ -196,36 +196,36 @@
     def _():
         second = lax.broadcasted_iota(jnp.int32, (R, tokens), 1) >= local
         copies = []
-        for h in range(HEADS):
-            logits = logits_of(h)
+        for i in range(GROUP):
+            h = group * GROUP + i
+            logits = logits_of(i)
             a0, b0, _ = pieces_of(jnp.max(jnp.where(second, LOW, logits), axis=1, keepdims=True))
             a1, b1, _ = pieces_of(jnp.max(jnp.where(second, logits, LOW), axis=1, keepdims=True))
             proj = jnp.exp(logits - jnp.where(second, a1 + b1, a0 + b0)).astype(bf16)
-            sums = jnp.dot(proj, kvh_ref[h], preferred_element_type=f32)
+            sums = dot_nn(proj, kvh_ref[h])
             n0 = from_first(sums[:, :LANES])
             n1 = from_first(sums[:, LANES:])
             n0 = jnp.where(at_a, a0, jnp.where(at_b, b0, n0))
             n1 = jnp.where(at_a, a1, jnp.where(at_b, b1, n1))
-            copies.append(put(h, n0, n1))
+            copies.append(put(i, n0, n1))
         for copy in copies:
             copy.wait()
 
 
-def combine_kernel(lines, ring, tokens, scal, in_ref, out_ref, tops, fine):
+def combine_kernel(starts, tokens, count, scal, in_ref, out_ref, tops, fine):
     senders = in_ref.shape[0]
     slot = scal[1]
     has_edge = scal[2] > 0
-    shape = (ROWS, LANES)
-    flat = (senders * ROWS, LANES)
+    shape = (count, LANES)
+    flat = (senders * count, LANES)
     row = lax.broadcasted_iota(jnp.int32, (LANES, LANES), 0)
     pick_both = jnp.where((row == 0) | (row == DH), 1.0, 0.0).astype(bf16)
     pick_first = jnp.where(row == 0, 1.0, 0.0).astype(bf16)
-    tops[...] = dot_nn(in_ref[:, :ROWS].reshape(flat), pick_both).reshape(tops.shape)
-    fine[...] = dot_nn(in_ref[:, ROWS:].reshape(flat), pick_first).reshape(fine.shape)
+    tops[...] = dot_nn(in_ref[:, :count].reshape(flat), pick_both).reshape(tops.shape)
+    fine[...] = dot_nn(in_ref[:, count:].reshape(flat), pick_first).reshape(fine.shape)
     low = jnp.full(shape, LOW, f32)
     border = jnp.full(shape, scal[0], jnp.int32)
-    starts = [((k // ring) * (ring * lines) + k % ring) * tokens for k in range(senders)]
-    extra = in_ref[slot, ROWS:]
+    extra = in_ref[slot, count:]
     extra_top = jnp.where(has_edge, dot_nn(extra, pick_both), low)
     top0, full0, top1, full1 = low, low, extra_top, extra_top
     for k in range(senders):
@@ -242,25 +242,26 @@
     for k in range(senders):
         late = border <= starts[k]
         is_edge = jnp.logical_and(border > starts[k], border < starts[k] + tokens)
-        value = in_ref[k, :ROWS].astype(f32) + jnp.where(is_edge, 0.0, in_ref[k, ROWS:].astype(f32))
+        value = in_ref[k, :count].astype(f32) + jnp.where(is_edge, 0.0, in_ref[k, count:].astype(f32))
         value = value * jnp.exp(tops[k] - jnp.where(late, top1, top0))
         n0 = n0 + jnp.where(late, 0.0, value)
         n1 = n1 + jnp.where(late, value, 0.0)
     lane = lanes_of(shape)
     n0 = jnp.where(lane == 0, top0, jnp.where(lane == DH, full0, n0))
     n1 = jnp.where(lane == 0, top1, jnp.where(lane == DH, full1, n1))
-    for at in range(lines):
-        out_ref[at, :ROWS] = n0
-        out_ref[at, ROWS:] = n1
+    for at in range(out_ref.shape[0]):
+        out_ref[at, :count] = n0
+        out_ref[at, count:] = n1
 
 
 def norm_kernel(in_ref, gain_ref, bias_ref, out_ref):
+    count = in_ref.shape[1] // 2
     got = in_ref[...]
     top = jnp.broadcast_to(got[:, :, 0:1], got.shape)
     whole = jnp.max(top, axis=0)
     full = jnp.max(jnp.broadcast_to(got[:, :, DH : DH + 1], got.shape), axis=0)
     n = jnp.sum(got * jnp.exp(top - whole[None]), axis=0)
-    lane = lanes_of((2 * ROWS, LANES))
+    lane = lanes_of((2 * count, LANES))
     left = lane < DH
     used = jnp.logical_and(lane != 0, lane != DH)
 
@@ -274,45 +275,51 @@
     variance = halves(centred * centred)
     scale = jnp.exp(2.0 * (full - whole))
     table = centred * lax.rsqrt(variance + EPS * scale) * gain_ref[...] + bias_ref[...]
-    t0, t1 = table[:ROWS], table[ROWS:]
-    left = left[:ROWS]
+    t0, t1 = table[:count], table[count:]
+    left = left[:count]
     keys = jnp.where(left, t0, pltpu.roll(t1, DH, 1))
     values = jnp.where(left, pltpu.roll(t0, DH, 1), t1)
     chunk = jnp.concatenate([keys, values], axis=0).astype(bf16)[None]
     out_ref[...] = jnp.broadcast_to(chunk, out_ref.shape)
 
 
-def far_kernel(q2_ref, tab_ref, o_ref, stat_ref, out_ref):
-    parts = R // ROWS
+def far_kernel(group, q2_ref, tab_ref, o_ref, stat_ref, *rest):
+    out_ref = rest[-1]
+    count = tab_ref.shape[1] // 2
+    parts = R // count
     second = stat_ref[HEADS : HEADS + 1, :] > 0.5
-
-    def rows_of(h, part):
-        return tab_ref[h * parts : (h + 1) * parts, part * ROWS : (part + 1) * ROWS].reshape(R, LANES)
-
-    def scores_of(h):
-        return dot_nt(rows_of(h, 0), q2_ref[h])
+    for i, done in enumerate(rest[:-1]):
+        out_ref[:, i * LANES : (i + 1) * LANES] = done[...]
+
+    def rows_of(i, part):
+        return tab_ref[
+            i * parts : (i + 1) * parts, part * count : (part + 1) * count
+        ].reshape(R, LANES)
+
+    def scores_of(i):
+        return dot_nt(rows_of(i, 0), q2_ref[group * GROUP + i])
 
     after = scores_of(0)
     outs = []
-    for h in range(HEADS):
+    for i in range(GROUP):
+        h = group * GROUP + i
         scores = after
-        if h + 1 < HEADS:
-            after = scores_of(h + 1)
+        if i + 1 < GROUP:
+            after = scores_of(i + 1)
         near_top = stat_ref[h : h + 1, :]
         near_total = stat_ref[2 * HEADS + h : 2 * HEADS + h + 1, :]
         top = jnp.maximum(jnp.max(scores, axis=0, keepdims=True), near_top)
         weight = jnp.exp(scores - top)
         scale = jnp.exp(near_top - top)
         total = jnp.sum(weight, axis=0, keepdims=True) + near_total * scale
-        far = dot_tn(rows_of(h, 1), weight.astype(bf16))
+        far = dot_tn(rows_of(i, 1), weight.astype(bf16))
         far = jnp.where(second, far[DH:], far[:DH])
         share = 1.0 / total
         outs.append(o_ref[h * DH : (h + 1) * DH] * (scale * share) + far * share)
-        if h % 2 == 1:
-            both = jnp.concatenate(outs, axis=0)
-            outs = []
-            at = (h // 2) * LANES
-            out_ref[:, at : at + LANES] = jnp.transpose(both).astype(bf16)
+    for pair in range(GROUP // 2):
+        both = jnp.concatenate(outs[2 * pair : 2 * pair + 2], axis=0)
+        at = (len(rest) - 1) * GROUP * DH + pair * LANES
+        out_ref[:, at : at + LANES] = jnp.transpose(both).astype(bf16)
 
 
 def on_device(inputs, queries, keys_values, slot_weight, slot_gain, slot_bias, bounds):
@@ -333,16 +340,6 @@
             (1 - yh) * 2 + 1 - c,
         ]
     ).astype(jnp.int32)
-    line = lax.axis_index(LINE)
-    slot = lax.axis_index(RING)
-    lines = lax.axis_size(LINE)
-    slots_held = lax.axis_size(RING)
-    ring = lax.axis_size("x")
-    edge = split // tokens
-    has_edge = (split % tokens != 0) & ((edge // ring) % lines == line)
-    edge_slot = jnp.where(has_edge, edge // (ring * lines) * ring + edge % ring, 0)
-    scal2 = jnp.stack([split - line * (ring * tokens), edge_slot, has_edge]).astype(jnp.int32)
-
     x2 = lax.ppermute(inputs, "yh", SWAP)
     x1 = lax.ppermute(inputs, "c", SWAP)
     x3 = lax.ppermute(x2, "c", SWAP)
@@ -365,21 +362,25 @@
         scal, inputs, x1, weight_t
     )
     acc = call(more_kernel, acc_shape, 3, 16, flops, 6 << 20)(scal, x2, weight_t, acc)
-    sent = pl.pallas_call(
-        project_kernel,
-        out_shape=jax.ShapeDtypeStruct((slots_held, 2 * ROWS, LANES), bf16),
-        in_specs=[SMEM] + [VMEM] * 4,
-        out_specs=pl.BlockSpec(memory_space=pltpu.HBM),
-        scratch_shapes=[
-            pltpu.VMEM((HEADS, R // ROWS, 2 * ROWS, LANES), bf16),
-            pltpu.SemaphoreType.DMA((HEADS,)),
-        ],
-        compiler_params=pltpu.CompilerParams(vmem_limit_bytes=24 << 20),
-        cost_estimate=pl.CostEstimate(
-            flops=2 * flops, bytes_accessed=5 << 20, transcendentals=tokens * slots
-        ),
-    )(scal, x3, weight_t, acc, kvh)
-    arrived = lax.all_to_all(sent, RING, 0, 0, tiled=True)
+    arrived = []
+    for g in range(HEADS // GROUP):
+        owners = lax.axis_size(GATHER[g])
+        count = GROUP * R // owners
+        sent = pl.pallas_call(
+            functools.partial(project_kernel, g, count),
+            out_shape=jax.ShapeDtypeStruct((owners, 2 * count, LANES), bf16),
+            in_specs=[SMEM] + [VMEM] * 4,
+            out_specs=pl.BlockSpec(memory_space=pltpu.HBM),
+            scratch_shapes=[
+                pltpu.VMEM((GROUP, R // count, 2 * count, LANES), bf16),
+                pltpu.SemaphoreType.DMA((GROUP,)),
+            ],
+            compiler_params=pltpu.CompilerParams(vmem_limit_bytes=16 << 20),
+            cost_estimate=pl.CostEstimate(
+                flops=flops, bytes_accessed=3 << 20, transcendentals=tokens * slots // 2
+            ),
+        )(scal, x3, weight_t, acc, kvh)
+        arrived.append(lax.all_to_all(sent, GATHER[g], 0, 0, tiled=True))
 
     near, stats, q2 = call(
         near_kernel,
@@ -391,28 +392,54 @@
         4, 8, 4 * tokens * 3 * W * HEADS * LANES, 2 << 20, tokens * 3 * W * HEADS,
     )(scal, queries, keys_values, before, after)
 
-    held = call(
-        functools.partial(combine_kernel, lines, lax.axis_size("x"), tokens),
-        jax.ShapeDtypeStruct((lines, 2 * ROWS, LANES), f32),
-        1, 8, 0, 1 << 20, 1 << 17,
-        scratch=[pltpu.VMEM((slots_held, ROWS, LANES), f32)] * 2,
-    )(scal2, arrived)
-    shared = lax.all_to_all(held, LINE, 0, 0, tiled=True)
-    head = lax.div(slot * ROWS, R)
-    gain = lax.dynamic_slice_in_dim(slot_gain, head * DH, DH, 1).reshape(1, 2 * DH)
-    bias = lax.dynamic_slice_in_dim(slot_bias, head * DH, DH, 1).reshape(1, 2 * DH)
-    chunk = call(
-        norm_kernel,
-        jax.ShapeDtypeStruct((slots_held, 2 * ROWS, LANES), bf16),
-        3, 8, 0, 1 << 20, 1 << 15, 0,
-    )(shared, gain, bias)
-    table = lax.all_to_all(chunk, RING, 0, 0, tiled=True)
-
-    return call(
-        far_kernel,
-        jax.ShapeDtypeStruct((tokens, HEADS * DH), bf16),
-        4, 12, 4 * tokens * R * HEADS * LANES, 2 << 20, tokens * R * HEADS, 0,
-    )(q2, table, near, stats)
+    place = {name: lax.axis_size(name) for name in SEQ}
+    stride = {"z": place["yl"] * place["x"], "yl": place["x"], "x": 1}
+    outs = []
+    tables = []
+    for g in range(HEADS // GROUP):
+        owners = lax.axis_size(GATHER[g])
+        count = GROUP * R // owners
+        first, inner = GATHER[g]
+        starts = [
+            ((k // place[inner]) * stride[first] + k % place[inner] * stride[inner]) * tokens
+            for k in range(owners)
+        ]
+        line = lax.axis_index(SHARE[g]) * stride[SHARE[g]]
+        edge = split // tokens
+        in_line = (edge // stride[SHARE[g]]) % place[SHARE[g]] == lax.axis_index(SHARE[g])
+        edge_slot = (edge // stride[first]) % place[first] * place[inner]
+        edge_slot = edge_slot + (edge // stride[inner]) % place[inner]
+        has_edge = (split % tokens != 0) & in_line
+        marks = jnp.stack(
+            [split - line * tokens, jnp.where(has_edge, edge_slot, 0), has_edge]
+        ).astype(jnp.int32)
+        peers = place[SHARE[g]]
+        held = call(
+            functools.partial(combine_kernel, starts, tokens, count),
+            jax.ShapeDtypeStruct((peers, 2 * count, LANES), f32),
+            1, 8, 0, 1 << 19, 1 << 16,
+            scratch=[pltpu.VMEM((owners, count, LANES), f32)] * 2,
+        )(marks, arrived[g])
+        shared = lax.all_to_all(held, SHARE[g], 0, 0, tiled=True)
+        head = g * GROUP + lax.div(lax.axis_index(GATHER[g]) * count, R)
+        gain = lax.dynamic_slice_in_dim(slot_gain, head * DH, DH, 1).reshape(1, 2 * DH)
+        bias = lax.dynamic_slice_in_dim(slot_bias, head * DH, DH, 1).reshape(1, 2 * DH)
+        chunk = call(
+            norm_kernel,
+            jax.ShapeDtypeStruct((owners, 2 * count, LANES), bf16),
+            3, 8, 0, 1 << 19, 1 << 14, 0,
+        )(shared, gain, bias)
+        tables.append(lax.all_to_all(chunk, GATHER[g], 0, 0, tiled=True))
+
+    for g in range(HEADS // GROUP):
+        outs.append(
+            call(
+                functools.partial(far_kernel, g),
+                jax.ShapeDtypeStruct((tokens, (g + 1) * GROUP * DH), bf16),
+                4 + g, 8, 2 * tokens * R * HEADS * LANES, 1 << 20, tokens * R * GROUP, 0,
+            )(q2, tables[g], near, stats, *outs)
+        )
+    return outs[-1]
 
 
 def solution(mesh):

time: 105 us -> 104 us (level)
  starting transfers between devices: 41 us -> 39.5 us
    all_to_all x3, starting transfers between devices: 25.3 us -> 24.2 us  [the longest x1 13.9 us: on_device(): arrived.append(lax.all_to_all(sent, GATHER[g], 0, 0, tiled=True))]
    ppermute x1, waiting for transfers between devices: 1.4 us -> 2.53 us  [on_device(): before = lax.ppermute(keys_values[:, tokens - W:], SEQ, up)]
  transfers between devices with their start and end apart: 8 -> 8, of which waited for: 5 -> 5; matrix products, arithmetic and copies ran while one was open for 4% -> 5% of each run, Pallas kernels for 6% -> 6%
where the time goes in v7:
time: 104 us
  waiting for transfers between devices  43.9 us (42%)
  starting transfers between devices  39.5 us (38%)
  Pallas kernels  13.2 us (13%)
  local copies, waits for them, and re-layouts  4.62 us (4%)
  between operations  2.24 us (2%)
    all_to_all x1, waiting for transfers between devices, on_device(): arrived.append(lax.all_to_all(sent, GATHER[g], 0, 0, tiled=True))  17.1 us
    all_to_all x1, starting transfers between devices, on_device(): arrived.append(lax.all_to_all(sent, GATHER[g], 0, 0, tiled=True))  13.9 us
    ppermute x1, waiting for transfers between devices, on_device(): x2 = lax.ppermute(inputs, 'yh', SWAP)  13.2 us
    ppermute x1, waiting for transfers between devices, on_device(): after = lax.ppermute(keys_values[:, :W], SEQ, down)  7.43 us
    all_to_all x1, starting transfers between devices, on_device(): tables.append(lax.all_to_all(chunk, GATHER[g], 0, 0, tiled=True))  5.52 us
    ppermute x1, starting transfers between devices, on_device(): before = lax.ppermute(keys_values[:, tokens - W:], SEQ, up)  4.88 us
    all_to_all x1, starting transfers between devices, on_device(): shared = lax.all_to_all(held, SHARE[g], 0, 0, tiled=True)  4.77 us
    ppermute x1, starting transfers between devices, on_device(): x2 = lax.ppermute(inputs, 'yh', SWAP)  4.7 us
  transfers between devices with their start and end apart: 8, of which 5 were waited for; matrix products, arithmetic and copies ran while one was open for 5% of the time, Pallas kernels for 6%

profile of v7, /device:TPU:62, one launch (start us, length us, event | category | flops | bytes accessed | tf_op | source)
XLA Modules:
  0.0 103.6 jit_solution(6566291931307515321)
XLA Ops:
  0.0 4.7 %collective-permute-start.2 = (bf16[512,256]{1,0:T(8,128)(2,1)}, bf16[512,256]{1,0:T(8,128)(2,1)}, u32[]{:S(2)}, u32[]{:S(2)}) collective-permute-start(bf16[512,256]{1,0:T(8,128)(2,1)} %x0.1), channel_id=1, source_target_pairs={{0,2},{2,0},{1,3},{3,1},{4,6},{6,4},{5,7},{7,5},{8,10},{10,8},{9,1... | collective-permute-start | bytes 786440 | tf_op jit(solution)/shard_map/ppermute | solution.py:343
  4.7 1.9 %collective-permute-start.4 = (bf16[512,256]{1,0:T(8,128)(2,1)}, bf16[512,256]{1,0:T(8,128)(2,1)S(1)}, u32[]{:S(2)}, u32[]{:S(2)}) collective-permute-start(bf16[512,256]{1,0:T(8,128)(2,1)} %x0.1), channel_id=1, source_target_pairs={{0,1},{1,0},{2,3},{3,2},{4,5},{5,4},{6,7},{7,6},{8,9},{9,8},{10,11... | collective-permute-start | bytes 786440 | tf_op jit(solution)/shard_map/ppermute | solution.py:344
  6.6 13.2 %collective-permute-done.2.x2 = bf16[512,256]{1,0:T(8,128)(2,1)} collective-permute-done((bf16[512,256]{1,0:T(8,128)(2,1)}, bf16[512,256]{1,0:T(8,128)(2,1)}, u32[]{:S(2)}, u32[]{:S(2)}) %collective-permute-start.2) | collective-permute-done | bytes 262176 | tf_op jit(solution)/shard_map/ppermute | solution.py:343
  19.8 1.9 %collective-permute-start.3 = (bf16[512,256]{1,0:T(8,128)(2,1)}, bf16[512,256]{1,0:T(8,128)(2,1)S(1)}, u32[]{:S(2)}, u32[]{:S(2)}) collective-permute-start(bf16[512,256]{1,0:T(8,128)(2,1)} %collective-permute-done.2.x2), channel_id=1, source_target_pairs={{0,1},{1,0},{2,3},{3,2},{4,5},{5,4},{6,7},{7,6},{8,9},{9,8},{10,11... | collective-permute-start | bytes 786440 | tf_op jit(solution)/shard_map/ppermute | solution.py:345
  21.8 0.0 copy-start
  21.8 0.0 copy-start.1
  21.8 2.9 %copy.8 = bf16[4,256,1024]{1,2,0:T(8,128)(2,1)S(1)} copy(bf16[4,256,1024]{2,1,0:T(8,128)(2,1)} %bitcast.16) | data formatting | bytes 4194304 | tf_op jit(solution)/shard_map/reshape | solution.py:351
  24.7 1.3 %fusion.1 = (s32[1,1]{1,0:T(1,128)}, s32[1,1]{1,0:T(1,128)}) fusion(s32[2,512]{1,0:T(2,128)} %param.13), kind=kLoop, calls=%fused_computation.4 | loop fusion | bytes 16 | tf_op jit(solution)/shard_map/slice | solution.py:329
  27.9 0.1 stack.42.scal
  28.0 0.0 copy-done
  28.0 0.9 shard_map.76.kvh_ref
  29.0 0.0 collective-permute-done.4.x1
  29.0 0.0 copy-done.1
  29.0 1.3 %shard_map.74.acc_ref = f32[1024,512]{1,0:T(8,128)S(1)} custom-call(s32[7]{0:T(128)S(1)} %stack.42.scal, bf16[512,256]{1,0:T(8,128)(2,1)S(1)} %copy-done.1, bf16[512,256]{1,0:T(8,128)(2,1)S(1)} %collective-permute-done.4.x1, bf16[4,1024,256]{2,1,0:T(8,128)(2,1)S(1)} %bitcast.13), custom_call_target="tpu_custom_call" | custom-call | flops 536870912 | bytes 5242880 | tf_op jit(solution)/shard_map/pallas_call | solution.py:361
  30.3 1.4 %shard_map.75.acc_ref = f32[1024,512]{1,0:T(8,128)S(1)} custom-call(s32[7]{0:T(128)S(1)} %stack.42.scal, bf16[512,256]{1,0:T(8,128)(2,1)} %collective-permute-done.2.x2, bf16[4,1024,256]{2,1,0:T(8,128)(2,1)S(1)} %bitcast.14, f32[1024,512]{1,0:T(8,128)S(1)} %shard_map.74.acc_ref), custom_call_target="tpu_custom_call" | custom-call | flops 268435456 | bytes 6291456 | tf_op jit(solution)/shard_map/pallas_call | solution.py:364
  31.7 0.0 collective-permute-done.3.x3
  31.7 2.5 %shard_map.77 = bf16[32,64,128]{2,1,0:T(8,128)(2,1)} custom-call(s32[7]{0:T(128)S(1)} %stack.42.scal, bf16[512,256]{1,0:T(8,128)(2,1)S(1)} %collective-permute-done.3.x3, bf16[4,1024,256]{2,1,0:T(8,128)(2,1)S(1)} %bitcast.15, f32[1024,512]{1,0:T(8,128)S(1)} %shard_map.75.acc_ref, bf16[4,512,256]{2,1,0:T(8,128)(2,1)S(1)} %shard_map.76.kvh_ref), custom_call_target="tpu_custom_call" | custom-call | flops 268435456 | bytes 3145728 | tf_op jit(solution)/shard_map/pallas_call | solution.py:369
  34.2 0.0 copy-start.3
  34.2 0.0 copy-start.4
  34.2 0.0 copy-start.2
  34.3 13.9 %all-to-all-start = ((bf16[32,64,128]{2,1,0:T(8,128)(2,1)}), bf16[32,64,128]{2,1,0:T(8,128)(2,1)S(1)}, u32[]{:S(2)}, u32[]{:S(2)}) async-start(bf16[32,64,128]{2,1,0:T(8,128)(2,1)} %shard_map.77), calls=%async_computation | async-start | bytes 1048576 | tf_op jit(solution)/shard_map/all_to_all | solution.py:383
  48.3 0.1 pad_add_fusion.scal
  48.3 17.1 %all-to-all-done.in_ref = bf16[32,64,128]{2,1,0:T(8,128)(2,1)S(1)} async-done(((bf16[32,64,128]{2,1,0:T(8,128)(2,1)}), bf16[32,64,128]{2,1,0:T(8,128)(2,1)S(1)}, u32[]{:S(2)}, u32[]{:S(2)}) %all-to-all-start) | async-done | bytes 524320 | tf_op jit(solution)/shard_map/all_to_all | solution.py:383
  65.5 1.8 %shard_map.78 = f32[4,64,128]{2,1,0:T(8,128)} custom-call(s32[3]{0:T(128)S(1)} %pad_add_fusion.scal, bf16[32,64,128]{2,1,0:T(8,128)(2,1)S(1)} %all-to-all-done.in_ref), custom_call_target="tpu_custom_call" | custom-call | bytes 524288 | tf_op jit(solution)/shard_map/pallas_call | solution.py:417
  67.2 4.8 %all-to-all-start.1 = ((f32[4,64,128]{2,1,0:T(8,128)}), f32[4,64,128]{2,1,0:T(8,128)S(1)}, u32[]{:S(2)}, u32[]{:S(2)}) async-start(f32[4,64,128]{2,1,0:T(8,128)} %shard_map.78), calls=%async_computation.1 | async-start | bytes 262144 | tf_op jit(solution)/shard_map/all_to_all | solution.py:423
  72.0 0.0 copy-done.3
  72.0 0.0 copy-done.4
  72.0 0.1 constant_dynamic-slice_fusion
  72.1 0.1 reshape.10.gain_ref
  72.2 0.1 reshape.11.bias_ref
  72.2 3.7 %all-to-all-done.1.in_ref = f32[4,64,128]{2,1,0:T(8,128)S(1)} async-done(((f32[4,64,128]{2,1,0:T(8,128)}), f32[4,64,128]{2,1,0:T(8,128)S(1)}, u32[]{:S(2)}, u32[]{:S(2)}) %all-to-all-start.1) | async-done | bytes 131104 | tf_op jit(solution)/shard_map/all_to_all | solution.py:423
  75.9 1.2 %shard_map.79 = bf16[32,64,128]{2,1,0:T(8,128)(2,1)} custom-call(f32[4,64,128]{2,1,0:T(8,128)S(1)} %all-to-all-done.1.in_ref, f32[1,128]{1,0:T(1,128)S(1)} %reshape.10.gain_ref, f32[1,128]{1,0:T(1,128)S(1)} %reshape.11.bias_ref), custom_call_target="tpu_custom_call" | custom-call | bytes 524288 | tf_op jit(solution)/shard_map/pallas_call | solution.py:427
  77.1 5.5 %all-to-all-start.2 = ((bf16[32,64,128]{2,1,0:T(8,128)(2,1)}), bf16[32,64,128]{2,1,0:T(8,128)(2,1)S(1)}, u32[]{:S(2)}, u32[]{:S(2)}) async-start(bf16[32,64,128]{2,1,0:T(8,128)(2,1)} %shard_map.79), calls=%async_computation.2 | async-start | bytes 1048576 | tf_op jit(solution)/shard_map/all_to_all | solution.py:432
  82.7 4.9 %collective-permute-start = (bf16[2,128,256]{2,1,0:T(8,128)(2,1)S(1)}, bf16[2,128,256]{2,1,0:T(8,128)(2,1)S(1)}, u32[]{:S(2)}, u32[]{:S(2)}) collective-permute-start(bf16[2,128,256]{2,1,0:T(8,128)(2,1)S(1)} %get-tuple-element.12), channel_id=1, source_target_pairs={{0,4},{4,8},{8,12},{12,16},{16,20},{20,24},{24,28},{28,32},{32,36}... | collective-permute-start | bytes 393224 | tf_op jit(solution)/shard_map/ppermute | solution.py:348
  87.6 1.9 %collective-permute-start.1 = (bf16[2,128,256]{2,1,0:T(8,128)(2,1)S(1)}, bf16[2,128,256]{2,1,0:T(8,128)(2,1)S(1)}, u32[]{:S(2)}, u32[]{:S(2)}) collective-permute-start(bf16[2,128,256]{2,1,0:T(8,128)(2,1)S(1)} %get-tuple-element.11), channel_id=1, source_target_pairs={{4,0},{8,4},{12,8},{16,12},{20,16},{24,20},{28,24},{32,28},{36,32}... | collective-permute-start | bytes 393224 | tf_op jit(solution)/shard_map/ppermute | solution.py:349
  89.5 2.5 %collective-permute-done.before_ref = bf16[2,128,256]{2,1,0:T(8,128)(2,1)S(1)} collective-permute-done((bf16[2,128,256]{2,1,0:T(8,128)(2,1)S(1)}, bf16[2,128,256]{2,1,0:T(8,128)(2,1)S(1)}, u32[]{:S(2)}, u32[]{:S(2)}) %collective-permute-start) | collective-permute-done | bytes 131104 | tf_op jit(solution)/shard_map/ppermute | solution.py:348
  92.0 7.4 %collective-permute-done.1.after_ref = bf16[2,128,256]{2,1,0:T(8,128)(2,1)S(1)} collective-permute-done((bf16[2,128,256]{2,1,0:T(8,128)(2,1)S(1)}, bf16[2,128,256]{2,1,0:T(8,128)(2,1)S(1)}, u32[]{:S(2)}, u32[]{:S(2)}) %collective-permute-start.1) | collective-permute-done | bytes 131104 | tf_op jit(solution)/shard_map/ppermute | solution.py:349
  99.5 0.0 copy-done.2
  99.5 2.2 %shard_map.73 = (f32[256,512]{1,0:T(8,128)S(1)}, f32[16,512]{1,0:T(8,128)S(1)}, bf16[4,512,128]{2,1,0:T(8,128)(2,1)S(1)}) custom-call(s32[7]{0:T(128)S(1)} %stack.42.scal, bf16[512,256]{1,0:T(8,128)(2,1)S(1)} %copy-done.2, bf16[2,512,256]{2,1,0:T(8,128)(2,1)S(1)} %copy-done, bf16[2,128,256]{2,1,0:T(8,128)(2,1)S(1)} %collective-permute-done.before_ref, ...), custom_call_target="tpu_custom_call" | custom-call | flops 402653184 | bytes 2097152 | tf_op jit(solution)/shard_map/pallas_call | solution.py:385
  101.7 0.0 all-to-all-done.2.tab_ref
  101.8 1.9 %shard_map.80 = bf16[512,256]{1,0:T(8,128)(2,1)} custom-call(bf16[4,512,128]{2,1,0:T(8,128)(2,1)S(1)} %get-tuple-element.8.q2_ref, bf16[32,64,128]{2,1,0:T(8,128)(2,1)S(1)} %all-to-all-done.2.tab_ref, f32[256,512]{1,0:T(8,128)S(1)} %get-tuple-element.9.o_ref, f32[16,512]{1,0:T(8,128)S(1)} %get-tuple-element.10.stat_ref), custom_call_target="tpu_custom_call" | custom-call | flops 134217728 | bytes 1048576 | tf_op jit(solution)/shard_map/pallas_call | solution.py:436
  (1 shorter events, 0.0 us)
Async XLA Ops:
  0.0 19.8 %collective-permute-start.2 = (bf16[512,256]{1,0:T(8,128)(2,1)}, bf16[512,256]{1,0:T(8,128)(2,1)}, u32[]{:S(2)}, u32[]{:S(2)}) collective-permute-start(bf16[512,256]{1,0:T(8,128)(2,1)} %x0.1), channel_id=1, source_target_pairs={{0,2},{2,0},{1,3},{3,1},{4,6},{6,4},{5,7},{7,5},{8,10},{10,8},{9,1... | collective-permute-start | bytes 786440 | tf_op jit(solution)/shard_map/ppermute | solution.py:343
  4.7 24.3 %collective-permute-start.4 = (bf16[512,256]{1,0:T(8,128)(2,1)}, bf16[512,256]{1,0:T(8,128)(2,1)S(1)}, u32[]{:S(2)}, u32[]{:S(2)}) collective-permute-start(bf16[512,256]{1,0:T(8,128)(2,1)} %x0.1), channel_id=1, source_target_pairs={{0,1},{1,0},{2,3},{3,2},{4,5},{5,4},{6,7},{7,6},{8,9},{9,8},{10,11... | collective-permute-start | bytes 786440 | tf_op jit(solution)/shard_map/ppermute | solution.py:344
  19.8 11.9 %collective-permute-start.3 = (bf16[512,256]{1,0:T(8,128)(2,1)}, bf16[512,256]{1,0:T(8,128)(2,1)S(1)}, u32[]{:S(2)}, u32[]{:S(2)}) collective-permute-start(bf16[512,256]{1,0:T(8,128)(2,1)} %collective-permute-done.2.x2), channel_id=1, source_target_pairs={{0,1},{1,0},{2,3},{3,2},{4,5},{5,4},{6,7},{7,6},{8,9},{9,8},{10,11... | collective-permute-start | bytes 786440 | tf_op jit(solution)/shard_map/ppermute | solution.py:345
  21.8 6.3 %copy-start = (bf16[2,512,256]{2,1,0:T(8,128)(2,1)S(1)}, bf16[2,512,256]{2,1,0:T(8,128)(2,1)}, u32[]{:S(2)}) copy-start(bf16[2,512,256]{2,1,0:T(8,128)(2,1)} %kv_ref.3) | copy-start | bytes 1572868
  21.8 7.2 %copy-start.1 = (bf16[512,256]{1,0:T(8,128)(2,1)S(1)}, bf16[512,256]{1,0:T(8,128)(2,1)}, u32[]{:S(2)}) copy-start(bf16[512,256]{1,0:T(8,128)(2,1)} %x0.1) | copy-start | bytes 786436
  34.2 37.8 %copy-start.3 = (f32[2,256]{1,0:T(2,128)S(1)}, f32[2,256]{1,0:T(2,128)}, u32[]{:S(2)}) copy-start(f32[2,256]{1,0:T(2,128)} %param.12) | copy-start | bytes 6148
  34.2 37.8 %copy-start.4 = (f32[2,256]{1,0:T(2,128)S(1)}, f32[2,256]{1,0:T(2,128)}, u32[]{:S(2)}) copy-start(f32[2,256]{1,0:T(2,128)} %param.11) | copy-start | bytes 6148
  34.2 65.2 %copy-start.2 = (bf16[512,256]{1,0:T(8,128)(2,1)S(1)}, bf16[512,256]{1,0:T(8,128)(2,1)}, u32[]{:S(2)}) copy-start(bf16[512,256]{1,0:T(8,128)(2,1)} %q_ref.1) | copy-start | bytes 786436
  34.3 31.2 %all-to-all-start = ((bf16[32,64,128]{2,1,0:T(8,128)(2,1)}), bf16[32,64,128]{2,1,0:T(8,128)(2,1)S(1)}, u32[]{:S(2)}, u32[]{:S(2)}) async-start(bf16[32,64,128]{2,1,0:T(8,128)(2,1)} %shard_map.77), calls=%async_computation | async-start | bytes 1048576 | tf_op jit(solution)/shard_map/all_to_all | solution.py:383
  67.2 8.7 %all-to-all-start.1 = ((f32[4,64,128]{2,1,0:T(8,128)}), f32[4,64,128]{2,1,0:T(8,128)S(1)}, u32[]{:S(2)}, u32[]{:S(2)}) async-start(f32[4,64,128]{2,1,0:T(8,128)} %shard_map.78), calls=%async_computation.1 | async-start | bytes 262144 | tf_op jit(solution)/shard_map/all_to_all | solution.py:423
  77.1 24.6 %all-to-all-start.2 = ((bf16[32,64,128]{2,1,0:T(8,128)(2,1)}), bf16[32,64,128]{2,1,0:T(8,128)(2,1)S(1)}, u32[]{:S(2)}, u32[]{:S(2)}) async-start(bf16[32,64,128]{2,1,0:T(8,128)(2,1)} %shard_map.79), calls=%async_computation.2 | async-start | bytes 1048576 | tf_op jit(solution)/shard_map/all_to_all | solution.py:432
  82.7 9.3 %collective-permute-start = (bf16[2,128,256]{2,1,0:T(8,128)(2,1)S(1)}, bf16[2,128,256]{2,1,0:T(8,128)(2,1)S(1)}, u32[]{:S(2)}, u32[]{:S(2)}) collective-permute-start(bf16[2,128,256]{2,1,0:T(8,128)(2,1)S(1)} %get-tuple-element.12), channel_id=1, source_target_pairs={{0,4},{4,8},{8,12},{12,16},{16,20},{20,24},{24,28},{28,32},{32,36}... | collective-permute-start | bytes 393224 | tf_op jit(solution)/shard_map/ppermute | solution.py:348
  87.6 11.9 %collective-permute-start.1 = (bf16[2,128,256]{2,1,0:T(8,128)(2,1)S(1)}, bf16[2,128,256]{2,1,0:T(8,128)(2,1)S(1)}, u32[]{:S(2)}, u32[]{:S(2)}) collective-permute-start(bf16[2,128,256]{2,1,0:T(8,128)(2,1)S(1)} %get-tuple-element.11), channel_id=1, source_target_pairs={{4,0},{8,4},{12,8},{16,12},{20,16},{24,20},{28,24},{32,28},{36,32}... | collective-permute-start | bytes 393224 | tf_op jit(solution)/shard_map/ppermute | solution.py:349

commit v8 on v7

--- a/solution.py
+++ b/solution.py
@@ -15,8 +15,7 @@
 HEADS = 4
 LANES = 128
 GROUP = 4
-GATHER = (("z", "yl"),)
-SHARE = ("x",)
+COUNT = 8
 SEQ = ("z", "yl", "x")
 DOC = ("yh", "c")
 EPS = 1e-05
@@ -26,7 +25,6 @@
 f32 = jnp.float32
 bf16 = jnp.bfloat16
 VMEM = pl.BlockSpec(memory_space=pltpu.VMEM)
-SMEM = pl.BlockSpec(memory_space=pltpu.SMEM)
 
 
 def call(kernel, out_shape, n_in, vmem_mib, flops, nbytes, exps=0, scalars=1, scratch=()):
@@ -34,7 +32,7 @@
     return pl.pallas_call(
         kernel,
         out_shape=out_shape,
-        in_specs=[SMEM] * scalars + [VMEM] * n_in,
+        in_specs=[VMEM] * (scalars + n_in),
         out_specs=VMEM if single else [VMEM] * len(out_shape),
         scratch_shapes=list(scratch),
         compiler_params=pltpu.CompilerParams(vmem_limit_bytes=vmem_mib << 20),
@@ -60,7 +58,7 @@
 
 def prep_kernel(scal, kv_ref, kvh_ref):
     tokens = kv_ref.shape[1]
-    local = scal[0]
+    local = scal[0, 0]
     second = lax.broadcasted_iota(jnp.int32, (tokens, LANES), 0) >= local
     left = lanes_of((tokens, LANES)) < DH
     for pair in range(HEADS // 2):
@@ -78,7 +76,7 @@
 
 def near_kernel(scal, q_ref, kv_ref, before_ref, after_ref, o_ref, stat_ref, q2_ref):
     tokens = q_ref.shape[0]
-    local, base, total = scal[0], scal[1], scal[2]
+    local, base, total = scal[0, 0], scal[0, 1], scal[0, 2]
     blocks = tokens // W
     span = 3 * W
     key = lax.broadcasted_iota(jnp.int32, (span, W), 0)
@@ -136,16 +134,16 @@
 
 
 def partial_kernel(scal, x0, x1, wt_ref, acc_ref):
-    acc_ref[...] = dot_nt(wt_ref[scal[3]], x0[...]) + dot_nt(wt_ref[scal[4]], x1[...])
+    acc_ref[...] = dot_nt(wt_ref[scal[0, 3]], x0[...]) + dot_nt(wt_ref[scal[0, 4]], x1[...])
 
 
 def more_kernel(scal, x2, wt_ref, acc_ref, out_ref):
-    out_ref[...] = acc_ref[...] + dot_nt(wt_ref[scal[5]], x2[...])
+    out_ref[...] = acc_ref[...] + dot_nt(wt_ref[scal[0, 5]], x2[...])
 
 
 def project_kernel(group, count, scal, x3, wt_ref, acc_ref, kvh_ref, out_ref, held, sems):
     tokens = x3.shape[0]
-    local = scal[0]
+    local = scal[0, 0]
     mixed = jnp.logical_and(local > 0, local < tokens)
     lane = lanes_of((R, LANES))
     at_a = lane == 0
@@ -156,7 +154,7 @@
     def logits_of(i):
         at = (group * GROUP + i) * R
         rows = slice(at, at + R)
-        return acc_ref[rows, :] + dot_nt(wt_ref[scal[6], rows, :], x3[...])
+        return acc_ref[rows, :] + dot_nt(wt_ref[scal[0, 6], rows, :], x3[...])
 
     def from_first(n):
         return n - jnp.where(left, n[:, 0:1], n[:, DH : DH + 1])
@@ -212,56 +210,40 @@
             copy.wait()
 
 
-def combine_kernel(starts, tokens, count, scal, in_ref, out_ref, tops, fine):
+def combine_kernel(tokens, scal, in_ref, gain_ref, bias_ref, out_ref, marks):
     senders = in_ref.shape[0]
-    slot = scal[1]
-    has_edge = scal[2] > 0
-    shape = (count, LANES)
-    flat = (senders * count, LANES)
-    row = lax.broadcasted_iota(jnp.int32, (LANES, LANES), 0)
-    pick_both = jnp.where((row == 0) | (row == DH), 1.0, 0.0).astype(bf16)
-    pick_first = jnp.where(row == 0, 1.0, 0.0).astype(bf16)
-    tops[...] = dot_nn(in_ref[:, :count].reshape(flat), pick_both).reshape(tops.shape)
-    fine[...] = dot_nn(in_ref[:, count:].reshape(flat), pick_first).reshape(fine.shape)
+    slot = scal[0, 1]
+    has_edge = scal[0, 2] > 0
+    shape = (COUNT, LANES)
+    row = lax.broadcasted_iota(jnp.int32, (LANES, 2 * LANES), 0)
+    col = lanes_of((LANES, 2 * LANES))
+    pick = jnp.where((row == 0) | ((row == DH) & (col < LANES)), 1.0, 0.0).astype(bf16)
+    marks[...] = dot_nn(in_ref[...].reshape(senders * 2 * COUNT, LANES), pick).reshape(marks.shape)
     low = jnp.full(shape, LOW, f32)
-    border = jnp.full(shape, scal[0], jnp.int32)
-    extra = in_ref[slot, count:]
-    extra_top = jnp.where(has_edge, dot_nn(extra, pick_both), low)
+    border = jnp.full(shape, scal[0, 0], jnp.int32)
+    extra = in_ref[slot].astype(f32)[COUNT:]
+    extra_top = jnp.where(has_edge, marks[slot][COUNT:, :LANES], low)
     top0, full0, top1, full1 = low, low, extra_top, extra_top
     for k in range(senders):
-        late = border <= starts[k]
-        is_edge = jnp.logical_and(border > starts[k], border < starts[k] + tokens)
-        top = tops[k]
-        full = top + jnp.where(is_edge, 0.0, fine[k])
+        late = border <= k * tokens
+        is_edge = jnp.logical_and(border > k * tokens, border < (k + 1) * tokens)
+        top = marks[k, :COUNT, :LANES]
+        full = top + jnp.where(is_edge, 0.0, marks[k, COUNT:, LANES:])
         top0 = jnp.maximum(top0, jnp.where(late, low, top))
         full0 = jnp.maximum(full0, jnp.where(late, low, full))
         top1 = jnp.maximum(top1, jnp.where(late, top, low))
         full1 = jnp.maximum(full1, jnp.where(late, full, low))
     n0 = jnp.zeros(shape, f32)
-    n1 = jnp.where(has_edge, extra.astype(f32) * jnp.exp(extra_top - top1), 0.0)
+    n1 = jnp.where(has_edge, extra * jnp.exp(extra_top - top1), 0.0)
     for k in range(senders):
-        late = border <= starts[k]
-        is_edge = jnp.logical_and(border > starts[k], border < starts[k] + tokens)
-        value = in_ref[k, :count].astype(f32) + jnp.where(is_edge, 0.0, in_ref[k, count:].astype(f32))
-        value = value * jnp.exp(tops[k] - jnp.where(late, top1, top0))
+        late = border <= k * tokens
+        is_edge = jnp.logical_and(border > k * tokens, border < (k + 1) * tokens)
+        got = in_ref[k].astype(f32)
+        value = got[:COUNT] + jnp.where(is_edge, 0.0, got[COUNT:])
+        value = value * jnp.exp(marks[k, :COUNT, :LANES] - jnp.where(late, top1, top0))
         n0 = n0 + jnp.where(late, 0.0, value)
         n1 = n1 + jnp.where(late, value, 0.0)
     lane = lanes_of(shape)
-    n0 = jnp.where(lane == 0, top0, jnp.where(lane == DH, full0, n0))
-    n1 = jnp.where(lane == 0, top1, jnp.where(lane == DH, full1, n1))
-    for at in range(out_ref.shape[0]):
-        out_ref[at, :count] = n0
-        out_ref[at, count:] = n1
-
-
-def norm_kernel(in_ref, gain_ref, bias_ref, out_ref):
-    count = in_ref.shape[1] // 2
-    got = in_ref[...]
-    top = jnp.broadcast_to(got[:, :, 0:1], got.shape)
-    whole = jnp.max(top, axis=0)
-    full = jnp.max(jnp.broadcast_to(got[:, :, DH : DH + 1], got.shape), axis=0)
-    n = jnp.sum(got * jnp.exp(top - whole[None]), axis=0)
-    lane = lanes_of((2 * count, LANES))
     left = lane < DH
     used = jnp.logical_and(lane != 0, lane != DH)
 
@@ -270,13 +252,15 @@
         b = jnp.sum(jnp.where(left, 0.0, v), axis=1, keepdims=True)
         return jnp.where(left, a, b) * (1.0 / DH)
 
-    n = jnp.where(used, n, 0.0)
-    centred = n - halves(n)
-    variance = halves(centred * centred)
-    scale = jnp.exp(2.0 * (full - whole))
-    table = centred * lax.rsqrt(variance + EPS * scale) * gain_ref[...] + bias_ref[...]
-    t0, t1 = table[:count], table[count:]
-    left = left[:count]
+    def norm(n, top, full):
+        n = jnp.where(used, n, 0.0)
+        centred = n - halves(n)
+        variance = halves(centred * centred)
+        scale = jnp.exp(2.0 * (full - top))
+        return centred * lax.rsqrt(variance + EPS * scale) * gain_ref[...] + bias_ref[...]
+
+    t0 = norm(n0, top0, full0)
+    t1 = norm(n1, top1, full1)
     keys = jnp.where(left, t0, pltpu.roll(t1, DH, 1))
     values = jnp.where(left, pltpu.roll(t0, DH, 1), t1)
     chunk = jnp.concatenate([keys, values], axis=0).astype(bf16)[None]
@@ -292,9 +276,8 @@
         out_ref[:, i * LANES : (i + 1) * LANES] = done[...]
 
     def rows_of(i, part):
-        return tab_ref[
-            i * parts : (i + 1) * parts, part * count : (part + 1) * count
-        ].reshape(R, LANES)
+        got = tab_ref[i * parts : (i + 1) * parts].astype(f32)
+        return got[:, part * count : (part + 1) * count].reshape(R, LANES).astype(bf16)
 
     def scores_of(i):
         return dot_nt(rows_of(i, 0), q2_ref[group * GROUP + i])
@@ -339,7 +322,7 @@
             (1 - yh) * 2 + c,
             (1 - yh) * 2 + 1 - c,
         ]
-    ).astype(jnp.int32)
+    ).astype(jnp.int32)[None]
     x2 = lax.ppermute(inputs, "yh", SWAP)
     x1 = lax.ppermute(inputs, "c", SWAP)
     x3 = lax.ppermute(x2, "c", SWAP)
@@ -364,12 +347,12 @@
     acc = call(more_kernel, acc_shape, 3, 16, flops, 6 << 20)(scal, x2, weight_t, acc)
     arrived = []
     for g in range(HEADS // GROUP):
-        owners = lax.axis_size(GATHER[g])
-        count = GROUP * R // owners
+        owners = shards
+        count = COUNT
         sent = pl.pallas_call(
             functools.partial(project_kernel, g, count),
             out_shape=jax.ShapeDtypeStruct((owners, 2 * count, LANES), bf16),
-            in_specs=[SMEM] + [VMEM] * 4,
+            in_specs=[VMEM] * 5,
             out_specs=pl.BlockSpec(memory_space=pltpu.HBM),
             scratch_shapes=[
                 pltpu.VMEM((GROUP, R // count, 2 * count, LANES), bf16),
@@ -380,7 +363,7 @@
                 flops=flops, bytes_accessed=3 << 20, transcendentals=tokens * slots // 2
             ),
         )(scal, x3, weight_t, acc, kvh)
-        arrived.append(lax.all_to_all(sent, GATHER[g], 0, 0, tiled=True))
+        arrived.append(lax.all_to_all(sent, SEQ, 0, 0, tiled=True))
 
     near, stats, q2 = call(
         near_kernel,
@@ -392,44 +375,20 @@
         4, 8, 4 * tokens * 3 * W * HEADS * LANES, 2 << 20, tokens * 3 * W * HEADS,
     )(scal, queries, keys_values, before, after)
 
-    place = {name: lax.axis_size(name) for name in SEQ}
-    stride = {"z": place["yl"] * place["x"], "yl": place["x"], "x": 1}
     outs = []
-    tables = []
-    for g in range(HEADS // GROUP):
-        owners = lax.axis_size(GATHER[g])
-        count = GROUP * R // owners
-        first, inner = GATHER[g]
-        starts = [
-            ((k // place[inner]) * stride[first] + k % place[inner] * stride[inner]) * tokens
-            for k in range(owners)
-        ]
-        line = lax.axis_index(SHARE[g]) * stride[SHARE[g]]
-        edge = split // tokens
-        in_line = (edge // stride[SHARE[g]]) % place[SHARE[g]] == lax.axis_index(SHARE[g])
-        edge_slot = (edge // stride[first]) % place[first] * place[inner]
-        edge_slot = edge_slot + (edge // stride[inner]) % place[inner]
-        has_edge = (split % tokens != 0) & in_line
-        marks = jnp.stack(
-            [split - line * tokens, jnp.where(has_edge, edge_slot, 0), has_edge]
-        ).astype(jnp.int32)
-        peers = place[SHARE[g]]
-        held = call(
-            functools.partial(combine_kernel, starts, tokens, count),
-            jax.ShapeDtypeStruct((peers, 2 * count, LANES), f32),
-            1, 8, 0, 1 << 19, 1 << 16,
-            scratch=[pltpu.VMEM((owners, count, LANES), f32)] * 2,
-        )(marks, arrived[g])
-        shared = lax.all_to_all(held, SHARE[g], 0, 0, tiled=True)
-        head = g * GROUP + lax.div(lax.axis_index(GATHER[g]) * count, R)
-        gain = lax.dynamic_slice_in_dim(slot_gain, head * DH, DH, 1).reshape(1, 2 * DH)
-        bias = lax.dynamic_slice_in_dim(slot_bias, head * DH, DH, 1).reshape(1, 2 * DH)
-        chunk = call(
-            norm_kernel,
-            jax.ShapeDtypeStruct((owners, 2 * count, LANES), bf16),
-            3, 8, 0, 1 << 19, 1 << 14, 0,
-        )(shared, gain, bias)
-        tables.append(lax.all_to_all(chunk, GATHER[g], 0, 0, tiled=True))
+    edge = split // tokens
+    has_edge = split % tokens != 0
+    marks = jnp.stack([split, jnp.where(has_edge, edge, 0), has_edge]).astype(jnp.int32)[None]
+    head = lax.div(shard * COUNT, R)
+    gain = lax.dynamic_slice_in_dim(slot_gain, head * DH, DH, 1).reshape(1, 2 * DH)
+    bias = lax.dynamic_slice_in_dim(slot_bias, head * DH, DH, 1).reshape(1, 2 * DH)
+    chunk = call(
+        functools.partial(combine_kernel, tokens),
+        jax.ShapeDtypeStruct((shards, 2 * COUNT, LANES), bf16),
+        3, 10, 0, 1 << 20, 1 << 17,
+        scratch=[pltpu.VMEM((shards, 2 * COUNT, 2 * LANES), f32)],
+    )(marks, arrived[0], gain, bias)
+    tables = [lax.all_to_all(chunk, SEQ, 0, 0, tiled=True)]
 
     for g in range(HEADS // GROUP):
         outs.append(

time: 104 us -> 103 us (level)
  the two profiles are of different devices: /device:TPU:62 before, /device:TPU:2 now
where the time goes in v8:
time: 103 us; the launch traced here: 102 us
  starting transfers between devices  44.8 us (43%)
  waiting for transfers between devices  40.5 us (39%)
  Pallas kernels  10.2 us (10%)
  local copies, waits for them, and re-layouts  4.58 us (4%)
  between operations  2.06 us (2%)
    all_to_all x1, starting transfers between devices, on_device(): arrived.append(lax.all_to_all(sent, SEQ, 0, 0, tiled=True))  20.7 us
    all_to_all x1, waiting for transfers between devices, on_device(): arrived.append(lax.all_to_all(sent, SEQ, 0, 0, tiled=True))  19.9 us
    all_to_all x1, waiting for transfers between devices, on_device(): tables = [lax.all_to_all(chunk, SEQ, 0, 0, tiled=True)]  8.33 us
    ppermute x1, starting transfers between devices, on_device(): x2 = lax.ppermute(inputs, 'yh', SWAP)  7.72 us
    all_to_all x1, starting transfers between devices, on_device(): tables = [lax.all_to_all(chunk, SEQ, 0, 0, tiled=True)]  6.57 us
    ppermute x1, waiting for transfers between devices, on_device(): x2 = lax.ppermute(inputs, 'yh', SWAP)  6.49 us
    ppermute x1, starting transfers between devices, on_device(): before = lax.ppermute(keys_values[:, tokens - W:], SEQ, up)  3.38 us
    ppermute x1, waiting for transfers between devices, on_device(): after = lax.ppermute(keys_values[:, :W], SEQ, down)  3.21 us
  transfers between devices with their start and end apart: 7, of which 5 were waited for; matrix products, arithmetic and copies ran while one was open for 5% of the time, Pallas kernels for 4%

profile of v8, /device:TPU:2, one launch (start us, length us, event | category | flops | bytes accessed | tf_op | source)
XLA Modules:
  0.0 102.2 jit_solution(3080208627931240738)
XLA Ops:
  0.0 7.7 %collective-permute-start.2 = (bf16[512,256]{1,0:T(8,128)(2,1)}, bf16[512,256]{1,0:T(8,128)(2,1)}, u32[]{:S(2)}, u32[]{:S(2)}) collective-permute-start(bf16[512,256]{1,0:T(8,128)(2,1)} %x0.1), channel_id=1, source_target_pairs={{0,2},{2,0},{1,3},{3,1},{4,6},{6,4},{5,7},{7,5},{8,10},{10,8},{9,1... | collective-permute-start | bytes 786440 | tf_op jit(solution)/shard_map/ppermute | solution.py:326
  7.7 1.9 %collective-permute-start.4 = (bf16[512,256]{1,0:T(8,128)(2,1)}, bf16[512,256]{1,0:T(8,128)(2,1)S(1)}, u32[]{:S(2)}, u32[]{:S(2)}) collective-permute-start(bf16[512,256]{1,0:T(8,128)(2,1)} %x0.1), channel_id=1, source_target_pairs={{0,1},{1,0},{2,3},{3,2},{4,5},{5,4},{6,7},{7,6},{8,9},{9,8},{10,11... | collective-permute-start | bytes 786440 | tf_op jit(solution)/shard_map/ppermute | solution.py:327
  9.7 6.5 %collective-permute-done.2.x2 = bf16[512,256]{1,0:T(8,128)(2,1)} collective-permute-done((bf16[512,256]{1,0:T(8,128)(2,1)}, bf16[512,256]{1,0:T(8,128)(2,1)}, u32[]{:S(2)}, u32[]{:S(2)}) %collective-permute-start.2) | collective-permute-done | bytes 262176 | tf_op jit(solution)/shard_map/ppermute | solution.py:326
  16.2 1.9 %collective-permute-start.3 = (bf16[512,256]{1,0:T(8,128)(2,1)}, bf16[512,256]{1,0:T(8,128)(2,1)S(1)}, u32[]{:S(2)}, u32[]{:S(2)}) collective-permute-start(bf16[512,256]{1,0:T(8,128)(2,1)} %collective-permute-done.2.x2), channel_id=1, source_target_pairs={{0,1},{1,0},{2,3},{3,2},{4,5},{5,4},{6,7},{7,6},{8,9},{9,8},{10,11... | collective-permute-start | bytes 786440 | tf_op jit(solution)/shard_map/ppermute | solution.py:328
  18.1 0.0 copy-start
  18.1 0.0 copy-start.1
  18.1 2.9 %copy.8 = bf16[4,256,1024]{1,2,0:T(8,128)(2,1)S(1)} copy(bf16[4,256,1024]{2,1,0:T(8,128)(2,1)} %bitcast.24) | data formatting | bytes 4194304 | tf_op jit(solution)/shard_map/reshape | solution.py:334
  21.1 1.3 %fusion.1 = (s32[1,1]{1,0:T(1,128)}, s32[1,1]{1,0:T(1,128)}) fusion(s32[2,512]{1,0:T(2,128)} %param.13), kind=kLoop, calls=%fused_computation.4 | loop fusion | bytes 16 | tf_op jit(solution)/shard_map/slice | solution.py:312
  24.1 0.1 stack.42
  24.2 0.0 copy-done
  24.2 0.4 shard_map.76.kvh_ref
  24.6 0.0 collective-permute-done.4.x1
  24.6 0.0 copy-done.1
  24.6 0.8 shard_map.74.acc_ref
  25.4 1.4 %shard_map.75.acc_ref = f32[1024,512]{1,0:T(8,128)S(1)} custom-call(s32[1,7]{1,0:T(1,128)S(1)} %bitcast.21, bf16[512,256]{1,0:T(8,128)(2,1)} %collective-permute-done.2.x2, bf16[4,1024,256]{2,1,0:T(8,128)(2,1)S(1)} %bitcast.17, f32[1024,512]{1,0:T(8,128)S(1)} %shard_map.74.acc_ref), custom_call_target="tpu_custom_call" | custom-call | flops 268435456 | bytes 6291456 | tf_op jit(solution)/shard_map/pallas_call | solution.py:347
  26.9 0.0 copy-start.3
  26.9 0.0 copy-start.4
  26.9 0.0 collective-permute-done.3.x3
  26.9 2.0 %shard_map.77 = bf16[128,16,128]{2,1,0:T(8,128)(2,1)} custom-call(s32[1,7]{1,0:T(1,128)S(1)} %bitcast.22, bf16[512,256]{1,0:T(8,128)(2,1)S(1)} %collective-permute-done.3.x3, bf16[4,1024,256]{2,1,0:T(8,128)(2,1)S(1)} %bitcast.18, f32[1024,512]{1,0:T(8,128)S(1)} %shard_map.75.acc_ref, bf16[4,512,256]{2,1,0:T(8,128)(2,1)S(1)} %shard_map.76.kvh_ref), custom_call_target="tpu_custom_call" | custom-call | flops 268435456 | bytes 3145728 | tf_op jit(solution)/shard_map/pallas_call | solution.py:352
  28.9 0.0 copy-start.2
  28.9 20.7 %all-to-all-start = ((bf16[128,16,128]{2,1,0:T(8,128)(2,1)}), bf16[128,16,128]{2,1,0:T(8,128)(2,1)S(1)}, u32[]{:S(2)}, u32[]{:S(2)}) async-start(bf16[128,16,128]{2,1,0:T(8,128)(2,1)} %shard_map.77), calls=%async_computation | async-start | bytes 1048576 | tf_op jit(solution)/shard_map/all_to_all | solution.py:366
  49.7 0.0 copy-done.3
  49.7 0.0 copy-done.4
  49.7 0.1 constant_dynamic-slice_fusion
  49.8 0.1 reshape.10.gain_ref
  49.8 0.1 reshape.11.bias_ref
  49.9 0.1 add_bitcast_fusion.scal
  50.0 19.9 %all-to-all-done.in_ref = bf16[128,16,128]{2,1,0:T(8,128)(2,1)S(1)} async-done(((bf16[128,16,128]{2,1,0:T(8,128)(2,1)}), bf16[128,16,128]{2,1,0:T(8,128)(2,1)S(1)}, u32[]{:S(2)}, u32[]{:S(2)}) %all-to-all-start) | async-done | bytes 524320 | tf_op jit(solution)/shard_map/all_to_all | solution.py:366
  69.9 1.8 %shard_map.78 = bf16[128,16,128]{2,1,0:T(8,128)(2,1)} custom-call(s32[1,3]{1,0:T(1,128)S(1)} %add_bitcast_fusion.scal, bf16[128,16,128]{2,1,0:T(8,128)(2,1)S(1)} %all-to-all-done.in_ref, f32[1,128]{1,0:T(1,128)S(1)} %reshape.10.gain_ref, f32[1,128]{1,0:T(1,128)S(1)} %reshape.11.bias_ref), custom_call_target="tpu_custom_call" | custom-call | bytes 1048576 | tf_op jit(solution)/shard_map/pallas_call | solution.py:385
  71.7 6.6 %all-to-all-start.1 = ((bf16[128,16,128]{2,1,0:T(8,128)(2,1)}), bf16[128,16,128]{2,1,0:T(8,128)(2,1)S(1)}, u32[]{:S(2)}, u32[]{:S(2)}) async-start(bf16[128,16,128]{2,1,0:T(8,128)(2,1)} %shard_map.78), calls=%async_computation.1 | async-start | bytes 1048576 | tf_op jit(solution)/shard_map/all_to_all | solution.py:391
  78.3 3.4 %collective-permute-start = (bf16[2,128,256]{2,1,0:T(8,128)(2,1)S(1)}, bf16[2,128,256]{2,1,0:T(8,128)(2,1)S(1)}, u32[]{:S(2)}, u32[]{:S(2)}) collective-permute-start(bf16[2,128,256]{2,1,0:T(8,128)(2,1)S(1)} %get-tuple-element.12), channel_id=1, source_target_pairs={{0,4},{4,8},{8,12},{12,16},{16,20},{20,24},{24,28},{28,32},{32,36}... | collective-permute-start | bytes 393224 | tf_op jit(solution)/shard_map/ppermute | solution.py:331
  81.7 2.6 %collective-permute-start.1 = (bf16[2,128,256]{2,1,0:T(8,128)(2,1)S(1)}, bf16[2,128,256]{2,1,0:T(8,128)(2,1)S(1)}, u32[]{:S(2)}, u32[]{:S(2)}) collective-permute-start(bf16[2,128,256]{2,1,0:T(8,128)(2,1)S(1)} %get-tuple-element.11), channel_id=1, source_target_pairs={{4,0},{8,4},{12,8},{16,12},{20,16},{24,20},{28,24},{32,28},{36,32}... | collective-permute-start | bytes 393224 | tf_op jit(solution)/shard_map/ppermute | solution.py:332
  84.4 2.5 %collective-permute-done.before_ref = bf16[2,128,256]{2,1,0:T(8,128)(2,1)S(1)} collective-permute-done((bf16[2,128,256]{2,1,0:T(8,128)(2,1)S(1)}, bf16[2,128,256]{2,1,0:T(8,128)(2,1)S(1)}, u32[]{:S(2)}, u32[]{:S(2)}) %collective-permute-start) | collective-permute-done | bytes 131104 | tf_op jit(solution)/shard_map/ppermute | solution.py:331
  86.9 3.2 %collective-permute-done.1.after_ref = bf16[2,128,256]{2,1,0:T(8,128)(2,1)S(1)} collective-permute-done((bf16[2,128,256]{2,1,0:T(8,128)(2,1)S(1)}, bf16[2,128,256]{2,1,0:T(8,128)(2,1)S(1)}, u32[]{:S(2)}, u32[]{:S(2)}) %collective-permute-start.1) | collective-permute-done | bytes 131104 | tf_op jit(solution)/shard_map/ppermute | solution.py:332
  90.1 0.0 copy-done.2
  90.1 1.9 %shard_map.73 = (f32[256,512]{1,0:T(8,128)S(1)}, f32[16,512]{1,0:T(8,128)S(1)}, bf16[4,512,128]{2,1,0:T(8,128)(2,1)S(1)}) custom-call(s32[1,7]{1,0:T(1,128)S(1)} %bitcast.23, bf16[512,256]{1,0:T(8,128)(2,1)S(1)} %copy-done.2, bf16[2,512,256]{2,1,0:T(8,128)(2,1)S(1)} %copy-done, bf16[2,128,256]{2,1,0:T(8,128)(2,1)S(1)} %collective-permute-done.before_ref, ...), custom_call_target="tpu_custom_call" | custom-call | flops 402653184 | bytes 2097152 | tf_op jit(solution)/shard_map/pallas_call | solution.py:368
  92.0 8.3 %all-to-all-done.1.tab_ref = bf16[128,16,128]{2,1,0:T(8,128)(2,1)S(1)} async-done(((bf16[128,16,128]{2,1,0:T(8,128)(2,1)}), bf16[128,16,128]{2,1,0:T(8,128)(2,1)S(1)}, u32[]{:S(2)}, u32[]{:S(2)}) %all-to-all-start.1) | async-done | bytes 524320 | tf_op jit(solution)/shard_map/all_to_all | solution.py:391
  100.3 1.9 %shard_map.79 = bf16[512,256]{1,0:T(8,128)(2,1)} custom-call(bf16[4,512,128]{2,1,0:T(8,128)(2,1)S(1)} %get-tuple-element.8.q2_ref, bf16[128,16,128]{2,1,0:T(8,128)(2,1)S(1)} %all-to-all-done.1.tab_ref, f32[256,512]{1,0:T(8,128)S(1)} %get-tuple-element.9.o_ref, f32[16,512]{1,0:T(8,128)S(1)} %get-tuple-element.10.stat_ref), custom_call_target="tpu_custom_call" | custom-call | flops 134217728 | bytes 1048576 | tf_op jit(solution)/shard_map/pallas_call | solution.py:395
  (1 shorter events, 0.0 us)
Async XLA Ops:
  0.0 16.2 %collective-permute-start.2 = (bf16[512,256]{1,0:T(8,128)(2,1)}, bf16[512,256]{1,0:T(8,128)(2,1)}, u32[]{:S(2)}, u32[]{:S(2)}) collective-permute-start(bf16[512,256]{1,0:T(8,128)(2,1)} %x0.1), channel_id=1, source_target_pairs={{0,2},{2,0},{1,3},{3,1},{4,6},{6,4},{5,7},{7,5},{8,10},{10,8},{9,1... | collective-permute-start | bytes 786440 | tf_op jit(solution)/shard_map/ppermute | solution.py:326
  7.7 16.9 %collective-permute-start.4 = (bf16[512,256]{1,0:T(8,128)(2,1)}, bf16[512,256]{1,0:T(8,128)(2,1)S(1)}, u32[]{:S(2)}, u32[]{:S(2)}) collective-permute-start(bf16[512,256]{1,0:T(8,128)(2,1)} %x0.1), channel_id=1, source_target_pairs={{0,1},{1,0},{2,3},{3,2},{4,5},{5,4},{6,7},{7,6},{8,9},{9,8},{10,11... | collective-permute-start | bytes 786440 | tf_op jit(solution)/shard_map/ppermute | solution.py:327
  16.2 10.7 %collective-permute-start.3 = (bf16[512,256]{1,0:T(8,128)(2,1)}, bf16[512,256]{1,0:T(8,128)(2,1)S(1)}, u32[]{:S(2)}, u32[]{:S(2)}) collective-permute-start(bf16[512,256]{1,0:T(8,128)(2,1)} %collective-permute-done.2.x2), channel_id=1, source_target_pairs={{0,1},{1,0},{2,3},{3,2},{4,5},{5,4},{6,7},{7,6},{8,9},{9,8},{10,11... | collective-permute-start | bytes 786440 | tf_op jit(solution)/shard_map/ppermute | solution.py:328
  18.1 6.1 %copy-start = (bf16[2,512,256]{2,1,0:T(8,128)(2,1)S(1)}, bf16[2,512,256]{2,1,0:T(8,128)(2,1)}, u32[]{:S(2)}) copy-start(bf16[2,512,256]{2,1,0:T(8,128)(2,1)} %kv_ref.3) | copy-start | bytes 1572868
  18.1 6.5 %copy-start.1 = (bf16[512,256]{1,0:T(8,128)(2,1)S(1)}, bf16[512,256]{1,0:T(8,128)(2,1)}, u32[]{:S(2)}) copy-start(bf16[512,256]{1,0:T(8,128)(2,1)} %x0.1) | copy-start | bytes 786436
  26.9 22.8 %copy-start.3 = (f32[2,256]{1,0:T(2,128)S(1)}, f32[2,256]{1,0:T(2,128)}, u32[]{:S(2)}) copy-start(f32[2,256]{1,0:T(2,128)} %param.12) | copy-start | bytes 6148
  26.9 22.8 %copy-start.4 = (f32[2,256]{1,0:T(2,128)S(1)}, f32[2,256]{1,0:T(2,128)}, u32[]{:S(2)}) copy-start(f32[2,256]{1,0:T(2,128)} %param.11) | copy-start | bytes 6148
  28.9 61.2 %copy-start.2 = (bf16[512,256]{1,0:T(8,128)(2,1)S(1)}, bf16[512,256]{1,0:T(8,128)(2,1)}, u32[]{:S(2)}) copy-start(bf16[512,256]{1,0:T(8,128)(2,1)} %q_ref.1) | copy-start | bytes 786436
  28.9 41.0 %all-to-all-start = ((bf16[128,16,128]{2,1,0:T(8,128)(2,1)}), bf16[128,16,128]{2,1,0:T(8,128)(2,1)S(1)}, u32[]{:S(2)}, u32[]{:S(2)}) async-start(bf16[128,16,128]{2,1,0:T(8,128)(2,1)} %shard_map.77), calls=%async_computation | async-start | bytes 1048576 | tf_op jit(solution)/shard_map/all_to_all | solution.py:366
  71.7 28.6 %all-to-all-start.1 = ((bf16[128,16,128]{2,1,0:T(8,128)(2,1)}), bf16[128,16,128]{2,1,0:T(8,128)(2,1)S(1)}, u32[]{:S(2)}, u32[]{:S(2)}) async-start(bf16[128,16,128]{2,1,0:T(8,128)(2,1)} %shard_map.78), calls=%async_computation.1 | async-start | bytes 1048576 | tf_op jit(solution)/shard_map/all_to_all | solution.py:391
  78.3 8.6 %collective-permute-start = (bf16[2,128,256]{2,1,0:T(8,128)(2,1)S(1)}, bf16[2,128,256]{2,1,0:T(8,128)(2,1)S(1)}, u32[]{:S(2)}, u32[]{:S(2)}) collective-permute-start(bf16[2,128,256]{2,1,0:T(8,128)(2,1)S(1)} %get-tuple-element.12), channel_id=1, source_target_pairs={{0,4},{4,8},{8,12},{12,16},{16,20},{20,24},{24,28},{28,32},{32,36}... | collective-permute-start | bytes 393224 | tf_op jit(solution)/shard_map/ppermute | solution.py:331
  81.7 8.4 %collective-permute-start.1 = (bf16[2,128,256]{2,1,0:T(8,128)(2,1)S(1)}, bf16[2,128,256]{2,1,0:T(8,128)(2,1)S(1)}, u32[]{:S(2)}, u32[]{:S(2)}) collective-permute-start(bf16[2,128,256]{2,1,0:T(8,128)(2,1)S(1)} %get-tuple-element.11), channel_id=1, source_target_pairs={{4,0},{8,4},{12,8},{16,12},{20,16},{24,20},{28,24},{32,28},{36,32}... | collective-permute-start | bytes 393224 | tf_op jit(solution)/shard_map/ppermute | solution.py:332

commit v9 on v8

--- a/solution.py
+++ b/solution.py
@@ -16,6 +16,7 @@
 LANES = 128
 GROUP = 4
 COUNT = 8
+ORDER = ("yl", "x", "z")
 SEQ = ("z", "yl", "x")
 DOC = ("yh", "c")
 EPS = 1e-05
@@ -210,7 +211,7 @@
             copy.wait()
 
 
-def combine_kernel(tokens, scal, in_ref, gain_ref, bias_ref, out_ref, marks):
+def combine_kernel(starts, tokens, scal, in_ref, gain_ref, bias_ref, out_ref, marks):
     senders = in_ref.shape[0]
     slot = scal[0, 1]
     has_edge = scal[0, 2] > 0
@@ -225,8 +226,8 @@
     extra_top = jnp.where(has_edge, marks[slot][COUNT:, :LANES], low)
     top0, full0, top1, full1 = low, low, extra_top, extra_top
     for k in range(senders):
-        late = border <= k * tokens
-        is_edge = jnp.logical_and(border > k * tokens, border < (k + 1) * tokens)
+        late = border <= starts[k]
+        is_edge = jnp.logical_and(border > starts[k], border < starts[k] + tokens)
         top = marks[k, :COUNT, :LANES]
         full = top + jnp.where(is_edge, 0.0, marks[k, COUNT:, LANES:])
         top0 = jnp.maximum(top0, jnp.where(late, low, top))
@@ -236,8 +237,8 @@
     n0 = jnp.zeros(shape, f32)
     n1 = jnp.where(has_edge, extra * jnp.exp(extra_top - top1), 0.0)
     for k in range(senders):
-        late = border <= k * tokens
-        is_edge = jnp.logical_and(border > k * tokens, border < (k + 1) * tokens)
+        late = border <= starts[k]
+        is_edge = jnp.logical_and(border > starts[k], border < starts[k] + tokens)
         got = in_ref[k].astype(f32)
         value = got[:COUNT] + jnp.where(is_edge, 0.0, got[COUNT:])
         value = value * jnp.exp(marks[k, :COUNT, :LANES] - jnp.where(late, top1, top0))
@@ -363,7 +364,7 @@
                 flops=flops, bytes_accessed=3 << 20, transcendentals=tokens * slots // 2
             ),
         )(scal, x3, weight_t, acc, kvh)
-        arrived.append(lax.all_to_all(sent, SEQ, 0, 0, tiled=True))
+        arrived.append(lax.all_to_all(sent, ORDER, 0, 0, tiled=True))
 
     near, stats, q2 = call(
         near_kernel,
@@ -376,19 +377,33 @@
     )(scal, queries, keys_values, before, after)
 
     outs = []
-    edge = split // tokens
+    size = {name: lax.axis_size(name) for name in SEQ}
+    stride = {"z": size["yl"] * size["x"], "yl": size["x"], "x": 1}
+    a, b, c = ORDER
+    starts = [
+        tokens
+        * (
+            k // (size[b] * size[c]) * stride[a]
+            + k // size[c] % size[b] * stride[b]
+            + k % size[c] * stride[c]
+        )
+        for k in range(shards)
+    ]
+    at = split // tokens
+    at = [at // stride[name] % size[name] for name in ORDER]
+    edge = (at[0] * size[b] + at[1]) * size[c] + at[2]
     has_edge = split % tokens != 0
     marks = jnp.stack([split, jnp.where(has_edge, edge, 0), has_edge]).astype(jnp.int32)[None]
-    head = lax.div(shard * COUNT, R)
+    head = lax.div(lax.axis_index(ORDER) * COUNT, R)
     gain = lax.dynamic_slice_in_dim(slot_gain, head * DH, DH, 1).reshape(1, 2 * DH)
     bias = lax.dynamic_slice_in_dim(slot_bias, head * DH, DH, 1).reshape(1, 2 * DH)
     chunk = call(
-        functools.partial(combine_kernel, tokens),
+        functools.partial(combine_kernel, starts, tokens),
         jax.ShapeDtypeStruct((shards, 2 * COUNT, LANES), bf16),
         3, 10, 0, 1 << 20, 1 << 17,
         scratch=[pltpu.VMEM((shards, 2 * COUNT, 2 * LANES), f32)],
     )(marks, arrived[0], gain, bias)
-    tables = [lax.all_to_all(chunk, SEQ, 0, 0, tiled=True)]
+    tables = [lax.all_to_all(chunk, ORDER, 0, 0, tiled=True)]
 
     for g in range(HEADS // GROUP):
         outs.append(

time: 103 us -> 102 us (level)
  the two profiles are of different devices: /device:TPU:2 before, /device:TPU:8 now
where the time goes in v9:
time: 102 us; the launch traced here: 101 us
  starting transfers between devices  43.2 us (42%)
  waiting for transfers between devices  40.9 us (40%)
  Pallas kernels  10.2 us (10%)
  local copies, waits for them, and re-layouts  4.58 us (4%)
  between operations  2.14 us (2%)
    all_to_all x1, waiting for transfers between devices, on_device(): arrived.append(lax.all_to_all(sent, ORDER, 0, 0, tiled=True))  18.9 us
    all_to_all x1, starting transfers between devices, on_device(): arrived.append(lax.all_to_all(sent, ORDER, 0, 0, tiled=True))  17.4 us
    ppermute x1, waiting for transfers between devices, on_device(): x2 = lax.ppermute(inputs, 'yh', SWAP)  10.7 us
    all_to_all x1, starting transfers between devices, on_device(): tables = [lax.all_to_all(chunk, ORDER, 0, 0, tiled=True)]  7 us
    ppermute x1, starting transfers between devices, on_device(): x2 = lax.ppermute(inputs, 'yh', SWAP)  6.82 us
    ppermute x1, waiting for transfers between devices, on_device(): before = lax.ppermute(keys_values[:, tokens - W:], SEQ, up)  6.3 us
    all_to_all x1, waiting for transfers between devices, on_device(): tables = [lax.all_to_all(chunk, ORDER, 0, 0, tiled=True)]  4.98 us
    ppermute x1, starting transfers between devices, on_device(): after = lax.ppermute(keys_values[:, :W], SEQ, down)  4.71 us
  transfers between devices with their start and end apart: 7, of which 4 were waited for; matrix products, arithmetic and copies ran while one was open for 5% of the time, Pallas kernels for 4%

profile of v9, /device:TPU:8, one launch (start us, length us, event | category | flops | bytes accessed | tf_op | source)
XLA Modules:
  0.0 101.1 jit_solution(14979594708232315118)
XLA Ops:
  0.0 6.8 %collective-permute-start.2 = (bf16[512,256]{1,0:T(8,128)(2,1)}, bf16[512,256]{1,0:T(8,128)(2,1)}, u32[]{:S(2)}, u32[]{:S(2)}) collective-permute-start(bf16[512,256]{1,0:T(8,128)(2,1)} %x0.1), channel_id=1, source_target_pairs={{0,2},{2,0},{1,3},{3,1},{4,6},{6,4},{5,7},{7,5},{8,10},{10,8},{9,1... | collective-permute-start | bytes 786440 | tf_op jit(solution)/shard_map/ppermute | solution.py:327
  6.8 1.9 %collective-permute-start.4 = (bf16[512,256]{1,0:T(8,128)(2,1)}, bf16[512,256]{1,0:T(8,128)(2,1)S(1)}, u32[]{:S(2)}, u32[]{:S(2)}) collective-permute-start(bf16[512,256]{1,0:T(8,128)(2,1)} %x0.1), channel_id=1, source_target_pairs={{0,1},{1,0},{2,3},{3,2},{4,5},{5,4},{6,7},{7,6},{8,9},{9,8},{10,11... | collective-permute-start | bytes 786440 | tf_op jit(solution)/shard_map/ppermute | solution.py:328
  8.8 10.7 %collective-permute-done.2.x2 = bf16[512,256]{1,0:T(8,128)(2,1)} collective-permute-done((bf16[512,256]{1,0:T(8,128)(2,1)}, bf16[512,256]{1,0:T(8,128)(2,1)}, u32[]{:S(2)}, u32[]{:S(2)}) %collective-permute-start.2) | collective-permute-done | bytes 262176 | tf_op jit(solution)/shard_map/ppermute | solution.py:327
  19.4 1.9 %collective-permute-start.3 = (bf16[512,256]{1,0:T(8,128)(2,1)}, bf16[512,256]{1,0:T(8,128)(2,1)S(1)}, u32[]{:S(2)}, u32[]{:S(2)}) collective-permute-start(bf16[512,256]{1,0:T(8,128)(2,1)} %collective-permute-done.2.x2), channel_id=1, source_target_pairs={{0,1},{1,0},{2,3},{3,2},{4,5},{5,4},{6,7},{7,6},{8,9},{9,8},{10,11... | collective-permute-start | bytes 786440 | tf_op jit(solution)/shard_map/ppermute | solution.py:329
  21.4 0.0 copy-start
  21.4 0.0 copy-start.1
  21.4 2.9 %copy.8 = bf16[4,256,1024]{1,2,0:T(8,128)(2,1)S(1)} copy(bf16[4,256,1024]{2,1,0:T(8,128)(2,1)} %bitcast.24) | data formatting | bytes 4194304 | tf_op jit(solution)/shard_map/reshape | solution.py:335
  24.3 1.3 %fusion.1 = (s32[1,1]{1,0:T(1,128)}, s32[1,1]{1,0:T(1,128)}) fusion(s32[2,512]{1,0:T(2,128)} %param.13), kind=kLoop, calls=%fused_computation.4 | loop fusion | bytes 16 | tf_op jit(solution)/shard_map/slice | solution.py:313
  27.4 0.1 stack.42
  27.5 0.0 copy-done
  27.5 0.4 shard_map.76.kvh_ref
  27.9 0.0 collective-permute-done.4.x1
  27.9 0.0 copy-done.1
  27.9 0.8 shard_map.74.acc_ref
  28.7 1.5 %shard_map.75.acc_ref = f32[1024,512]{1,0:T(8,128)S(1)} custom-call(s32[1,7]{1,0:T(1,128)S(1)} %bitcast.21, bf16[512,256]{1,0:T(8,128)(2,1)} %collective-permute-done.2.x2, bf16[4,1024,256]{2,1,0:T(8,128)(2,1)S(1)} %bitcast.17, f32[1024,512]{1,0:T(8,128)S(1)} %shard_map.74.acc_ref), custom_call_target="tpu_custom_call" | custom-call | flops 268435456 | bytes 6291456 | tf_op jit(solution)/shard_map/pallas_call | solution.py:348
  30.2 0.0 copy-start.3
  30.2 0.0 copy-start.4
  30.2 0.0 collective-permute-done.3.x3
  30.2 2.0 %shard_map.77 = bf16[128,16,128]{2,1,0:T(8,128)(2,1)} custom-call(s32[1,7]{1,0:T(1,128)S(1)} %bitcast.22, bf16[512,256]{1,0:T(8,128)(2,1)S(1)} %collective-permute-done.3.x3, bf16[4,1024,256]{2,1,0:T(8,128)(2,1)S(1)} %bitcast.18, f32[1024,512]{1,0:T(8,128)S(1)} %shard_map.75.acc_ref, bf16[4,512,256]{2,1,0:T(8,128)(2,1)S(1)} %shard_map.76.kvh_ref), custom_call_target="tpu_custom_call" | custom-call | flops 268435456 | bytes 3145728 | tf_op jit(solution)/shard_map/pallas_call | solution.py:353
  32.2 0.0 copy-start.2
  32.2 17.4 %all-to-all-start = ((bf16[128,16,128]{2,1,0:T(8,128)(2,1)}), bf16[128,16,128]{2,1,0:T(8,128)(2,1)S(1)}, u32[]{:S(2)}, u32[]{:S(2)}) async-start(bf16[128,16,128]{2,1,0:T(8,128)(2,1)} %shard_map.77), calls=%async_computation | async-start | bytes 1048576 | tf_op jit(solution)/shard_map/all_to_all | solution.py:367
  49.8 0.0 copy-done.3
  49.8 0.0 copy-done.4
  49.8 0.1 constant_dynamic-slice_fusion
  49.9 0.1 reshape.10.gain_ref
  50.0 0.1 reshape.11.bias_ref
  50.1 0.1 add_bitcast_fusion.scal
  50.1 18.9 %all-to-all-done.in_ref = bf16[128,16,128]{2,1,0:T(8,128)(2,1)S(1)} async-done(((bf16[128,16,128]{2,1,0:T(8,128)(2,1)}), bf16[128,16,128]{2,1,0:T(8,128)(2,1)S(1)}, u32[]{:S(2)}, u32[]{:S(2)}) %all-to-all-start) | async-done | bytes 524320 | tf_op jit(solution)/shard_map/all_to_all | solution.py:367
  69.1 1.8 %shard_map.78 = bf16[128,16,128]{2,1,0:T(8,128)(2,1)} custom-call(s32[1,3]{1,0:T(1,128)S(1)} %add_bitcast_fusion.scal, bf16[128,16,128]{2,1,0:T(8,128)(2,1)S(1)} %all-to-all-done.in_ref, f32[1,128]{1,0:T(1,128)S(1)} %reshape.10.gain_ref, f32[1,128]{1,0:T(1,128)S(1)} %reshape.11.bias_ref), custom_call_target="tpu_custom_call" | custom-call | bytes 1048576 | tf_op jit(solution)/shard_map/pallas_call | solution.py:400
  70.9 7.0 %all-to-all-start.1 = ((bf16[128,16,128]{2,1,0:T(8,128)(2,1)}), bf16[128,16,128]{2,1,0:T(8,128)(2,1)S(1)}, u32[]{:S(2)}, u32[]{:S(2)}) async-start(bf16[128,16,128]{2,1,0:T(8,128)(2,1)} %shard_map.78), calls=%async_computation.1 | async-start | bytes 1048576 | tf_op jit(solution)/shard_map/all_to_all | solution.py:406
  77.9 3.4 %collective-permute-start = (bf16[2,128,256]{2,1,0:T(8,128)(2,1)S(1)}, bf16[2,128,256]{2,1,0:T(8,128)(2,1)S(1)}, u32[]{:S(2)}, u32[]{:S(2)}) collective-permute-start(bf16[2,128,256]{2,1,0:T(8,128)(2,1)S(1)} %get-tuple-element.12), channel_id=1, source_target_pairs={{0,4},{4,8},{8,12},{12,16},{16,20},{20,24},{24,28},{28,32},{32,36}... | collective-permute-start | bytes 393224 | tf_op jit(solution)/shard_map/ppermute | solution.py:332
  81.3 4.7 %collective-permute-start.1 = (bf16[2,128,256]{2,1,0:T(8,128)(2,1)S(1)}, bf16[2,128,256]{2,1,0:T(8,128)(2,1)S(1)}, u32[]{:S(2)}, u32[]{:S(2)}) collective-permute-start(bf16[2,128,256]{2,1,0:T(8,128)(2,1)S(1)} %get-tuple-element.11), channel_id=1, source_target_pairs={{4,0},{8,4},{12,8},{16,12},{20,16},{24,20},{28,24},{32,28},{36,32}... | collective-permute-start | bytes 393224 | tf_op jit(solution)/shard_map/ppermute | solution.py:333
  86.0 6.3 %collective-permute-done.before_ref = bf16[2,128,256]{2,1,0:T(8,128)(2,1)S(1)} collective-permute-done((bf16[2,128,256]{2,1,0:T(8,128)(2,1)S(1)}, bf16[2,128,256]{2,1,0:T(8,128)(2,1)S(1)}, u32[]{:S(2)}, u32[]{:S(2)}) %collective-permute-start) | collective-permute-done | bytes 131104 | tf_op jit(solution)/shard_map/ppermute | solution.py:332
  92.3 0.0 collective-permute-done.1.after_ref
  92.3 0.0 copy-done.2
  92.3 1.9 %shard_map.73 = (f32[256,512]{1,0:T(8,128)S(1)}, f32[16,512]{1,0:T(8,128)S(1)}, bf16[4,512,128]{2,1,0:T(8,128)(2,1)S(1)}) custom-call(s32[1,7]{1,0:T(1,128)S(1)} %bitcast.23, bf16[512,256]{1,0:T(8,128)(2,1)S(1)} %copy-done.2, bf16[2,512,256]{2,1,0:T(8,128)(2,1)S(1)} %copy-done, bf16[2,128,256]{2,1,0:T(8,128)(2,1)S(1)} %collective-permute-done.before_ref, ...), custom_call_target="tpu_custom_call" | custom-call | flops 402653184 | bytes 2097152 | tf_op jit(solution)/shard_map/pallas_call | solution.py:369
  94.3 5.0 %all-to-all-done.1.tab_ref = bf16[128,16,128]{2,1,0:T(8,128)(2,1)S(1)} async-done(((bf16[128,16,128]{2,1,0:T(8,128)(2,1)}), bf16[128,16,128]{2,1,0:T(8,128)(2,1)S(1)}, u32[]{:S(2)}, u32[]{:S(2)}) %all-to-all-start.1) | async-done | bytes 524320 | tf_op jit(solution)/shard_map/all_to_all | solution.py:406
  99.2 1.9 %shard_map.79 = bf16[512,256]{1,0:T(8,128)(2,1)} custom-call(bf16[4,512,128]{2,1,0:T(8,128)(2,1)S(1)} %get-tuple-element.8.q2_ref, bf16[128,16,128]{2,1,0:T(8,128)(2,1)S(1)} %all-to-all-done.1.tab_ref, f32[256,512]{1,0:T(8,128)S(1)} %get-tuple-element.9.o_ref, f32[16,512]{1,0:T(8,128)S(1)} %get-tuple-element.10.stat_ref), custom_call_target="tpu_custom_call" | custom-call | flops 134217728 | bytes 1048576 | tf_op jit(solution)/shard_map/pallas_call | solution.py:410
  (1 shorter events, 0.0 us)
Async XLA Ops:
  0.0 19.4 %collective-permute-start.2 = (bf16[512,256]{1,0:T(8,128)(2,1)}, bf16[512,256]{1,0:T(8,128)(2,1)}, u32[]{:S(2)}, u32[]{:S(2)}) collective-permute-start(bf16[512,256]{1,0:T(8,128)(2,1)} %x0.1), channel_id=1, source_target_pairs={{0,2},{2,0},{1,3},{3,1},{4,6},{6,4},{5,7},{7,5},{8,10},{10,8},{9,1... | collective-permute-start | bytes 786440 | tf_op jit(solution)/shard_map/ppermute | solution.py:327
  6.8 21.1 %collective-permute-start.4 = (bf16[512,256]{1,0:T(8,128)(2,1)}, bf16[512,256]{1,0:T(8,128)(2,1)S(1)}, u32[]{:S(2)}, u32[]{:S(2)}) collective-permute-start(bf16[512,256]{1,0:T(8,128)(2,1)} %x0.1), channel_id=1, source_target_pairs={{0,1},{1,0},{2,3},{3,2},{4,5},{5,4},{6,7},{7,6},{8,9},{9,8},{10,11... | collective-permute-start | bytes 786440 | tf_op jit(solution)/shard_map/ppermute | solution.py:328
  19.4 10.8 %collective-permute-start.3 = (bf16[512,256]{1,0:T(8,128)(2,1)}, bf16[512,256]{1,0:T(8,128)(2,1)S(1)}, u32[]{:S(2)}, u32[]{:S(2)}) collective-permute-start(bf16[512,256]{1,0:T(8,128)(2,1)} %collective-permute-done.2.x2), channel_id=1, source_target_pairs={{0,1},{1,0},{2,3},{3,2},{4,5},{5,4},{6,7},{7,6},{8,9},{9,8},{10,11... | collective-permute-start | bytes 786440 | tf_op jit(solution)/shard_map/ppermute | solution.py:329
  21.4 6.1 %copy-start = (bf16[2,512,256]{2,1,0:T(8,128)(2,1)S(1)}, bf16[2,512,256]{2,1,0:T(8,128)(2,1)}, u32[]{:S(2)}) copy-start(bf16[2,512,256]{2,1,0:T(8,128)(2,1)} %kv_ref.3) | copy-start | bytes 1572868
  21.4 6.5 %copy-start.1 = (bf16[512,256]{1,0:T(8,128)(2,1)S(1)}, bf16[512,256]{1,0:T(8,128)(2,1)}, u32[]{:S(2)}) copy-start(bf16[512,256]{1,0:T(8,128)(2,1)} %x0.1) | copy-start | bytes 786436
  30.2 19.6 %copy-start.3 = (f32[2,256]{1,0:T(2,128)S(1)}, f32[2,256]{1,0:T(2,128)}, u32[]{:S(2)}) copy-start(f32[2,256]{1,0:T(2,128)} %param.12) | copy-start | bytes 6148
  30.2 19.6 %copy-start.4 = (f32[2,256]{1,0:T(2,128)S(1)}, f32[2,256]{1,0:T(2,128)}, u32[]{:S(2)}) copy-start(f32[2,256]{1,0:T(2,128)} %param.11) | copy-start | bytes 6148
  32.2 60.1 %copy-start.2 = (bf16[512,256]{1,0:T(8,128)(2,1)S(1)}, bf16[512,256]{1,0:T(8,128)(2,1)}, u32[]{:S(2)}) copy-start(bf16[512,256]{1,0:T(8,128)(2,1)} %q_ref.1) | copy-start | bytes 786436
  32.2 36.8 %all-to-all-start = ((bf16[128,16,128]{2,1,0:T(8,128)(2,1)}), bf16[128,16,128]{2,1,0:T(8,128)(2,1)S(1)}, u32[]{:S(2)}, u32[]{:S(2)}) async-start(bf16[128,16,128]{2,1,0:T(8,128)(2,1)} %shard_map.77), calls=%async_computation | async-start | bytes 1048576 | tf_op jit(solution)/shard_map/all_to_all | solution.py:367
  70.9 28.4 %all-to-all-start.1 = ((bf16[128,16,128]{2,1,0:T(8,128)(2,1)}), bf16[128,16,128]{2,1,0:T(8,128)(2,1)S(1)}, u32[]{:S(2)}, u32[]{:S(2)}) async-start(bf16[128,16,128]{2,1,0:T(8,128)(2,1)} %shard_map.78), calls=%async_computation.1 | async-start | bytes 1048576 | tf_op jit(solution)/shard_map/all_to_all | solution.py:406
  77.9 14.4 %collective-permute-start = (bf16[2,128,256]{2,1,0:T(8,128)(2,1)S(1)}, bf16[2,128,256]{2,1,0:T(8,128)(2,1)S(1)}, u32[]{:S(2)}, u32[]{:S(2)}) collective-permute-start(bf16[2,128,256]{2,1,0:T(8,128)(2,1)S(1)} %get-tuple-element.12), channel_id=1, source_target_pairs={{0,4},{4,8},{8,12},{12,16},{16,20},{20,24},{24,28},{28,32},{32,36}... | collective-permute-start | bytes 393224 | tf_op jit(solution)/shard_map/ppermute | solution.py:332
  81.3 11.0 %collective-permute-start.1 = (bf16[2,128,256]{2,1,0:T(8,128)(2,1)S(1)}, bf16[2,128,256]{2,1,0:T(8,128)(2,1)S(1)}, u32[]{:S(2)}, u32[]{:S(2)}) collective-permute-start(bf16[2,128,256]{2,1,0:T(8,128)(2,1)S(1)} %get-tuple-element.11), channel_id=1, source_target_pairs={{4,0},{8,4},{12,8},{16,12},{20,16},{24,20},{28,24},{32,28},{36,32}... | collective-permute-start | bytes 393224 | tf_op jit(solution)/shard_map/ppermute | solution.py:333

commit v10 on v9

--- a/solution.py
+++ b/solution.py
@@ -16,8 +16,8 @@
 LANES = 128
 GROUP = 4
 COUNT = 8
-ORDER = ("yl", "x", "z")
-SEQ = ("z", "yl", "x")
+ORDER = ("yl", "x", "zl", "zh")
+SEQ = ("zh", "zl", "yl", "x")
 DOC = ("yh", "c")
 EPS = 1e-05
 LOW = -1e30
@@ -378,20 +378,17 @@
 
     outs = []
     size = {name: lax.axis_size(name) for name in SEQ}
-    stride = {"z": size["yl"] * size["x"], "yl": size["x"], "x": 1}
-    a, b, c = ORDER
-    starts = [
-        tokens
-        * (
-            k // (size[b] * size[c]) * stride[a]
-            + k // size[c] % size[b] * stride[b]
-            + k % size[c] * stride[c]
-        )
-        for k in range(shards)
-    ]
-    at = split // tokens
-    at = [at // stride[name] % size[name] for name in ORDER]
-    edge = (at[0] * size[b] + at[1]) * size[c] + at[2]
+    stride = {}
+    step = 1
+    for name in reversed(SEQ):
+        stride[name] = step
+        step *= size[name]
+    starts = [0]
+    for name in ORDER:
+        starts = [s + i * stride[name] * tokens for s in starts for i in range(size[name])]
+    edge = jnp.int32(0)
+    for name in ORDER:
+        edge = edge * size[name] + split // tokens // stride[name] % size[name]
     has_edge = split % tokens != 0
     marks = jnp.stack([split, jnp.where(has_edge, edge, 0), has_edge]).astype(jnp.int32)[None]
     head = lax.div(lax.axis_index(ORDER) * COUNT, R)
@@ -417,7 +414,7 @@
 
 
 def solution(mesh):
-    finer = Mesh(mesh.devices.reshape(8, 4, 4, 2, 2), SEQ + DOC)
+    finer = Mesh(mesh.devices.reshape(2, 4, 4, 4, 2, 2), SEQ + DOC)
     return jax.shard_map(
         on_device,
         mesh=finer,

time: 102 us -> 102 us (level)
  the two profiles are of different devices: /device:TPU:8 before, /device:TPU:10 now
where the time goes in v10:
time: 102 us; the launch traced here: 101 us
  waiting for transfers between devices  42.9 us (42%)
  starting transfers between devices  41.4 us (41%)
  Pallas kernels  10.2 us (10%)
  local copies, waits for them, and re-layouts  4.58 us (4%)
  between operations  2.18 us (2%)
    all_to_all x1, waiting for transfers between devices, on_device(): arrived.append(lax.all_to_all(sent, ORDER, 0, 0, tiled=True))  18.7 us
    all_to_all x1, starting transfers between devices, on_device(): arrived.append(lax.all_to_all(sent, ORDER, 0, 0, tiled=True))  17.4 us
    ppermute x1, waiting for transfers between devices, on_device(): x2 = lax.ppermute(inputs, 'yh', SWAP)  10.7 us
    all_to_all x1, waiting for transfers between devices, on_device(): tables = [lax.all_to_all(chunk, ORDER, 0, 0, tiled=True)]  7.52 us
    all_to_all x1, starting transfers between devices, on_device(): tables = [lax.all_to_all(chunk, ORDER, 0, 0, tiled=True)]  7.27 us
    ppermute x1, starting transfers between devices, on_device(): x2 = lax.ppermute(inputs, 'yh', SWAP)  6.82 us
    ppermute x1, starting transfers between devices, on_device(): before = lax.ppermute(keys_values[:, tokens - W:], SEQ, up)  3.43 us
    ppermute x1, waiting for transfers between devices, on_device(): before = lax.ppermute(keys_values[:, tokens - W:], SEQ, up)  3.22 us
  transfers between devices with their start and end apart: 7, of which 5 were waited for; matrix products, arithmetic and copies ran while one was open for 5% of the time, Pallas kernels for 4%

profile of v10, /device:TPU:10, one launch (start us, length us, event | category | flops | bytes accessed | tf_op | source)
XLA Modules:
  0.0 101.4 jit_solution(10535323449313334545)
XLA Ops:
  0.0 6.8 %collective-permute-start.2 = (bf16[512,256]{1,0:T(8,128)(2,1)}, bf16[512,256]{1,0:T(8,128)(2,1)}, u32[]{:S(2)}, u32[]{:S(2)}) collective-permute-start(bf16[512,256]{1,0:T(8,128)(2,1)} %x0.1), channel_id=1, source_target_pairs={{0,2},{2,0},{1,3},{3,1},{4,6},{6,4},{5,7},{7,5},{8,10},{10,8},{9,1... | collective-permute-start | bytes 786440 | tf_op jit(solution)/shard_map/ppermute | solution.py:327
  6.8 1.9 %collective-permute-start.4 = (bf16[512,256]{1,0:T(8,128)(2,1)}, bf16[512,256]{1,0:T(8,128)(2,1)S(1)}, u32[]{:S(2)}, u32[]{:S(2)}) collective-permute-start(bf16[512,256]{1,0:T(8,128)(2,1)} %x0.1), channel_id=1, source_target_pairs={{0,1},{1,0},{2,3},{3,2},{4,5},{5,4},{6,7},{7,6},{8,9},{9,8},{10,11... | collective-permute-start | bytes 786440 | tf_op jit(solution)/shard_map/ppermute | solution.py:328
  8.8 10.7 %collective-permute-done.2.x2 = bf16[512,256]{1,0:T(8,128)(2,1)} collective-permute-done((bf16[512,256]{1,0:T(8,128)(2,1)}, bf16[512,256]{1,0:T(8,128)(2,1)}, u32[]{:S(2)}, u32[]{:S(2)}) %collective-permute-start.2) | collective-permute-done | bytes 262176 | tf_op jit(solution)/shard_map/ppermute | solution.py:327
  19.4 1.9 %collective-permute-start.3 = (bf16[512,256]{1,0:T(8,128)(2,1)}, bf16[512,256]{1,0:T(8,128)(2,1)S(1)}, u32[]{:S(2)}, u32[]{:S(2)}) collective-permute-start(bf16[512,256]{1,0:T(8,128)(2,1)} %collective-permute-done.2.x2), channel_id=1, source_target_pairs={{0,1},{1,0},{2,3},{3,2},{4,5},{5,4},{6,7},{7,6},{8,9},{9,8},{10,11... | collective-permute-start | bytes 786440 | tf_op jit(solution)/shard_map/ppermute | solution.py:329
  21.4 0.0 copy-start
  21.4 0.0 copy-start.1
  21.4 2.9 %copy.8 = bf16[4,256,1024]{1,2,0:T(8,128)(2,1)S(1)} copy(bf16[4,256,1024]{2,1,0:T(8,128)(2,1)} %bitcast.24) | data formatting | bytes 4194304 | tf_op jit(solution)/shard_map/reshape | solution.py:335
  24.3 1.3 %fusion.1 = (s32[1,1]{1,0:T(1,128)}, s32[1,1]{1,0:T(1,128)}) fusion(s32[2,512]{1,0:T(2,128)} %param.13), kind=kLoop, calls=%fused_computation.4 | loop fusion | bytes 16 | tf_op jit(solution)/shard_map/slice | solution.py:313
  27.4 0.1 stack.42
  27.5 0.0 copy-done
  27.5 0.4 shard_map.76.kvh_ref
  27.9 0.0 collective-permute-done.4.x1
  27.9 0.0 copy-done.1
  27.9 0.8 shard_map.74.acc_ref
  28.7 1.4 %shard_map.75.acc_ref = f32[1024,512]{1,0:T(8,128)S(1)} custom-call(s32[1,7]{1,0:T(1,128)S(1)} %bitcast.21, bf16[512,256]{1,0:T(8,128)(2,1)} %collective-permute-done.2.x2, bf16[4,1024,256]{2,1,0:T(8,128)(2,1)S(1)} %bitcast.17, f32[1024,512]{1,0:T(8,128)S(1)} %shard_map.74.acc_ref), custom_call_target="tpu_custom_call" | custom-call | flops 268435456 | bytes 6291456 | tf_op jit(solution)/shard_map/pallas_call | solution.py:348
  30.2 0.0 copy-start.3
  30.2 0.0 copy-start.4
  30.2 0.0 collective-permute-done.3.x3
  30.2 2.0 %shard_map.77 = bf16[128,16,128]{2,1,0:T(8,128)(2,1)} custom-call(s32[1,7]{1,0:T(1,128)S(1)} %bitcast.22, bf16[512,256]{1,0:T(8,128)(2,1)S(1)} %collective-permute-done.3.x3, bf16[4,1024,256]{2,1,0:T(8,128)(2,1)S(1)} %bitcast.18, f32[1024,512]{1,0:T(8,128)S(1)} %shard_map.75.acc_ref, bf16[4,512,256]{2,1,0:T(8,128)(2,1)S(1)} %shard_map.76.kvh_ref), custom_call_target="tpu_custom_call" | custom-call | flops 268435456 | bytes 3145728 | tf_op jit(solution)/shard_map/pallas_call | solution.py:353
  32.2 0.0 copy-start.2
  32.2 17.4 %all-to-all-start = ((bf16[128,16,128]{2,1,0:T(8,128)(2,1)}), bf16[128,16,128]{2,1,0:T(8,128)(2,1)S(1)}, u32[]{:S(2)}, u32[]{:S(2)}) async-start(bf16[128,16,128]{2,1,0:T(8,128)(2,1)} %shard_map.77), calls=%async_computation | async-start | bytes 1048576 | tf_op jit(solution)/shard_map/all_to_all | solution.py:367
  49.9 0.0 copy-done.3
  49.9 0.0 copy-done.4
  49.9 0.1 constant_dynamic-slice_fusion
  50.0 0.1 reshape.10.gain_ref
  50.0 0.1 reshape.11.bias_ref
  50.1 0.1 add_bitcast_fusion.scal
  50.2 18.7 %all-to-all-done.in_ref = bf16[128,16,128]{2,1,0:T(8,128)(2,1)S(1)} async-done(((bf16[128,16,128]{2,1,0:T(8,128)(2,1)}), bf16[128,16,128]{2,1,0:T(8,128)(2,1)S(1)}, u32[]{:S(2)}, u32[]{:S(2)}) %all-to-all-start) | async-done | bytes 524320 | tf_op jit(solution)/shard_map/all_to_all | solution.py:367
  68.9 1.8 %shard_map.78 = bf16[128,16,128]{2,1,0:T(8,128)(2,1)} custom-call(s32[1,3]{1,0:T(1,128)S(1)} %add_bitcast_fusion.scal, bf16[128,16,128]{2,1,0:T(8,128)(2,1)S(1)} %all-to-all-done.in_ref, f32[1,128]{1,0:T(1,128)S(1)} %reshape.10.gain_ref, f32[1,128]{1,0:T(1,128)S(1)} %reshape.11.bias_ref), custom_call_target="tpu_custom_call" | custom-call | bytes 1048576 | tf_op jit(solution)/shard_map/pallas_call | solution.py:397
  70.7 7.3 %all-to-all-start.1 = ((bf16[128,16,128]{2,1,0:T(8,128)(2,1)}), bf16[128,16,128]{2,1,0:T(8,128)(2,1)S(1)}, u32[]{:S(2)}, u32[]{:S(2)}) async-start(bf16[128,16,128]{2,1,0:T(8,128)(2,1)} %shard_map.78), calls=%async_computation.1 | async-start | bytes 1048576 | tf_op jit(solution)/shard_map/all_to_all | solution.py:403
  78.0 3.4 %collective-permute-start = (bf16[2,128,256]{2,1,0:T(8,128)(2,1)S(1)}, bf16[2,128,256]{2,1,0:T(8,128)(2,1)S(1)}, u32[]{:S(2)}, u32[]{:S(2)}) collective-permute-start(bf16[2,128,256]{2,1,0:T(8,128)(2,1)S(1)} %get-tuple-element.12), channel_id=1, source_target_pairs={{0,4},{4,8},{8,12},{12,16},{16,20},{20,24},{24,28},{28,32},{32,36}... | collective-permute-start | bytes 393224 | tf_op jit(solution)/shard_map/ppermute | solution.py:332
  81.5 2.6 %collective-permute-start.1 = (bf16[2,128,256]{2,1,0:T(8,128)(2,1)S(1)}, bf16[2,128,256]{2,1,0:T(8,128)(2,1)S(1)}, u32[]{:S(2)}, u32[]{:S(2)}) collective-permute-start(bf16[2,128,256]{2,1,0:T(8,128)(2,1)S(1)} %get-tuple-element.11), channel_id=1, source_target_pairs={{4,0},{8,4},{12,8},{16,12},{20,16},{24,20},{28,24},{32,28},{36,32}... | collective-permute-start | bytes 393224 | tf_op jit(solution)/shard_map/ppermute | solution.py:333
  84.1 3.2 %collective-permute-done.before_ref = bf16[2,128,256]{2,1,0:T(8,128)(2,1)S(1)} collective-permute-done((bf16[2,128,256]{2,1,0:T(8,128)(2,1)S(1)}, bf16[2,128,256]{2,1,0:T(8,128)(2,1)S(1)}, u32[]{:S(2)}, u32[]{:S(2)}) %collective-permute-start) | collective-permute-done | bytes 131104 | tf_op jit(solution)/shard_map/ppermute | solution.py:332
  87.3 2.8 %collective-permute-done.1.after_ref = bf16[2,128,256]{2,1,0:T(8,128)(2,1)S(1)} collective-permute-done((bf16[2,128,256]{2,1,0:T(8,128)(2,1)S(1)}, bf16[2,128,256]{2,1,0:T(8,128)(2,1)S(1)}, u32[]{:S(2)}, u32[]{:S(2)}) %collective-permute-start.1) | collective-permute-done | bytes 131104 | tf_op jit(solution)/shard_map/ppermute | solution.py:333
  90.1 0.0 copy-done.2
  90.1 1.9 %shard_map.73 = (f32[256,512]{1,0:T(8,128)S(1)}, f32[16,512]{1,0:T(8,128)S(1)}, bf16[4,512,128]{2,1,0:T(8,128)(2,1)S(1)}) custom-call(s32[1,7]{1,0:T(1,128)S(1)} %bitcast.23, bf16[512,256]{1,0:T(8,128)(2,1)S(1)} %copy-done.2, bf16[2,512,256]{2,1,0:T(8,128)(2,1)S(1)} %copy-done, bf16[2,128,256]{2,1,0:T(8,128)(2,1)S(1)} %collective-permute-done.before_ref, ...), custom_call_target="tpu_custom_call" | custom-call | flops 402653184 | bytes 2097152 | tf_op jit(solution)/shard_map/pallas_call | solution.py:369
  92.0 7.5 %all-to-all-done.1.tab_ref = bf16[128,16,128]{2,1,0:T(8,128)(2,1)S(1)} async-done(((bf16[128,16,128]{2,1,0:T(8,128)(2,1)}), bf16[128,16,128]{2,1,0:T(8,128)(2,1)S(1)}, u32[]{:S(2)}, u32[]{:S(2)}) %all-to-all-start.1) | async-done | bytes 524320 | tf_op jit(solution)/shard_map/all_to_all | solution.py:403
  99.5 1.9 %shard_map.79 = bf16[512,256]{1,0:T(8,128)(2,1)} custom-call(bf16[4,512,128]{2,1,0:T(8,128)(2,1)S(1)} %get-tuple-element.8.q2_ref, bf16[128,16,128]{2,1,0:T(8,128)(2,1)S(1)} %all-to-all-done.1.tab_ref, f32[256,512]{1,0:T(8,128)S(1)} %get-tuple-element.9.o_ref, f32[16,512]{1,0:T(8,128)S(1)} %get-tuple-element.10.stat_ref), custom_call_target="tpu_custom_call" | custom-call | flops 134217728 | bytes 1048576 | tf_op jit(solution)/shard_map/pallas_call | solution.py:407
  (1 shorter events, 0.0 us)
Async XLA Ops:
  0.0 19.4 %collective-permute-start.2 = (bf16[512,256]{1,0:T(8,128)(2,1)}, bf16[512,256]{1,0:T(8,128)(2,1)}, u32[]{:S(2)}, u32[]{:S(2)}) collective-permute-start(bf16[512,256]{1,0:T(8,128)(2,1)} %x0.1), channel_id=1, source_target_pairs={{0,2},{2,0},{1,3},{3,1},{4,6},{6,4},{5,7},{7,5},{8,10},{10,8},{9,1... | collective-permute-start | bytes 786440 | tf_op jit(solution)/shard_map/ppermute | solution.py:327
  6.8 21.1 %collective-permute-start.4 = (bf16[512,256]{1,0:T(8,128)(2,1)}, bf16[512,256]{1,0:T(8,128)(2,1)S(1)}, u32[]{:S(2)}, u32[]{:S(2)}) collective-permute-start(bf16[512,256]{1,0:T(8,128)(2,1)} %x0.1), channel_id=1, source_target_pairs={{0,1},{1,0},{2,3},{3,2},{4,5},{5,4},{6,7},{7,6},{8,9},{9,8},{10,11... | collective-permute-start | bytes 786440 | tf_op jit(solution)/shard_map/ppermute | solution.py:328
  19.4 10.8 %collective-permute-start.3 = (bf16[512,256]{1,0:T(8,128)(2,1)}, bf16[512,256]{1,0:T(8,128)(2,1)S(1)}, u32[]{:S(2)}, u32[]{:S(2)}) collective-permute-start(bf16[512,256]{1,0:T(8,128)(2,1)} %collective-permute-done.2.x2), channel_id=1, source_target_pairs={{0,1},{1,0},{2,3},{3,2},{4,5},{5,4},{6,7},{7,6},{8,9},{9,8},{10,11... | collective-permute-start | bytes 786440 | tf_op jit(solution)/shard_map/ppermute | solution.py:329
  21.4 6.1 %copy-start = (bf16[2,512,256]{2,1,0:T(8,128)(2,1)S(1)}, bf16[2,512,256]{2,1,0:T(8,128)(2,1)}, u32[]{:S(2)}) copy-start(bf16[2,512,256]{2,1,0:T(8,128)(2,1)} %kv_ref.3) | copy-start | bytes 1572868
  21.4 6.5 %copy-start.1 = (bf16[512,256]{1,0:T(8,128)(2,1)S(1)}, bf16[512,256]{1,0:T(8,128)(2,1)}, u32[]{:S(2)}) copy-start(bf16[512,256]{1,0:T(8,128)(2,1)} %x0.1) | copy-start | bytes 786436
  30.2 19.7 %copy-start.3 = (f32[2,256]{1,0:T(2,128)S(1)}, f32[2,256]{1,0:T(2,128)}, u32[]{:S(2)}) copy-start(f32[2,256]{1,0:T(2,128)} %param.12) | copy-start | bytes 6148
  30.2 19.7 %copy-start.4 = (f32[2,256]{1,0:T(2,128)S(1)}, f32[2,256]{1,0:T(2,128)}, u32[]{:S(2)}) copy-start(f32[2,256]{1,0:T(2,128)} %param.11) | copy-start | bytes 6148
  32.2 57.9 %copy-start.2 = (bf16[512,256]{1,0:T(8,128)(2,1)S(1)}, bf16[512,256]{1,0:T(8,128)(2,1)}, u32[]{:S(2)}) copy-start(bf16[512,256]{1,0:T(8,128)(2,1)} %q_ref.1) | copy-start | bytes 786436
  32.2 36.7 %all-to-all-start = ((bf16[128,16,128]{2,1,0:T(8,128)(2,1)}), bf16[128,16,128]{2,1,0:T(8,128)(2,1)S(1)}, u32[]{:S(2)}, u32[]{:S(2)}) async-start(bf16[128,16,128]{2,1,0:T(8,128)(2,1)} %shard_map.77), calls=%async_computation | async-start | bytes 1048576 | tf_op jit(solution)/shard_map/all_to_all | solution.py:367
  70.7 28.8 %all-to-all-start.1 = ((bf16[128,16,128]{2,1,0:T(8,128)(2,1)}), bf16[128,16,128]{2,1,0:T(8,128)(2,1)S(1)}, u32[]{:S(2)}, u32[]{:S(2)}) async-start(bf16[128,16,128]{2,1,0:T(8,128)(2,1)} %shard_map.78), calls=%async_computation.1 | async-start | bytes 1048576 | tf_op jit(solution)/shard_map/all_to_all | solution.py:403
  78.0 9.3 %collective-permute-start = (bf16[2,128,256]{2,1,0:T(8,128)(2,1)S(1)}, bf16[2,128,256]{2,1,0:T(8,128)(2,1)S(1)}, u32[]{:S(2)}, u32[]{:S(2)}) collective-permute-start(bf16[2,128,256]{2,1,0:T(8,128)(2,1)S(1)} %get-tuple-element.12), channel_id=1, source_target_pairs={{0,4},{4,8},{8,12},{12,16},{16,20},{20,24},{24,28},{28,32},{32,36}... | collective-permute-start | bytes 393224 | tf_op jit(solution)/shard_map/ppermute | solution.py:332
  81.5 8.6 %collective-permute-start.1 = (bf16[2,128,256]{2,1,0:T(8,128)(2,1)S(1)}, bf16[2,128,256]{2,1,0:T(8,128)(2,1)S(1)}, u32[]{:S(2)}, u32[]{:S(2)}) collective-permute-start(bf16[2,128,256]{2,1,0:T(8,128)(2,1)S(1)} %get-tuple-element.11), channel_id=1, source_target_pairs={{4,0},{8,4},{12,8},{16,12},{20,16},{24,20},{28,24},{32,28},{36,32}... | collective-permute-start | bytes 393224 | tf_op jit(solution)/shard_map/ppermute | solution.py:333
